TPU v7x, 32 devices: a whole 2x2x4 slice. The times are simulated.
32 devices in a mesh: ctx: 16 (over z, x, core), tp: 2 (over y).
Axes of the slice: x: 2, y: 2, z: 4, core: 2. Of those that a mesh axis runs over, the one named last changes fastest.
Arguments:
- layer_input: bfloat16 [8192, 5376], P('ctx', 'tp'), may hold values from -60 to 60
- norm_weight: bfloat16 [5376], P('tp'), may hold values from 0.099609375 to 1.8984375
- document_index: int32 [8192], P('ctx'), may hold values from 0 to 3, never falling along the last dimension, each value on 1 to 4096 neighbouring positions
- stored_queries: bfloat16 [8192, 4096], P('ctx', 'tp'), may hold values from -6 to 6
- stored_keys: bfloat16 [8192, 2048], P('ctx', 'tp'), may hold values from -6 to 6
- stored_values: bfloat16 [8192, 2048], P('ctx', 'tp'), may hold values from -6 to 6
- output_weight: bfloat16 [4096, 5376], P(None, 'tp'), may hold values from -0.1500248 to 0.1500248
- projection_gradient: bfloat16 [8192, 5376], P('ctx', 'tp'), may hold values from -600 to 600
- adapter_down_maps: bfloat16 [5376, 24], P('tp'), may hold values from -0.078125 to 0.078125
Outputs:
- feature_q: float32 [8, 4096], P(None, 'tp')
- feature_k: float32 [8, 2048], P(None, 'tp')
- feature_v: float32 [8, 2048], P(None, 'tp')
Inputs may be any that keep to these rules, and one draw needn't show every extreme that they name: `document_index`: document numbers never fall along the sequence; every document is one run of positions.
All inputs are finite; a program needn't handle non-finite values.
Results may differ from a plain program's by a relative error of at most 0.0095.
Values may be sent and summed in bfloat16 or wider, within the bound.
No kernel may reach another device: no remote copies, remote signals or barrier semaphores. Data moves between devices by JAX's collectives and lax.ppermute only.
A program may use at most 192 MiB of HBM per device.

v0:
```python
import functools

import jax
import jax.numpy as jnp
from jax import lax
from jax.experimental import pallas as pl
from jax.experimental.pallas import tpu as pltpu
from jax.sharding import PartitionSpec as P


MODEL_WIDTH = 5376
QUERY_HEADS = 32
KEY_VALUE_HEADS = 16
HEAD_SIZE = 128
LOOKBACK_SPAN = 1024
ADAPTER_RANK = 8
LOG2E = 1.4426950408889634
SCALE = float(MODEL_WIDTH // QUERY_HEADS) ** (-0.5)
LANES = 128
GRANT = 62 << 20
ROW_K, ROW_V, ROW_ONE, ROW_DOC = 0, ADAPTER_RANK, 2 * ADAPTER_RANK, 2 * ADAPTER_RANK + 1
TABLE = 4 * ADAPTER_RANK

NT = (((1,), (1,)), ((), ()))
NN = (((1,), (0,)), ((), ()))
TN = (((0,), (0,)), ((), ()))


def dotf(left, right, dims):
    return lax.dot_general(left, right, dims, preferred_element_type=jnp.float32)


def shifted(value, axis, steps):
    count = lax.axis_size(axis)
    first, last = (max(0, -steps), min(count, count - steps))
    return lax.ppermute(value, axis, [(source, source + steps) for source in range(first, last)])


def xor_move(value, axis, step):
    return lax.ppermute(value, axis, [(at, at ^ step) for at in range(lax.axis_size(axis))])


def project_body(offset_ref, gradient_ref, weight_ref, out_ref):
    out_ref[...] = dotf(gradient_ref[...], weight_ref[...], NT).astype(out_ref.dtype)


def project(gradient, weight, first_block, blocks, width):
    rows, depth = gradient.shape
    return pl.pallas_call(
        project_body,
        grid_spec=pltpu.PrefetchScalarGridSpec(
            num_scalar_prefetch=1,
            grid=(blocks,),
            in_specs=[
                pl.BlockSpec((rows, depth), lambda i, off: (0, 0)),
                pl.BlockSpec((width, depth), lambda i, off: (off[0] + i, 0)),
            ],
            out_specs=pl.BlockSpec((rows, width), lambda i, off: (0, i)),
        ),
        out_shape=jax.ShapeDtypeStruct((rows, blocks * width), jnp.bfloat16),
        cost_estimate=pl.CostEstimate(
            flops=2 * rows * depth * width * blocks,
            bytes_accessed=2 * (rows * depth + width * blocks * depth + rows * width * blocks),
            transcendentals=0,
        ),
        compiler_params=pltpu.CompilerParams(vmem_limit_bytes=GRANT),
    )(first_block, gradient, weight)


def open_body(chunks, offset_ref, gradient_ref, weight_ref, x_ref, down_ref, k_ref, v_ref, out_ref, low_ref, *packs):
    step = pl.program_id(0)
    out_ref[...] = dotf(gradient_ref[...], weight_ref[...], NT).astype(out_ref.dtype)
    low_ref[0 : 3 * ADAPTER_RANK, :] = dotf(down_ref[...], x_ref[...], NT)
    hidden = x_ref[...].astype(jnp.float32)
    ones = jnp.ones((ADAPTER_RANK, hidden.shape[1]), jnp.bfloat16)
    low_ref[3 * ADAPTER_RANK :, :] = dotf(ones, (hidden * hidden).astype(jnp.bfloat16), NT)
    wide = k_ref.shape[1]
    each = pl.num_programs(0) // chunks
    for c, pack_ref in enumerate(packs):

        @pl.when(step // each == c)
        def _(pack_ref=pack_ref):
            pack_ref[:, :wide] = k_ref[...]
            pack_ref[:, wide:] = v_ref[...]


def open_call(gradient, weight, first_block, blocks, width, x, down, keys, values, chunks):
    rows, depth = gradient.shape
    slab = rows // blocks
    wide = keys.shape[1] // blocks
    each = blocks // chunks
    pack_specs = [
        pl.BlockSpec((rows, 2 * wide), lambda i, off, c=c: (0, jnp.clip(i - c * each, 0, each - 1)))
        for c in range(chunks)
    ]
    pack_shape = jax.ShapeDtypeStruct((rows, 2 * wide * each), keys.dtype)
    return pl.pallas_call(
        functools.partial(open_body, chunks),
        grid_spec=pltpu.PrefetchScalarGridSpec(
            num_scalar_prefetch=1,
            grid=(blocks,),
            in_specs=[
                pl.BlockSpec((rows, depth), lambda i, off: (0, 0)),
                pl.BlockSpec((width, depth), lambda i, off: (off[0] + i, 0)),
                pl.BlockSpec((slab, depth), lambda i, off: (i, 0)),
                pl.BlockSpec((3 * ADAPTER_RANK, depth), lambda i, off: (0, 0)),
                pl.BlockSpec((rows, wide), lambda i, off: (0, i)),
                pl.BlockSpec((rows, wide), lambda i, off: (0, i)),
            ],
            out_specs=[
                pl.BlockSpec((rows, width), lambda i, off: (0, i)),
                pl.BlockSpec((TABLE, slab), lambda i, off: (0, i)),
            ]
            + pack_specs,
        ),
        out_shape=[
            jax.ShapeDtypeStruct((rows, blocks * width), jnp.bfloat16),
            jax.ShapeDtypeStruct((TABLE, rows), jnp.float32),
        ]
        + [pack_shape] * chunks,
        cost_estimate=pl.CostEstimate(
            flops=2 * rows * depth * width * blocks,
            bytes_accessed=2 * (2 * rows * depth + width * blocks * depth + rows * width * blocks),
            transcendentals=0,
        ),
        compiler_params=pltpu.CompilerParams(vmem_limit_bytes=GRANT),
    )(first_block, gradient, weight, x, down, keys, values)


def table_body(mine_ref, theirs_ref, doc_ref, out_ref):
    joined = mine_ref[...] + theirs_ref[...]
    inverse = lax.rsqrt(joined[3 * ADAPTER_RANK : 3 * ADAPTER_RANK + 1] / float(MODEL_WIDTH) + 1e-06)
    low = joined * inverse
    rank = ADAPTER_RANK
    row = lax.broadcasted_iota(jnp.int32, (rank, low.shape[1]), 0)
    extra = jnp.where(row == 0, 1.0, jnp.where(row == 1, doc_ref[...].astype(jnp.float32), 0.0))
    out_ref[...] = jnp.concatenate([low[rank : 3 * rank], extra, low[:rank]], 0).astype(out_ref.dtype)


def prep_body(first_ref, t2_ref, t1_ref, t0_ref, ext_ref, st_ref):
    rows = t0_ref.shape[1]
    tables = [ref[...].astype(jnp.float32) for ref in (t2_ref, t1_ref, t0_ref)]
    blank = jnp.zeros((LANES - TABLE, rows), jnp.float32)
    for at, table in enumerate(tables):
        turned = jnp.concatenate([table, blank], 0).T
        ext_ref[at * rows : (at + 1) * rows, :] = turned.astype(ext_ref.dtype)
    ids = [table[ROW_DOC : ROW_DOC + 1] for table in tables]
    column = turned[:, ROW_DOC : ROW_DOC + 1]
    leading = column[0:1]
    before = sum(jnp.sum((one < leading).astype(jnp.float32), axis=1, keepdims=True) for one in ids[:2])
    inside = jnp.sum((ids[2] < column).astype(jnp.float32), axis=1, keepdims=True)
    begin = jnp.where(column > leading, inside + float(2 * rows), before).astype(jnp.int32)
    begin = jnp.broadcast_to(begin, st_ref.shape)
    band = lax.broadcasted_iota(jnp.int32, st_ref.shape, 0) + (2 * rows + 1 - LOOKBACK_SPAN)
    st_ref[...] = jnp.maximum(jnp.maximum(begin, band), first_ref[0])


def attend_body(
    steps, step_units, base, offset_ref, q_ref, pg_ref, w_ref, recv_ref, k0, k1, k2, v0, v1, v2, ext_ref, lq_ref, st_ref, *rest
):
    if base:
        before_ref, out_ref, s_scr, e_scr, ve, ke, do_scr = rest
    else:
        out_ref, s_scr, e_scr, ve, ke, do_scr = rest
    rows = pg_ref.shape[0]
    tile = s_scr.shape[1] // 2
    keys = s_scr.shape[2]
    width = tile
    factor = SCALE * LOG2E
    parts = rows // tile
    units = [(g, t) for g in range(step_units) for t in range(parts)]
    state = [{} for _ in units]
    columns = range(keys // width)
    step = pl.program_id(0)
    if base:

        @pl.when(step == 0)
        def _():
            out_ref[:, :base] = before_ref[...]

    def prepare(i):
        g, t = units[i]
        if t == 0:
            own = dotf(pg_ref[...], w_ref[2 * LANES * g : 2 * LANES * (g + 1), :], NT)
            got = recv_ref[:, 2 * LANES * g : 2 * LANES * (g + 1)].astype(jnp.float32)
            do_scr[g % 2] = (own + got).astype(jnp.bfloat16)
            for b, (k_ref, v_ref) in enumerate(((k0, v0), (k1, v1), (k2, v2))):
                span = slice(b * rows, (b + 1) * rows)
                ke[g % 2, span, :LANES] = k_ref[:, g * LANES : (g + 1) * LANES]
                ve[g % 2, span, :LANES] = v_ref[:, g * LANES : (g + 1) * LANES]
                ke[g % 2, span, LANES:] = ext_ref[span, :]
                ve[g % 2, span, LANES:] = ext_ref[span, :]
        s = state[i]
        r0 = t * tile
        c0 = 2 * LANES * g
        s["q"] = jnp.concatenate(
            [q_ref[r0 : r0 + tile, c0 : c0 + LANES], q_ref[r0 : r0 + tile, c0 + LANES : c0 + 2 * LANES]], 0
        )
        start = st_ref[r0 : r0 + tile, :]
        s["start"] = jnp.concatenate([start, start], 0)
        s["peak"] = None

    def score(i, j):
        g, t = units[i]
        s = state[i]
        at = t * tile + j * width
        raw = dotf(s["q"], ke[g % 2, at : at + width, :LANES], NT)
        for h in range(width // LANES):
            value = raw[:, h * LANES : (h + 1) * LANES]
            pos = lax.broadcasted_iota(jnp.int32, value.shape, 1) + (at + h * LANES)
            ok = pos >= s["start"]
            if j == len(columns) - 1:
                row = lax.broadcasted_iota(jnp.int32, value.shape, 0)
                row = jnp.where(row >= tile, row - tile, row)
                ok = ok & (pos <= row + (2 * rows + t * tile))
            value = jnp.where(ok, value, -1e30)
            s_scr[i % 2, :, j * width + h * LANES : j * width + (h + 1) * LANES] = value
            s["peak"] = value if s["peak"] is None else jnp.maximum(s["peak"], value)

    def weigh(i, j):
        g, t = units[i]
        s = state[i]
        at = t * tile + j * width
        cols = slice(j * width, (j + 1) * width)
        e = jnp.exp2((s_scr[i % 2, :, cols] - s["top"]) * factor).astype(jnp.bfloat16)
        e_scr[i % 2, :, cols] = e
        part = dotf(e, ve[g % 2, at : at + width, :], NN)
        s["acc"] = part if j == 0 else s["acc"] + part

    def weighed(i):
        g, t = units[i]
        s = state[i]
        acc = s["acc"]
        do = do_scr[g % 2, t * tile : (t + 1) * tile, :]
        s["do"] = jnp.concatenate([do[:, :LANES], do[:, LANES:]], 0)
        s["inverse"] = 1.0 / acc[:, LANES + ROW_ONE : LANES + ROW_ONE + 1]
        s["delta"] = (
            jnp.sum(s["do"].astype(jnp.float32) * acc[:, :LANES], axis=1, keepdims=True) * s["inverse"]
        )
        s["uv"] = (acc[:, LANES:] * s["inverse"]).astype(jnp.bfloat16)

    def back(i, j):
        g, t = units[i]
        s = state[i]
        at = t * tile + j * width
        dp = dotf(s["do"], ve[g % 2, at : at + width, :LANES], NT)
        e = e_scr[i % 2, :, j * width : (j + 1) * width].astype(jnp.float32)
        ds = (e * (dp - s["delta"])).astype(jnp.bfloat16)
        part = dotf(ds, ke[g % 2, at : at + width, :], NN)
        s["back"] = part if j == 0 else s["back"] + part

    def backed(i):
        g, t = units[i]
        s = state[i]
        fin = (s["back"] * (s["inverse"] * SCALE)).astype(jnp.bfloat16)
        dq = jnp.concatenate([fin[:tile, :LANES], fin[tile:, :LANES]], 1)
        low_q = lq_ref[2 * ADAPTER_RANK :, t * tile : (t + 1) * tile]
        out = (dotf(low_q, dq, NN), dotf(fin[:, LANES:], s["q"], TN), dotf(s["uv"], s["do"], TN))
        if t > 0:
            out = tuple(a + b for a, b in zip(out, state[i - 1]["out"]))
            state[i - 1].clear()
        s["out"] = out
        if t == parts - 1:
            for unit_step in range(steps):

                @pl.when(step == unit_step)
                def _():
                    at = base + 4 * LANES * (unit_step * step_units + g)
                    out_ref[:, at : at + 2 * LANES] = out[0][ADAPTER_RANK:].astype(out_ref.dtype)
                    out_ref[:, at + 2 * LANES : at + 3 * LANES] = out[1][ROW_K : ROW_K + ADAPTER_RANK].astype(out_ref.dtype)
                    out_ref[:, at + 3 * LANES : at + 4 * LANES] = out[2][ROW_V : ROW_V + ADAPTER_RANK].astype(out_ref.dtype)

    prepare(0)
    for j in columns:
        score(0, j)
    for i in range(len(units) + 1):
        if i < len(units):
            state[i]["top"] = jnp.max(state[i]["peak"], axis=1, keepdims=True)
        if i + 1 < len(units):
            prepare(i + 1)
        for j in columns:
            if i < len(units):
                weigh(i, j)
            if i + 1 < len(units):
                score(i + 1, j)
            if i > 0:
                back(i - 1, j)
        if i < len(units):
            weighed(i)
        if i > 0:
            backed(i - 1)


def attend(queries, gradient, weight, recv, packs, ext, table, starts, first, skip, steps, units, before):
    rows, depth = gradient.shape
    tile = rows // 2
    keys = LOOKBACK_SPAN + tile
    base = 0 if before is None else before.shape[1]
    groups = steps * units
    col = lambda width, fn: pl.BlockSpec((rows, width), fn)
    total = base + 4 * LANES * groups
    wide = units * LANES
    operands = [queries, gradient, weight, recv, *packs, *packs, ext, table, starts]
    in_specs = (
        [
            col(2 * wide, lambda g, off: (0, g + skip)),
            col(depth, lambda g, off: (0, 0)),
            pl.BlockSpec((2 * wide, depth), lambda g, off: (g + off[0], 0)),
            col(2 * wide, lambda g, off: (0, g)),
        ]
        + [col(wide, lambda g, off: (0, 2 * g))] * 3
        + [col(wide, lambda g, off: (0, 2 * g + 1))] * 3
        + [
            pl.BlockSpec((3 * rows, LANES), lambda g, off: (0, 0)),
            pl.BlockSpec((TABLE, rows), lambda g, off: (0, 0)),
            pl.BlockSpec((rows, LANES), lambda g, off: (0, 0)),
        ]
    )
    if base:
        operands.append(before)
        in_specs.append(pl.BlockSpec((ADAPTER_RANK, base), lambda g, off: (0, 0)))
    pushes = rows * groups * 2 * keys // 256 * 4
    return pl.pallas_call(
        functools.partial(attend_body, steps, units, base),
        grid_spec=pltpu.PrefetchScalarGridSpec(
            num_scalar_prefetch=1,
            grid=(steps,),
            in_specs=in_specs,
            out_specs=pl.BlockSpec((ADAPTER_RANK, total), lambda g, off: (0, 0)),
            scratch_shapes=[
                pltpu.VMEM((2, 2 * tile, keys), jnp.float32),
                pltpu.VMEM((2, 2 * tile, keys), jnp.bfloat16),
                pltpu.VMEM((2, 3 * rows, 2 * LANES), jnp.bfloat16),
                pltpu.VMEM((2, 3 * rows, 2 * LANES), jnp.bfloat16),
                pltpu.VMEM((2, rows, 2 * LANES), jnp.bfloat16),
            ],
        ),
        out_shape=jax.ShapeDtypeStruct((ADAPTER_RANK, total), jnp.bfloat16),
        cost_estimate=pl.CostEstimate(
            flops=pushes * 256 * 256 * 2 + 2 * rows * depth * 2 * LANES * groups,
            bytes_accessed=groups * rows * LANES * 20 + 4 * LANES * groups * depth,
            transcendentals=rows * groups * 2 * keys,
        ),
        compiler_params=pltpu.CompilerParams(vmem_limit_bytes=GRANT),
    )(first, *operands)


def finish_body(*refs):
    q_ref, k_ref, v_ref = refs[-3:]
    mine = refs[0][...].astype(jnp.float32) + refs[1][...].astype(jnp.float32)
    total = jnp.sum(mine * mine, keepdims=True)
    if len(refs) == 7:
        theirs = refs[2][...].astype(jnp.float32) + refs[3][...].astype(jnp.float32)
        total = total + jnp.sum(theirs * theirs, keepdims=True)
    else:
        total = refs[2][0:1, 0:1]
    count = float(ADAPTER_RANK * (QUERY_HEADS + 2 * KEY_VALUE_HEADS) * HEAD_SIZE)
    mine = mine * jnp.sqrt(count / (total + 1e-06))
    for g in range(k_ref.shape[1] // LANES):
        at = 4 * LANES * g
        q_ref[:, 2 * LANES * g : 2 * LANES * (g + 1)] = mine[:, at : at + 2 * LANES]
        k_ref[:, LANES * g : LANES * (g + 1)] = mine[:, at + 2 * LANES : at + 3 * LANES]
        v_ref[:, LANES * g : LANES * (g + 1)] = mine[:, at + 3 * LANES : at + 4 * LANES]


def local(
    layer_input,
    norm_weight,
    document_index,
    stored_queries,
    stored_keys,
    stored_values,
    output_weight,
    projection_gradient,
    adapter_down_maps,
):
    rows = stored_queries.shape[0]
    heads_width = stored_queries.shape[1]
    groups = stored_keys.shape[1] // HEAD_SIZE
    tp, ctx = lax.axis_size("tp"), lax.axis_size("ctx")
    tp_at, ctx_at = lax.axis_index("tp"), lax.axis_index("ctx")
    chunks = 2 if groups % 4 == 0 else 1
    units = chunks
    steps = groups // (chunks * units)
    width = 2 * LANES
    half = heads_width // width
    per = half // chunks
    scalar = lambda value: jnp.asarray(value, jnp.int32).reshape(1)
    gain = norm_weight.astype(jnp.float32)[None, :]
    down = (adapter_down_maps.T.astype(jnp.float32) * gain).astype(jnp.bfloat16)

    received = []
    for c in range(chunks):
        got = []
        for d in range(1, tp):
            first = scalar(((tp_at + d) % tp) * half + c * per)
            if c == 0 and d == 1:
                part, low, *packs = open_call(
                    projection_gradient,
                    output_weight,
                    first,
                    per,
                    width,
                    layer_input,
                    down,
                    stored_keys,
                    stored_values,
                    chunks,
                )
            else:
                part = project(projection_gradient, output_weight, first, per, width)
            got.append(lax.ppermute(part, "tp", [(at, (at + d) % tp) for at in range(tp)]))
        total = got[0]
        if len(got) > 1:
            total = sum(one.astype(jnp.float32) for one in got)
        received.append(total)

    move = 1
    while 2 * move < tp:
        low = low + xor_move(low, "tp", move)
        move *= 2
    other = xor_move(low, "tp", move)
    table = pl.pallas_call(table_body, out_shape=jax.ShapeDtypeStruct((TABLE, rows), jnp.bfloat16))(
        low, other, document_index[None, :]
    )
    table2 = shifted(table, "ctx", 2)
    table1 = shifted(table, "ctx", 1)
    prepare = pl.pallas_call(
        prep_body,
        grid_spec=pltpu.PrefetchScalarGridSpec(
            num_scalar_prefetch=1,
            grid=(1,),
            in_specs=[pl.BlockSpec((TABLE, rows), lambda i, off: (0, 0))] * 3,
            out_specs=[
                pl.BlockSpec((3 * rows, LANES), lambda i, off: (0, 0)),
                pl.BlockSpec((rows, LANES), lambda i, off: (0, 0)),
            ],
        ),
        out_shape=[
            jax.ShapeDtypeStruct((3 * rows, LANES), jnp.bfloat16),
            jax.ShapeDtypeStruct((rows, LANES), jnp.int32),
        ],
    )
    ext, starts = prepare(scalar(2 * rows - ctx_at * rows), table2, table1, table)

    second = (ctx_at % 2) == 1
    sums = None
    for c in range(chunks):
        own = packs[c]
        far = shifted(own, "ctx", 2)
        near = xor_move(jnp.where(second, far, own), "ctx", 1)
        first = scalar((tp_at * half + c * per) // units)
        sums = attend(
            stored_queries,
            projection_gradient,
            output_weight,
            received[c],
            (far, near, own),
            ext,
            table,
            starts,
            first,
            c * steps,
            steps,
            units,
            sums,
        )

    order = [1] + [1 << at for at in range(2, ctx.bit_length() - 1)]
    for move in order:
        sums = (sums.astype(jnp.float32) + xor_move(sums, "ctx", move).astype(jnp.float32)).astype(jnp.bfloat16)
    last = [sums, xor_move(sums, "ctx", 2)]
    if tp == 2:
        both = [(at, at ^ 5) for at in range(2 * ctx)]
        last = last + [xor_move(sums, "tp", 1), lax.ppermute(sums, ("ctx", "tp"), both)]
    else:
        squared = jnp.sum(jnp.square(last[0].astype(jnp.float32) + last[1].astype(jnp.float32))).reshape(1, 1)
        move = 1
        while move < tp:
            squared = squared + xor_move(squared, "tp", move)
            move *= 2
        last.append(squared)
    sizes = (heads_width, groups * HEAD_SIZE, groups * HEAD_SIZE)
    return pl.pallas_call(
        finish_body,
        out_shape=[jax.ShapeDtypeStruct((ADAPTER_RANK, size), jnp.float32) for size in sizes],
    )(*last)


def solution(mesh):
    placed = (
        P("ctx", "tp"),
        P("tp"),
        P("ctx"),
        P("ctx", "tp"),
        P("ctx", "tp"),
        P("ctx", "tp"),
        P(None, "tp"),
        P("ctx", "tp"),
        P("tp", None),
    )
    return jax.shard_map(
        local,
        mesh=mesh,
        in_specs=placed,
        out_specs=(P(None, "tp"), P(None, "tp"), P(None, "tp")),
        check_vma=False,
    )
```

profile of v0, /device:TPU:0, one launch (start us, length us, event | category | flops | bytes accessed | tf_op | source)
XLA Modules:
  0.0 147.8 jit_solution(3540251194932050372)
XLA Ops:
  1.3 1.6 %fusion.down_ref = bf16[24,2688]{1,0:T(8,128)(2,1)} fusion(bf16[2688,24]{0,1:T(8,128)(2,1)} %param.17, f32[2688]{0:T(1024)S(1)} %convert_element_type.40), kind=kLoop, calls=%fused_computation.6 | loop fusion | flops 193536 | bytes 268800 | tf_op jit(solution)/shard_map/convert_element_type | solution.py:390
  2.9 10.0 %shard_map.113 = (bf16[512,1024]{1,0:T(8,128)(2,1)}, f32[32,512]{1,0:T(8,128)}, bf16[512,1024]{1,0:T(8,128)(2,1)}, bf16[512,1024]{1,0:T(8,128)(2,1)}) custom-call(s32[1]{0:T(128)} %bitcast.2.offset_ref, bf16[512,2688]{1,0:T(8,128)(2,1)} %pg_ref.3, bf16[4096,2688]{1,0:T(8,128)(2,1)} %w_ref.3, bf16[512,2688]{1,0:T(8,128)(2,1)} %x_ref.1, ...), custom_call_target="tpu_custom_call" | custom-call | flops 2818572288 | bytes 12058624 | tf_op jit(solution)/shard_map/pallas_call | solution.py:97
  12.9 5.1 %collective-permute-start.7 = (bf16[512,1024]{1,0:T(8,128)(2,1)}, bf16[512,1024]{1,0:T(8,128)(2,1)S(1)}, u32[]{:S(2)}, u32[]{:S(2)}) collective-permute-start(bf16[512,1024]{1,0:T(8,128)(2,1)} %get-tuple-element.14.k2.v2), channel_id=1, source_target_pairs={{0,4},{2,6},{4,8},{6,10},{8,12},{10,14},{12,16},{14,18},{16,20},{1... | collective-permute-start | bytes 3145736 | tf_op jit(solution)/shard_map/ppermute | solution.py:36
  18.0 1.6 %collective-permute-start.6 = (bf16[512,1024]{1,0:T(8,128)(2,1)}, bf16[512,1024]{1,0:T(8,128)(2,1)}, u32[]{:S(2)}, u32[]{:S(2)}) collective-permute-start(bf16[512,1024]{1,0:T(8,128)(2,1)} %get-tuple-element.13), channel_id=1, source_target_pairs={{0,1},{1,0},{2,3},{3,2},{4,5},{5,4},{6,7},{7,6},{8,9},{9,8},{10,11... | collective-permute-start | bytes 3145736 | tf_op jit(solution)/shard_map/ppermute | solution.py:412
  19.6 4.3 %collective-permute-start.1 = (bf16[512,1024]{1,0:T(8,128)(2,1)}, bf16[512,1024]{1,0:T(8,128)(2,1)}, u32[]{:S(2)}, u32[]{:S(2)}) collective-permute-start(bf16[512,1024]{1,0:T(8,128)(2,1)} %get-tuple-element.9.k2.v2), channel_id=1, source_target_pairs={{0,4},{2,6},{4,8},{6,10},{8,12},{10,14},{12,16},{14,18},{16,20},{1... | collective-permute-start | bytes 3145736 | tf_op jit(solution)/shard_map/ppermute | solution.py:36
  23.9 17.9 %collective-permute-done.7.k0.v0 = bf16[512,1024]{1,0:T(8,128)(2,1)S(1)} collective-permute-done((bf16[512,1024]{1,0:T(8,128)(2,1)}, bf16[512,1024]{1,0:T(8,128)(2,1)S(1)}, u32[]{:S(2)}, u32[]{:S(2)}) %collective-permute-start.7) | collective-permute-done | bytes 1048608 | tf_op jit(solution)/shard_map/ppermute | solution.py:36
  41.8 2.7 %broadcast_select_fusion = bf16[512,1024]{1,0:T(8,128)(2,1)} fusion(bf16[512,1024]{1,0:T(8,128)(2,1)S(1)} %collective-permute-done.7.k0.v0, bf16[512,1024]{1,0:T(8,128)(2,1)} %get-tuple-element.14.k2.v2, pred[]{:T(512)S(6)} %eq.7), kind=kLoop, calls=%fused_computation | loop fusion | flops 524288 | bytes 3145729 | tf_op jit(solution)/shard_map/jit(_where)/select_n | solution.py:451
  44.5 1.5 %collective-permute-start.3 = (f32[32,512]{1,0:T(8,128)S(1)}, f32[32,512]{1,0:T(8,128)S(1)}, u32[]{:S(2)}, u32[]{:S(2)}) collective-permute-start(f32[32,512]{1,0:T(8,128)S(1)} %copy-done.3), channel_id=1, source_target_pairs={{0,1},{1,0},{2,3},{3,2},{4,5},{5,4},{6,7},{7,6},{8,9},{9,8},{10,11... | collective-permute-start | bytes 196616 | tf_op jit(solution)/shard_map/ppermute | solution.py:40
  46.0 3.0 %collective-permute-done.3.theirs_ref = f32[32,512]{1,0:T(8,128)S(1)} collective-permute-done((f32[32,512]{1,0:T(8,128)S(1)}, f32[32,512]{1,0:T(8,128)S(1)}, u32[]{:S(2)}, u32[]{:S(2)}) %collective-permute-start.3) | collective-permute-done | bytes 65568 | tf_op jit(solution)/shard_map/ppermute | solution.py:40
  49.6 1.5 %shard_map.114.t0_ref.lq_ref = bf16[32,512]{1,0:T(8,128)(2,1)} custom-call(f32[32,512]{1,0:T(8,128)} %get-tuple-element.10.mine_ref, f32[32,512]{1,0:T(8,128)} %copy-done.7, s32[1,512]{1,0:T(1,128)} %bitcast.8), custom_call_target="tpu_custom_call" | custom-call | tf_op jit(solution)/shard_map/pallas_call | solution.py:423
  51.1 4.3 %collective-permute-start.4 = (bf16[32,512]{1,0:T(8,128)(2,1)}, bf16[32,512]{1,0:T(8,128)(2,1)S(1)}, u32[]{:S(2)}, u32[]{:S(2)}) collective-permute-start(bf16[32,512]{1,0:T(8,128)(2,1)} %shard_map.114.t0_ref.lq_ref), channel_id=1, source_target_pairs={{0,4},{2,6},{4,8},{6,10},{8,12},{10,14},{12,16},{14,18},{16,20},{1... | collective-permute-start | bytes 98312 | tf_op jit(solution)/shard_map/ppermute | solution.py:36
  56.8 7.4 %shard_map.112 = bf16[512,1024]{1,0:T(8,128)(2,1)} custom-call(s32[1]{0:T(128)} %bitcast.1.offset_ref, bf16[512,2688]{1,0:T(8,128)(2,1)} %pg_ref.3, bf16[4096,2688]{1,0:T(8,128)(2,1)} %w_ref.3), custom_call_target="tpu_custom_call" | custom-call | flops 2818572288 | bytes 9306112 | tf_op jit(solution)/shard_map/pallas_call | solution.py:49
  64.3 1.5 %collective-permute-start = (bf16[512,1024]{1,0:T(8,128)(2,1)}, bf16[512,1024]{1,0:T(8,128)(2,1)}, u32[]{:S(2)}, u32[]{:S(2)}) collective-permute-start(bf16[512,1024]{1,0:T(8,128)(2,1)} %shard_map.112), channel_id=1, source_target_pairs={{0,1},{1,0},{2,3},{3,2},{4,5},{5,4},{6,7},{7,6},{8,9},{9,8},{10,11... | collective-permute-start | bytes 3145736 | tf_op jit(solution)/shard_map/ppermute | solution.py:412
  66.4 2.1 %shard_map.115 = (bf16[1536,128]{1,0:T(8,128)(2,1)}, s32[512,128]{1,0:T(8,128)}) custom-call(s32[1]{0:T(128)} %bitcast.4.first_ref, bf16[32,512]{1,0:T(8,128)(2,1)} %copy-done.8, bf16[32,512]{1,0:T(8,128)(2,1)} %copy-done.9, bf16[32,512]{1,0:T(8,128)(2,1)} %shard_map.114.t0_ref.lq_ref), custom_call_target="tpu_custom_call" | custom-call | tf_op jit(solution)/shard_map/pallas_call | solution.py:444
  69.6 4.0 %collective-permute-start.2 = (bf16[512,1024]{1,0:T(8,128)(2,1)}, bf16[512,1024]{1,0:T(8,128)(2,1)S(1)}, u32[]{:S(2)}, u32[]{:S(2)}) collective-permute-start(bf16[512,1024]{1,0:T(8,128)(2,1)} %broadcast_select_fusion.1), channel_id=1, source_target_pairs={{0,2},{2,0},{4,6},{6,4},{8,10},{10,8},{12,14},{14,12},{16,18},{18,... | collective-permute-start | bytes 3145736 | tf_op jit(solution)/shard_map/ppermute | solution.py:40
  73.7 26.2 %shard_map.116.rest_0_ = bf16[8,2048]{1,0:T(8,128)(2,1)} custom-call(s32[1]{0:T(128)} %bitcast.6.offset_ref, bf16[512,2048]{1,0:T(8,128)(2,1)} %q_ref.3, bf16[512,2688]{1,0:T(8,128)(2,1)} %pg_ref.3, bf16[4096,2688]{1,0:T(8,128)(2,1)} %w_ref.3, bf16[512,1024]{1,0:T(8,128)(2,1)} %collective-permute-done.6.recv_ref, bf16[512,1024]{1,0:T(8,128)(2,1)} %copy-done.1, ...), custom_call_target="tpu_custom_call" | custom-call | flops 13555990528 | bytes 10747904 | tf_op jit(solution)/shard_map/pallas_call | solution.py:323
  100.9 26.3 %shard_map.117 = bf16[8,4096]{1,0:T(8,128)(2,1)} custom-call(s32[1]{0:T(128)} %bitcast.offset_ref, bf16[512,2048]{1,0:T(8,128)(2,1)} %q_ref.3, bf16[512,2688]{1,0:T(8,128)(2,1)} %pg_ref.3, bf16[4096,2688]{1,0:T(8,128)(2,1)} %w_ref.3, bf16[512,1024]{1,0:T(8,128)(2,1)} %collective-permute-done.recv_ref, bf16[512,1024]{1,0:T(8,128)(2,1)} %collective-permute-done.1.k0.v0, ...), custom_call_target="tpu_custom_call" | custom-call | flops 13555990528 | bytes 10747904 | tf_op jit(solution)/shard_map/pallas_call | solution.py:323
  127.1 1.5 collective-permute-done.9
  129.5 1.6 %collective-permute-start.10 = (bf16[8,4096]{1,0:T(8,128)(2,1)S(1)}, bf16[8,4096]{1,0:T(8,128)(2,1)S(1)}, u32[]{:S(2)}, u32[]{:S(2)}) collective-permute-start(bf16[8,4096]{1,0:T(8,128)(2,1)S(1)} %add_convert_fusion.2), channel_id=1, source_target_pairs={{0,8},{2,10},{4,12},{6,14},{8,0},{10,2},{12,4},{14,6},{16,24},{18,... | collective-permute-start | bytes 196616 | tf_op jit(solution)/shard_map/ppermute | solution.py:40
  131.1 2.7 %collective-permute-done.10 = bf16[8,4096]{1,0:T(8,128)(2,1)S(1)} collective-permute-done((bf16[8,4096]{1,0:T(8,128)(2,1)S(1)}, bf16[8,4096]{1,0:T(8,128)(2,1)S(1)}, u32[]{:S(2)}, u32[]{:S(2)}) %collective-permute-start.10) | collective-permute-done | bytes 65568 | tf_op jit(solution)/shard_map/ppermute | solution.py:40
  133.8 2.6 %collective-permute-start.11 = (bf16[8,4096]{1,0:T(8,128)(2,1)S(1)}, bf16[8,4096]{1,0:T(8,128)(2,1)S(1)}, u32[]{:S(2)}, u32[]{:S(2)}) collective-permute-start(bf16[8,4096]{1,0:T(8,128)(2,1)S(1)} %add_convert_fusion.1), channel_id=1, source_target_pairs={{0,16},{2,18},{4,20},{6,22},{8,24},{10,26},{12,28},{14,30},{16,0},... | collective-permute-start | bytes 196616 | tf_op jit(solution)/shard_map/ppermute | solution.py:40
  136.4 2.6 %collective-permute-done.11 = bf16[8,4096]{1,0:T(8,128)(2,1)S(1)} collective-permute-done((bf16[8,4096]{1,0:T(8,128)(2,1)S(1)}, bf16[8,4096]{1,0:T(8,128)(2,1)S(1)}, u32[]{:S(2)}, u32[]{:S(2)}) %collective-permute-start.11) | collective-permute-done | bytes 65568 | tf_op jit(solution)/shard_map/ppermute | solution.py:40
  140.2 2.4 %collective-permute-start.14 = (bf16[8,4096]{1,0:T(8,128)(2,1)S(1)}, bf16[8,4096]{1,0:T(8,128)(2,1)S(1)}, u32[]{:S(2)}, u32[]{:S(2)}) collective-permute-start(bf16[8,4096]{1,0:T(8,128)(2,1)S(1)} %add_convert_fusion.refs_0_), channel_id=1, source_target_pairs={{0,5},{1,4},{2,7},{3,6},{4,1},{5,0},{6,3},{7,2},{8,13},{9,12},{10,... | collective-permute-start | bytes 196616 | tf_op jit(solution)/shard_map/ppermute | solution.py:475
  146.0 1.8 %shard_map.118 = (f32[8,2048]{1,0:T(8,128)}, f32[8,1024]{1,0:T(8,128)}, f32[8,1024]{1,0:T(8,128)}) custom-call(bf16[8,4096]{1,0:T(8,128)(2,1)} %copy-done.2, bf16[8,4096]{1,0:T(8,128)(2,1)} %copy-done.4, bf16[8,4096]{1,0:T(8,128)(2,1)} %copy-done.5, bf16[8,4096]{1,0:T(8,128)(2,1)} %copy-done.6), custom_call_target="tpu_custom_call" | custom-call | tf_op jit(solution)/shard_map/pallas_call | solution.py:484
  (42 shorter events, 10.9 us)
Async XLA Ops:
  12.9 31.6 %copy-start.3 = (f32[32,512]{1,0:T(8,128)S(1)}, f32[32,512]{1,0:T(8,128)}, u32[]{:S(2)}) copy-start(f32[32,512]{1,0:T(8,128)} %get-tuple-element.10.mine_ref) | copy-start | bytes 196612
  12.9 28.9 %collective-permute-start.7 = (bf16[512,1024]{1,0:T(8,128)(2,1)}, bf16[512,1024]{1,0:T(8,128)(2,1)S(1)}, u32[]{:S(2)}, u32[]{:S(2)}) collective-permute-start(bf16[512,1024]{1,0:T(8,128)(2,1)} %get-tuple-element.14.k2.v2), channel_id=1, source_target_pairs={{0,4},{2,6},{4,8},{6,10},{8,12},{10,14},{12,16},{14,18},{16,20},{1... | collective-permute-start | bytes 3145736 | tf_op jit(solution)/shard_map/ppermute | solution.py:36
  18.0 55.6 %collective-permute-start.6 = (bf16[512,1024]{1,0:T(8,128)(2,1)}, bf16[512,1024]{1,0:T(8,128)(2,1)}, u32[]{:S(2)}, u32[]{:S(2)}) collective-permute-start(bf16[512,1024]{1,0:T(8,128)(2,1)} %get-tuple-element.13), channel_id=1, source_target_pairs={{0,1},{1,0},{2,3},{3,2},{4,5},{5,4},{6,7},{7,6},{8,9},{9,8},{10,11... | collective-permute-start | bytes 3145736 | tf_op jit(solution)/shard_map/ppermute | solution.py:412
  19.6 48.9 %collective-permute-start.1 = (bf16[512,1024]{1,0:T(8,128)(2,1)}, bf16[512,1024]{1,0:T(8,128)(2,1)}, u32[]{:S(2)}, u32[]{:S(2)}) collective-permute-start(bf16[512,1024]{1,0:T(8,128)(2,1)} %get-tuple-element.9.k2.v2), channel_id=1, source_target_pairs={{0,4},{2,6},{4,8},{6,10},{8,12},{10,14},{12,16},{14,18},{16,20},{1... | collective-permute-start | bytes 3145736 | tf_op jit(solution)/shard_map/ppermute | solution.py:36
  41.8 15.0 %copy-start.1 = (bf16[512,1024]{1,0:T(8,128)(2,1)}, bf16[512,1024]{1,0:T(8,128)(2,1)S(1)}, u32[]{:S(2)}) copy-start(bf16[512,1024]{1,0:T(8,128)(2,1)S(1)} %collective-permute-done.7.k0.v0) | copy-start | bytes 3145732
  44.5 29.1 %collective-permute-start.8 = (bf16[512,1024]{1,0:T(8,128)(2,1)}, bf16[512,1024]{1,0:T(8,128)(2,1)}, u32[]{:S(2)}, u32[]{:S(2)}) collective-permute-start(bf16[512,1024]{1,0:T(8,128)(2,1)} %broadcast_select_fusion), channel_id=1, source_target_pairs={{0,2},{2,0},{4,6},{6,4},{8,10},{10,8},{12,14},{14,12},{16,18},{18,... | collective-permute-start | bytes 3145736 | tf_op jit(solution)/shard_map/ppermute | solution.py:40
  44.5 4.5 %collective-permute-start.3 = (f32[32,512]{1,0:T(8,128)S(1)}, f32[32,512]{1,0:T(8,128)S(1)}, u32[]{:S(2)}, u32[]{:S(2)}) collective-permute-start(f32[32,512]{1,0:T(8,128)S(1)} %copy-done.3), channel_id=1, source_target_pairs={{0,1},{1,0},{2,3},{3,2},{4,5},{5,4},{6,7},{7,6},{8,9},{9,8},{10,11... | collective-permute-start | bytes 196616 | tf_op jit(solution)/shard_map/ppermute | solution.py:40
  49.0 0.6 copy-start.7
  51.1 13.1 %collective-permute-start.4 = (bf16[32,512]{1,0:T(8,128)(2,1)}, bf16[32,512]{1,0:T(8,128)(2,1)S(1)}, u32[]{:S(2)}, u32[]{:S(2)}) collective-permute-start(bf16[32,512]{1,0:T(8,128)(2,1)} %shard_map.114.t0_ref.lq_ref), channel_id=1, source_target_pairs={{0,4},{2,6},{4,8},{6,10},{8,12},{10,14},{12,16},{14,18},{16,20},{1... | collective-permute-start | bytes 98312 | tf_op jit(solution)/shard_map/ppermute | solution.py:36
  55.4 10.4 %collective-permute-start.5 = (bf16[32,512]{1,0:T(8,128)(2,1)}, bf16[32,512]{1,0:T(8,128)(2,1)S(1)}, u32[]{:S(2)}, u32[]{:S(2)}) collective-permute-start(bf16[32,512]{1,0:T(8,128)(2,1)} %shard_map.114.t0_ref.lq_ref), channel_id=1, source_target_pairs={{0,2},{2,4},{4,6},{6,8},{8,10},{10,12},{12,14},{14,16},{16,18},{18... | collective-permute-start | bytes 98312 | tf_op jit(solution)/shard_map/ppermute | solution.py:36
  56.8 11.7 %copy-start = (bf16[512,1024]{1,0:T(8,128)(2,1)S(1)}, bf16[512,1024]{1,0:T(8,128)(2,1)}, u32[]{:S(2)}) copy-start(bf16[512,1024]{1,0:T(8,128)(2,1)} %get-tuple-element.9.k2.v2) | copy-start | bytes 3145732
  64.3 1.5 %copy-start.8 = (bf16[32,512]{1,0:T(8,128)(2,1)}, bf16[32,512]{1,0:T(8,128)(2,1)S(1)}, u32[]{:S(2)}) copy-start(bf16[32,512]{1,0:T(8,128)(2,1)S(1)} %collective-permute-done.4.t2_ref) | copy-start | bytes 98308
  64.3 35.6 %collective-permute-start = (bf16[512,1024]{1,0:T(8,128)(2,1)}, bf16[512,1024]{1,0:T(8,128)(2,1)}, u32[]{:S(2)}, u32[]{:S(2)}) collective-permute-start(bf16[512,1024]{1,0:T(8,128)(2,1)} %shard_map.112), channel_id=1, source_target_pairs={{0,1},{1,0},{2,3},{3,2},{4,5},{5,4},{6,7},{7,6},{8,9},{9,8},{10,11... | collective-permute-start | bytes 3145736 | tf_op jit(solution)/shard_map/ppermute | solution.py:412
  69.6 30.3 %collective-permute-start.2 = (bf16[512,1024]{1,0:T(8,128)(2,1)}, bf16[512,1024]{1,0:T(8,128)(2,1)S(1)}, u32[]{:S(2)}, u32[]{:S(2)}) collective-permute-start(bf16[512,1024]{1,0:T(8,128)(2,1)} %broadcast_select_fusion.1), channel_id=1, source_target_pairs={{0,2},{2,0},{4,6},{6,4},{8,10},{10,8},{12,14},{14,12},{16,18},{18,... | collective-permute-start | bytes 3145736 | tf_op jit(solution)/shard_map/ppermute | solution.py:40
  99.9 1.0 copy-start.10
  127.1 1.5 collective-permute-start.9
  129.5 4.3 %collective-permute-start.10 = (bf16[8,4096]{1,0:T(8,128)(2,1)S(1)}, bf16[8,4096]{1,0:T(8,128)(2,1)S(1)}, u32[]{:S(2)}, u32[]{:S(2)}) collective-permute-start(bf16[8,4096]{1,0:T(8,128)(2,1)S(1)} %add_convert_fusion.2), channel_id=1, source_target_pairs={{0,8},{2,10},{4,12},{6,14},{8,0},{10,2},{12,4},{14,6},{16,24},{18,... | collective-permute-start | bytes 196616 | tf_op jit(solution)/shard_map/ppermute | solution.py:40
  133.8 5.2 %collective-permute-start.11 = (bf16[8,4096]{1,0:T(8,128)(2,1)S(1)}, bf16[8,4096]{1,0:T(8,128)(2,1)S(1)}, u32[]{:S(2)}, u32[]{:S(2)}) collective-permute-start(bf16[8,4096]{1,0:T(8,128)(2,1)S(1)} %add_convert_fusion.1), channel_id=1, source_target_pairs={{0,16},{2,18},{4,20},{6,22},{8,24},{10,26},{12,28},{14,30},{16,0},... | collective-permute-start | bytes 196616 | tf_op jit(solution)/shard_map/ppermute | solution.py:40
  139.1 6.3 %copy-start.2 = (bf16[8,4096]{1,0:T(8,128)(2,1)}, bf16[8,4096]{1,0:T(8,128)(2,1)S(1)}, u32[]{:S(2)}) copy-start(bf16[8,4096]{1,0:T(8,128)(2,1)S(1)} %add_convert_fusion.refs_0_) | copy-start | bytes 196612
  139.1 4.3 %collective-permute-start.12 = (bf16[8,4096]{1,0:T(8,128)(2,1)S(1)}, bf16[8,4096]{1,0:T(8,128)(2,1)S(1)}, u32[]{:S(2)}, u32[]{:S(2)}) collective-permute-start(bf16[8,4096]{1,0:T(8,128)(2,1)S(1)} %add_convert_fusion.refs_0_), channel_id=1, source_target_pairs={{0,4},{2,6},{4,0},{6,2},{8,12},{10,14},{12,8},{14,10},{16,20},{18,... | collective-permute-start | bytes 196616 | tf_op jit(solution)/shard_map/ppermute | solution.py:40
  139.7 4.3 %collective-permute-start.13 = (bf16[8,4096]{1,0:T(8,128)(2,1)S(1)}, bf16[8,4096]{1,0:T(8,128)(2,1)S(1)}, u32[]{:S(2)}, u32[]{:S(2)}) collective-permute-start(bf16[8,4096]{1,0:T(8,128)(2,1)S(1)} %add_convert_fusion.refs_0_), channel_id=1, source_target_pairs={{0,1},{1,0},{2,3},{3,2},{4,5},{5,4},{6,7},{7,6},{8,9},{9,8},{10,11... | collective-permute-start | bytes 196616 | tf_op jit(solution)/shard_map/ppermute | solution.py:40
  140.2 5.2 %collective-permute-start.14 = (bf16[8,4096]{1,0:T(8,128)(2,1)S(1)}, bf16[8,4096]{1,0:T(8,128)(2,1)S(1)}, u32[]{:S(2)}, u32[]{:S(2)}) collective-permute-start(bf16[8,4096]{1,0:T(8,128)(2,1)S(1)} %add_convert_fusion.refs_0_), channel_id=1, source_target_pairs={{0,5},{1,4},{2,7},{3,6},{4,1},{5,0},{6,3},{7,2},{8,13},{9,12},{10,... | collective-permute-start | bytes 196616 | tf_op jit(solution)/shard_map/ppermute | solution.py:475
  143.4 2.0 %copy-start.4 = (bf16[8,4096]{1,0:T(8,128)(2,1)}, bf16[8,4096]{1,0:T(8,128)(2,1)S(1)}, u32[]{:S(2)}) copy-start(bf16[8,4096]{1,0:T(8,128)(2,1)S(1)} %collective-permute-done.12.refs_1_) | copy-start | bytes 196612
  144.0 1.4 copy-start.5
  (2 other events, 1.2 us)
where the time goes:
time: 148 us
  Pallas kernels  75.3 us (51%)
  starting transfers between devices  31.6 us (21%)
  waiting for transfers between devices  30.4 us (21%)
  other arithmetic  6.97 us (5%)
  local copies, waits for them, and re-layouts  2.86 us (2%)
    pallas_call x2, Pallas kernels, attend(): pl.pallas_call(functools.partial(attend_body, steps, units, base), grid_s...  52.5 us
    ppermute x4, waiting for transfers between devices, shifted(): lax.ppermute(value, axis, [(source, source + steps) for source in range(f...  17.9 us
    ppermute x4, starting transfers between devices, shifted(): lax.ppermute(value, axis, [(source, source + steps) for source in range(f...  15.1 us
    ppermute x8, waiting for transfers between devices, xor_move(): lax.ppermute(value, axis, [(at, at ^ step) for at in range(lax.axis_size(...  11.1 us
    ppermute x8, starting transfers between devices, xor_move(): lax.ppermute(value, axis, [(at, at ^ step) for at in range(lax.axis_size(...  11 us
    pallas_call x1, Pallas kernels, open_call(): pl.pallas_call(functools.partial(open_body, chunks), grid_spec=pltpu.Pref...  10 us
    pallas_call x1, Pallas kernels, project(): pl.pallas_call(project_body, grid_spec=pltpu.PrefetchScalarGridSpec(num_s...  7.43 us
    select_n x2, other arithmetic, local(): near = xor_move(jnp.where(second, far, own), 'ctx', 1)  3.8 us
  transfers between devices with their start and end apart: 15, of which 8 were waited for; matrix products, arithmetic and copies ran while one was open for 3% of the time, Pallas kernels for 25%

commit v1 on v0

--- a/solution.py
+++ b/solution.py
@@ -67,15 +67,21 @@
     )(first_block, gradient, weight)
 
 
-def open_body(chunks, offset_ref, gradient_ref, weight_ref, x_ref, down_ref, k_ref, v_ref, out_ref, low_ref, *packs):
+def open_body(each, offset_ref, gradient_ref, weight_ref, x_ref, norm_ref, down_ref, *rest):
+    k_ref, v_ref, out_ref, low_ref, *packs, down_scr = rest
     step = pl.program_id(0)
     out_ref[...] = dotf(gradient_ref[...], weight_ref[...], NT).astype(out_ref.dtype)
-    low_ref[0 : 3 * ADAPTER_RANK, :] = dotf(down_ref[...], x_ref[...], NT)
+
+    @pl.when(step == 0)
+    def _():
+        gain = norm_ref[...].astype(jnp.float32).reshape(1, -1)
+        down_scr[...] = (down_ref[...].astype(jnp.float32) * gain).astype(jnp.bfloat16)
+
+    low_ref[0 : 3 * ADAPTER_RANK, :] = dotf(down_scr[...], x_ref[...], NT)
     hidden = x_ref[...].astype(jnp.float32)
     ones = jnp.ones((ADAPTER_RANK, hidden.shape[1]), jnp.bfloat16)
     low_ref[3 * ADAPTER_RANK :, :] = dotf(ones, (hidden * hidden).astype(jnp.bfloat16), NT)
     wide = k_ref.shape[1]
-    each = pl.num_programs(0) // chunks
     for c, pack_ref in enumerate(packs):
 
         @pl.when(step // each == c)
@@ -84,18 +90,35 @@
             pack_ref[:, wide:] = v_ref[...]
 
 
-def open_call(gradient, weight, first_block, blocks, width, x, down, keys, values, chunks):
+def pack_body(k_ref, v_ref, out_ref):
+    wide = k_ref.shape[1]
+    out_ref[:, :wide] = k_ref[...]
+    out_ref[:, wide:] = v_ref[...]
+
+
+def pack_call(keys, values, wide, blocks):
+    rows = keys.shape[0]
+    return pl.pallas_call(
+        pack_body,
+        grid=(blocks,),
+        in_specs=[pl.BlockSpec((rows, wide), lambda i: (0, i))] * 2,
+        out_specs=pl.BlockSpec((rows, 2 * wide), lambda i: (0, i)),
+        out_shape=jax.ShapeDtypeStruct((rows, 2 * wide * blocks), keys.dtype),
+        compiler_params=pltpu.CompilerParams(vmem_limit_bytes=GRANT),
+    )(keys, values)
+
+
+def open_call(gradient, weight, first_block, blocks, width, x, norm, down, keys, values, chunks):
     rows, depth = gradient.shape
     slab = rows // blocks
     wide = keys.shape[1] // blocks
     each = blocks // chunks
-    pack_specs = [
-        pl.BlockSpec((rows, 2 * wide), lambda i, off, c=c: (0, jnp.clip(i - c * each, 0, each - 1)))
-        for c in range(chunks)
-    ]
+    skip = each
+    extra = chunks - 1
+    pack_specs = [pl.BlockSpec((rows, 2 * wide), lambda i, off: (0, jnp.minimum(i, each - 1)))] * extra
     pack_shape = jax.ShapeDtypeStruct((rows, 2 * wide * each), keys.dtype)
     return pl.pallas_call(
-        functools.partial(open_body, chunks),
+        functools.partial(open_body, each),
         grid_spec=pltpu.PrefetchScalarGridSpec(
             num_scalar_prefetch=1,
             grid=(blocks,),
@@ -103,28 +126,30 @@
                 pl.BlockSpec((rows, depth), lambda i, off: (0, 0)),
                 pl.BlockSpec((width, depth), lambda i, off: (off[0] + i, 0)),
                 pl.BlockSpec((slab, depth), lambda i, off: (i, 0)),
+                pl.BlockSpec((depth,), lambda i, off: (0,)),
                 pl.BlockSpec((3 * ADAPTER_RANK, depth), lambda i, off: (0, 0)),
-                pl.BlockSpec((rows, wide), lambda i, off: (0, i)),
-                pl.BlockSpec((rows, wide), lambda i, off: (0, i)),
+                pl.BlockSpec((rows, wide), lambda i, off: (0, jnp.minimum(i + skip, blocks - 1))),
+                pl.BlockSpec((rows, wide), lambda i, off: (0, jnp.minimum(i + skip, blocks - 1))),
             ],
             out_specs=[
                 pl.BlockSpec((rows, width), lambda i, off: (0, i)),
                 pl.BlockSpec((TABLE, slab), lambda i, off: (0, i)),
             ]
             + pack_specs,
+            scratch_shapes=[pltpu.VMEM((3 * ADAPTER_RANK, depth), jnp.bfloat16)],
         ),
         out_shape=[
             jax.ShapeDtypeStruct((rows, blocks * width), jnp.bfloat16),
             jax.ShapeDtypeStruct((TABLE, rows), jnp.float32),
         ]
-        + [pack_shape] * chunks,
+        + [pack_shape] * extra,
         cost_estimate=pl.CostEstimate(
             flops=2 * rows * depth * width * blocks,
             bytes_accessed=2 * (2 * rows * depth + width * blocks * depth + rows * width * blocks),
             transcendentals=0,
         ),
         compiler_params=pltpu.CompilerParams(vmem_limit_bytes=GRANT),
-    )(first_block, gradient, weight, x, down, keys, values)
+    )(first_block, gradient, weight, x, norm, down, keys, values)
 
 
 def table_body(mine_ref, theirs_ref, doc_ref, out_ref):
@@ -156,7 +181,7 @@
 
 
 def attend_body(
-    steps, step_units, base, offset_ref, q_ref, pg_ref, w_ref, recv_ref, k0, k1, k2, v0, v1, v2, ext_ref, lq_ref, st_ref, *rest
+    steps, step_units, base, offset_ref, second_ref, q_ref, pg_ref, w_ref, recv_ref, k0, ka, kb, k2, v0, va, vb, v2, ext_ref, lq_ref, st_ref, *rest
 ):
     if base:
         before_ref, out_ref, s_scr, e_scr, ve, ke, do_scr = rest
@@ -184,10 +209,15 @@
             own = dotf(pg_ref[...], w_ref[2 * LANES * g : 2 * LANES * (g + 1), :], NT)
             got = recv_ref[:, 2 * LANES * g : 2 * LANES * (g + 1)].astype(jnp.float32)
             do_scr[g % 2] = (own + got).astype(jnp.bfloat16)
-            for b, (k_ref, v_ref) in enumerate(((k0, v0), (k1, v1), (k2, v2))):
+            for b, pair in enumerate((((k0, v0),), ((ka, va), (kb, vb)), ((k2, v2),))):
                 span = slice(b * rows, (b + 1) * rows)
-                ke[g % 2, span, :LANES] = k_ref[:, g * LANES : (g + 1) * LANES]
-                ve[g % 2, span, :LANES] = v_ref[:, g * LANES : (g + 1) * LANES]
+                cols = slice(g * LANES, (g + 1) * LANES)
+                key, value = pair[0][0][:, cols], pair[0][1][:, cols]
+                if len(pair) > 1:
+                    key = jnp.where(second_ref[0] == 1, pair[1][0][:, cols], key)
+                    value = jnp.where(second_ref[0] == 1, pair[1][1][:, cols], value)
+                ke[g % 2, span, :LANES] = key
+                ve[g % 2, span, :LANES] = value
                 ke[g % 2, span, LANES:] = ext_ref[span, :]
                 ve[g % 2, span, LANES:] = ext_ref[span, :]
         s = state[i]
@@ -291,7 +321,7 @@
             backed(i - 1)
 
 
-def attend(queries, gradient, weight, recv, packs, ext, table, starts, first, skip, steps, units, before):
+def attend(queries, gradient, weight, recv, packs, ext, table, starts, first, second, skip, steps, units, before):
     rows, depth = gradient.shape
     tile = rows // 2
     keys = LOOKBACK_SPAN + tile
@@ -303,30 +333,30 @@
     operands = [queries, gradient, weight, recv, *packs, *packs, ext, table, starts]
     in_specs = (
         [
-            col(2 * wide, lambda g, off: (0, g + skip)),
-            col(depth, lambda g, off: (0, 0)),
-            pl.BlockSpec((2 * wide, depth), lambda g, off: (g + off[0], 0)),
-            col(2 * wide, lambda g, off: (0, g)),
+            col(2 * wide, lambda g, off, sec: (0, g + skip)),
+            col(depth, lambda g, off, sec: (0, 0)),
+            pl.BlockSpec((2 * wide, depth), lambda g, off, sec: (g + off[0], 0)),
+            col(2 * wide, lambda g, off, sec: (0, g)),
         ]
-        + [col(wide, lambda g, off: (0, 2 * g))] * 3
-        + [col(wide, lambda g, off: (0, 2 * g + 1))] * 3
+        + [col(wide, lambda g, off, sec: (0, 2 * g))] * 4
+        + [col(wide, lambda g, off, sec: (0, 2 * g + 1))] * 4
         + [
-            pl.BlockSpec((3 * rows, LANES), lambda g, off: (0, 0)),
-            pl.BlockSpec((TABLE, rows), lambda g, off: (0, 0)),
-            pl.BlockSpec((rows, LANES), lambda g, off: (0, 0)),
+            pl.BlockSpec((3 * rows, LANES), lambda g, off, sec: (0, 0)),
+            pl.BlockSpec((TABLE, rows), lambda g, off, sec: (0, 0)),
+            pl.BlockSpec((rows, LANES), lambda g, off, sec: (0, 0)),
         ]
     )
     if base:
         operands.append(before)
-        in_specs.append(pl.BlockSpec((ADAPTER_RANK, base), lambda g, off: (0, 0)))
+        in_specs.append(pl.BlockSpec((ADAPTER_RANK, base), lambda g, off, sec: (0, 0)))
     pushes = rows * groups * 2 * keys // 256 * 4
     return pl.pallas_call(
         functools.partial(attend_body, steps, units, base),
         grid_spec=pltpu.PrefetchScalarGridSpec(
-            num_scalar_prefetch=1,
+            num_scalar_prefetch=2,
             grid=(steps,),
             in_specs=in_specs,
-            out_specs=pl.BlockSpec((ADAPTER_RANK, total), lambda g, off: (0, 0)),
+            out_specs=pl.BlockSpec((ADAPTER_RANK, total), lambda g, off, sec: (0, 0)),
             scratch_shapes=[
                 pltpu.VMEM((2, 2 * tile, keys), jnp.float32),
                 pltpu.VMEM((2, 2 * tile, keys), jnp.bfloat16),
@@ -341,8 +371,8 @@
             bytes_accessed=groups * rows * LANES * 20 + 4 * LANES * groups * depth,
             transcendentals=rows * groups * 2 * keys,
         ),
-        compiler_params=pltpu.CompilerParams(vmem_limit_bytes=GRANT),
-    )(first, *operands)
+        compiler_params=pltpu.CompilerParams(vmem_limit_bytes=40 << 20),
+    )(first, second, *operands)
 
 
 def finish_body(*refs):
@@ -386,8 +416,12 @@
     half = heads_width // width
     per = half // chunks
     scalar = lambda value: jnp.asarray(value, jnp.int32).reshape(1)
-    gain = norm_weight.astype(jnp.float32)[None, :]
-    down = (adapter_down_maps.T.astype(jnp.float32) * gain).astype(jnp.bfloat16)
+
+    pair = [(at, at + 1) for at in range(0, ctx, 2)]
+    packs = [pack_call(stored_keys, stored_values, units * LANES, steps)]
+    fars, befores = [], []
+    fars.append(shifted(packs[0], "ctx", 2))
+    befores.append(lax.ppermute(packs[0], "ctx", pair))
 
     received = []
     for c in range(chunks):
@@ -395,14 +429,15 @@
         for d in range(1, tp):
             first = scalar(((tp_at + d) % tp) * half + c * per)
             if c == 0 and d == 1:
-                part, low, *packs = open_call(
+                part, low, *more = open_call(
                     projection_gradient,
                     output_weight,
                     first,
                     per,
                     width,
                     layer_input,
-                    down,
+                    norm_weight,
+                    adapter_down_maps.T,
                     stored_keys,
                     stored_values,
                     chunks,
@@ -443,23 +478,26 @@
     )
     ext, starts = prepare(scalar(2 * rows - ctx_at * rows), table2, table1, table)
 
-    second = (ctx_at % 2) == 1
+    second = scalar(ctx_at % 2)
     sums = None
     for c in range(chunks):
-        own = packs[c]
-        far = shifted(own, "ctx", 2)
-        near = xor_move(jnp.where(second, far, own), "ctx", 1)
+        if c > 0:
+            packs.append(more[c - 1])
+            fars.append(shifted(packs[c], "ctx", 2))
+            befores.append(lax.ppermute(packs[c], "ctx", pair))
+        back = lax.ppermute(fars[c], "ctx", [(b, a) for a, b in pair])
         first = scalar((tp_at * half + c * per) // units)
         sums = attend(
             stored_queries,
             projection_gradient,
             output_weight,
             received[c],
-            (far, near, own),
+            (fars[c], back, befores[c], packs[c]),
             ext,
             table,
             starts,
             first,
+            second,
             c * steps,
             steps,
             units,

time: 148 us -> 148 us (level)
  other arithmetic: 6.97 us -> 0.06 us
  starting transfers between devices: 31.6 us -> 37.2 us
  local copies, waits for them, and re-layouts: 2.86 us -> 6.57 us
  waiting for transfers between devices: 30.4 us -> 28.6 us
    ppermute x4, waiting for transfers between devices: 17.9 us -> 4.95 us  [shifted(): lax.ppermute(value, axis, [(source, source + steps) for source in range(f...]
    ppermute x8 -> x6, waiting for transfers between devices: 11.1 us -> 22.2 us  [xor_move(): lax.ppermute(value, axis, [(at, at ^ step) for at in range(lax.axis_size(...]
    ppermute x0 -> x4, starting transfers between devices: none -> 9.96 us  [the longest x1 4.91 us: local(): befores.append(lax.ppermute(packs[c], 'ctx', pair))]
    pallas_call x2, Pallas kernels: 52.5 us -> 46.8 us  [attend(): pl.pallas_call(functools.partial(attend_body, steps, units, base), grid_s...]
    pallas_call x1 -> x2, Pallas kernels: 10 us -> 14.6 us  [the longest x1 12.5 us: open_call(): pl.pallas_call(functools.partial(open_body, each), grid_spec=pltpu.Prefet...]
    select_n x2 -> x0, other arithmetic: 3.8 us -> none  [local(): near = xor_move(jnp.where(second, far, own), 'ctx', 1)]
    unnamed x22 -> x28, local copies, waits for them, and re-layouts: 2.86 us -> 6.57 us
    convert_element_type x2 -> x0, other arithmetic: 2.27 us -> none  [the longest x1 1.57 us: local(): down = (adapter_down_maps.T.astype(jnp.float32) * gain).astype(jnp.bfloat16)]
  transfers between devices with their start and end apart: 15 -> 17, of which waited for: 8 -> 9; matrix products, arithmetic and copies ran while one was open for 3% -> 0% of each run, Pallas kernels for 25% -> 32%
where the time goes in v1:
time: 148 us; the launch traced here: 147 us
  Pallas kernels  74.2 us (50%)
  starting transfers between devices  37.2 us (25%)
  waiting for transfers between devices  28.6 us (19%)
  local copies, waits for them, and re-layouts  6.57 us (4%)
    pallas_call x2, Pallas kernels, attend(): pl.pallas_call(functools.partial(attend_body, steps, units, base), grid_s...  46.8 us
    ppermute x6, waiting for transfers between devices, xor_move(): lax.ppermute(value, axis, [(at, at ^ step) for at in range(lax.axis_size(...  22.2 us
    ppermute x4, starting transfers between devices, shifted(): lax.ppermute(value, axis, [(source, source + steps) for source in range(f...  13.1 us
    pallas_call x1, Pallas kernels, open_call(): pl.pallas_call(functools.partial(open_body, each), grid_spec=pltpu.Prefet...  12.5 us
    ppermute x6, starting transfers between devices, xor_move(): lax.ppermute(value, axis, [(at, at ^ step) for at in range(lax.axis_size(...  10.1 us
    pallas_call x1, Pallas kernels, project(): pl.pallas_call(project_body, grid_spec=pltpu.PrefetchScalarGridSpec(num_s...  7.37 us
    unnamed x28, local copies, waits for them, and re-layouts  6.57 us
    ppermute x4, waiting for transfers between devices, shifted(): lax.ppermute(value, axis, [(source, source + steps) for source in range(f...  4.95 us
  transfers between devices with their start and end apart: 17, of which 9 were waited for; matrix products, arithmetic and copies ran while one was open for 0% of the time, Pallas kernels for 32%

profile of v1, /device:TPU:0, one launch (start us, length us, event | category | flops | bytes accessed | tf_op | source)
XLA Modules:
  0.0 147.4 jit_solution(12176117180609513756)
XLA Ops:
  0.6 2.1 %shard_map.116.k2.v2 = bf16[512,1024]{1,0:T(8,128)(2,1)} custom-call(bf16[512,1024]{1,0:T(8,128)(2,1)} %k_ref.1, bf16[512,1024]{1,0:T(8,128)(2,1)} %v_ref.1), custom_call_target="tpu_custom_call" | custom-call | tf_op jit(solution)/shard_map/pallas_call | solution.py:101
  2.7 5.9 %collective-permute-start.8 = (bf16[512,1024]{1,0:T(8,128)(2,1)}, bf16[512,1024]{1,0:T(8,128)(2,1)}, u32[]{:S(2)}, u32[]{:S(2)}) collective-permute-start(bf16[512,1024]{1,0:T(8,128)(2,1)} %shard_map.116.k2.v2), channel_id=1, source_target_pairs={{0,4},{2,6},{4,8},{6,10},{8,12},{10,14},{12,16},{14,18},{16,20},{1... | collective-permute-start | bytes 3145736 | tf_op jit(solution)/shard_map/ppermute | solution.py:36
  8.6 12.5 %shard_map.113 = (bf16[512,1024]{1,0:T(8,128)(2,1)}, f32[32,512]{1,0:T(8,128)}, bf16[512,1024]{1,0:T(8,128)(2,1)}) custom-call(s32[1]{0:T(128)} %bitcast.3.offset_ref, bf16[512,2688]{1,0:T(8,128)(2,1)} %pg_ref.3, bf16[4096,2688]{1,0:T(8,128)(2,1)} %w_ref.3, bf16[512,2688]{1,0:T(8,128)(2,1)} %x_ref.1, bf16[2688]{0:T(1024)(128)(2,1)} %norm_ref.1, ...), custom_call_target="tpu_custom_call" | custom-call | flops 2818572288 | bytes 12058624 | tf_op jit(solution)/shard_map/pallas_call | solution.py:120
  22.6 3.5 %collective-permute-start.1 = (bf16[512,1024]{1,0:T(8,128)(2,1)}, bf16[512,1024]{1,0:T(8,128)(2,1)}, u32[]{:S(2)}, u32[]{:S(2)}) collective-permute-start(bf16[512,1024]{1,0:T(8,128)(2,1)} %get-tuple-element.8.k2.v2), channel_id=1, source_target_pairs={{0,4},{2,6},{4,8},{6,10},{8,12},{10,14},{12,16},{14,18},{16,20},{1... | collective-permute-start | bytes 3145736 | tf_op jit(solution)/shard_map/ppermute | solution.py:36
  26.1 2.3 %collective-permute-start.10 = (bf16[512,1024]{1,0:T(8,128)(2,1)S(1)}, bf16[512,1024]{1,0:T(8,128)(2,1)}, u32[]{:S(2)}, u32[]{:S(2)}) collective-permute-start(bf16[512,1024]{1,0:T(8,128)(2,1)S(1)} %copy-done.1), channel_id=1, source_target_pairs={{0,2},{4,6},{8,10},{12,14},{16,18},{20,22},{24,26},{28,30},{1,3},{... | collective-permute-start | bytes 3145736 | tf_op jit(solution)/shard_map/ppermute | solution.py:424
  28.4 3.1 %collective-permute-done.8.k0.v0 = bf16[512,1024]{1,0:T(8,128)(2,1)} collective-permute-done((bf16[512,1024]{1,0:T(8,128)(2,1)}, bf16[512,1024]{1,0:T(8,128)(2,1)}, u32[]{:S(2)}, u32[]{:S(2)}) %collective-permute-start.8) | collective-permute-done | bytes 1048608 | tf_op jit(solution)/shard_map/ppermute | solution.py:36
  32.7 1.6 %collective-permute-start.4 = (f32[32,512]{1,0:T(8,128)}, f32[32,512]{1,0:T(8,128)S(1)}, u32[]{:S(2)}, u32[]{:S(2)}) collective-permute-start(f32[32,512]{1,0:T(8,128)} %get-tuple-element.9.mine_ref), channel_id=1, source_target_pairs={{0,1},{1,0},{2,3},{3,2},{4,5},{5,4},{6,7},{7,6},{8,9},{9,8},{10,11... | collective-permute-start | bytes 196616 | tf_op jit(solution)/shard_map/ppermute | solution.py:40
  34.3 13.0 %collective-permute-done.4.theirs_ref = f32[32,512]{1,0:T(8,128)S(1)} collective-permute-done((f32[32,512]{1,0:T(8,128)}, f32[32,512]{1,0:T(8,128)S(1)}, u32[]{:S(2)}, u32[]{:S(2)}) %collective-permute-start.4) | collective-permute-done | bytes 65568 | tf_op jit(solution)/shard_map/ppermute | solution.py:40
  49.4 2.5 %collective-permute-start.5 = (bf16[32,512]{1,0:T(8,128)(2,1)}, bf16[32,512]{1,0:T(8,128)(2,1)S(1)}, u32[]{:S(2)}, u32[]{:S(2)}) collective-permute-start(bf16[32,512]{1,0:T(8,128)(2,1)} %shard_map.114.t0_ref.lq_ref), channel_id=1, source_target_pairs={{0,4},{2,6},{4,8},{6,10},{8,12},{10,14},{12,16},{14,18},{16,20},{1... | collective-permute-start | bytes 98312 | tf_op jit(solution)/shard_map/ppermute | solution.py:36
  51.9 1.9 %collective-permute-done.5.t2_ref = bf16[32,512]{1,0:T(8,128)(2,1)S(1)} collective-permute-done((bf16[32,512]{1,0:T(8,128)(2,1)}, bf16[32,512]{1,0:T(8,128)(2,1)S(1)}, u32[]{:S(2)}, u32[]{:S(2)}) %collective-permute-start.5) | collective-permute-done | bytes 32800 | tf_op jit(solution)/shard_map/ppermute | solution.py:36
  55.1 7.4 %shard_map.112 = bf16[512,1024]{1,0:T(8,128)(2,1)} custom-call(s32[1]{0:T(128)} %bitcast.2.offset_ref, bf16[512,2688]{1,0:T(8,128)(2,1)} %pg_ref.3, bf16[4096,2688]{1,0:T(8,128)(2,1)} %w_ref.3), custom_call_target="tpu_custom_call" | custom-call | flops 2818572288 | bytes 9306112 | tf_op jit(solution)/shard_map/pallas_call | solution.py:49
  62.5 4.9 %collective-permute-start.3 = (bf16[512,1024]{1,0:T(8,128)(2,1)}, bf16[512,1024]{1,0:T(8,128)(2,1)S(1)}, u32[]{:S(2)}, u32[]{:S(2)}) collective-permute-start(bf16[512,1024]{1,0:T(8,128)(2,1)} %get-tuple-element.8.k2.v2), channel_id=1, source_target_pairs={{0,2},{4,6},{8,10},{12,14},{16,18},{20,22},{24,26},{28,30},{1,3},{... | collective-permute-start | bytes 3145736 | tf_op jit(solution)/shard_map/ppermute | solution.py:487
  67.4 2.2 %shard_map.115 = (bf16[1536,128]{1,0:T(8,128)(2,1)}, s32[512,128]{1,0:T(8,128)}) custom-call(s32[1]{0:T(128)} %bitcast.5.first_ref, bf16[32,512]{1,0:T(8,128)(2,1)} %copy-done.12, bf16[32,512]{1,0:T(8,128)(2,1)} %copy-done.13, bf16[32,512]{1,0:T(8,128)(2,1)} %shard_map.114.t0_ref.lq_ref), custom_call_target="tpu_custom_call" | custom-call | tf_op jit(solution)/shard_map/pallas_call | solution.py:479
  69.6 1.5 %collective-permute-start = (bf16[512,1024]{1,0:T(8,128)(2,1)}, bf16[512,1024]{1,0:T(8,128)(2,1)S(1)}, u32[]{:S(2)}, u32[]{:S(2)}) collective-permute-start(bf16[512,1024]{1,0:T(8,128)(2,1)} %shard_map.112), channel_id=1, source_target_pairs={{0,1},{1,0},{2,3},{3,2},{4,5},{5,4},{6,7},{7,6},{8,9},{9,8},{10,11... | collective-permute-start | bytes 3145736 | tf_op jit(solution)/shard_map/ppermute | solution.py:447
  72.6 1.8 %copy-done = bf16[512,2688]{1,0:T(8,128)(2,1)S(1)} copy-done((bf16[512,2688]{1,0:T(8,128)(2,1)S(1)}, bf16[512,2688]{1,0:T(8,128)(2,1)}, u32[]{:S(2)}) %copy-start) | copy-done | bytes 2752536
  74.4 1.6 %copy-done.3 = bf16[512,2048]{1,0:T(8,128)(2,1)S(1)} copy-done((bf16[512,2048]{1,0:T(8,128)(2,1)S(1)}, bf16[512,2048]{1,0:T(8,128)(2,1)}, u32[]{:S(2)}) %copy-start.3) | copy-done | bytes 2097176
  78.0 23.5 %shard_map.117.rest_0_ = bf16[8,2048]{1,0:T(8,128)(2,1)S(1)} custom-call(s32[1]{0:T(128)} %bitcast.7.offset_ref, s32[1]{0:T(128)} %bitcast.1.second_ref, bf16[512,2048]{1,0:T(8,128)(2,1)S(1)} %copy-done.3, bf16[512,2688]{1,0:T(8,128)(2,1)S(1)} %copy-done, bf16[4096,2688]{1,0:T(8,128)(2,1)} %w_ref.3, bf16[512,1024]{1,0:T(8,128)(2,1)} %collective-permute-done.7.recv_ref, ...), custom_call_target="tpu_custom_call" | custom-call | flops 13555990528 | bytes 10747904 | tf_op jit(solution)/shard_map/pallas_call | solution.py:353
  101.6 23.2 %shard_map.118 = bf16[8,4096]{1,0:T(8,128)(2,1)S(1)} custom-call(s32[1]{0:T(128)} %bitcast.offset_ref, s32[1]{0:T(128)} %bitcast.1.second_ref, bf16[512,2048]{1,0:T(8,128)(2,1)S(1)} %copy-done.3, bf16[512,2688]{1,0:T(8,128)(2,1)S(1)} %copy-done, bf16[4096,2688]{1,0:T(8,128)(2,1)} %w_ref.3, bf16[512,1024]{1,0:T(8,128)(2,1)S(1)} %collective-permute-done.recv_ref, ...), custom_call_target="tpu_custom_call" | custom-call | flops 13555990528 | bytes 10747904 | tf_op jit(solution)/shard_map/pallas_call | solution.py:353
  127.0 1.6 %collective-permute-start.12 = (bf16[8,4096]{1,0:T(8,128)(2,1)S(1)}, bf16[8,4096]{1,0:T(8,128)(2,1)S(1)}, u32[]{:S(2)}, u32[]{:S(2)}) collective-permute-start(bf16[8,4096]{1,0:T(8,128)(2,1)S(1)} %add_convert_fusion.2), channel_id=1, source_target_pairs={{0,8},{2,10},{4,12},{6,14},{8,0},{10,2},{12,4},{14,6},{16,24},{18,... | collective-permute-start | bytes 196616 | tf_op jit(solution)/shard_map/ppermute | solution.py:40
  128.6 2.8 %collective-permute-done.12 = bf16[8,4096]{1,0:T(8,128)(2,1)S(1)} collective-permute-done((bf16[8,4096]{1,0:T(8,128)(2,1)S(1)}, bf16[8,4096]{1,0:T(8,128)(2,1)S(1)}, u32[]{:S(2)}, u32[]{:S(2)}) %collective-permute-start.12) | collective-permute-done | bytes 65568 | tf_op jit(solution)/shard_map/ppermute | solution.py:40
  131.4 2.6 %collective-permute-start.13 = (bf16[8,4096]{1,0:T(8,128)(2,1)S(1)}, bf16[8,4096]{1,0:T(8,128)(2,1)S(1)}, u32[]{:S(2)}, u32[]{:S(2)}) collective-permute-start(bf16[8,4096]{1,0:T(8,128)(2,1)S(1)} %add_convert_fusion.1), channel_id=1, source_target_pairs={{0,16},{2,18},{4,20},{6,22},{8,24},{10,26},{12,28},{14,30},{16,0},... | collective-permute-start | bytes 196616 | tf_op jit(solution)/shard_map/ppermute | solution.py:40
  134.0 2.8 %collective-permute-done.13 = bf16[8,4096]{1,0:T(8,128)(2,1)S(1)} collective-permute-done((bf16[8,4096]{1,0:T(8,128)(2,1)S(1)}, bf16[8,4096]{1,0:T(8,128)(2,1)S(1)}, u32[]{:S(2)}, u32[]{:S(2)}) %collective-permute-start.13) | collective-permute-done | bytes 65568 | tf_op jit(solution)/shard_map/ppermute | solution.py:40
  136.9 2.5 %collective-permute-start.14 = (bf16[8,4096]{1,0:T(8,128)(2,1)S(1)}, bf16[8,4096]{1,0:T(8,128)(2,1)S(1)}, u32[]{:S(2)}, u32[]{:S(2)}) collective-permute-start(bf16[8,4096]{1,0:T(8,128)(2,1)S(1)} %add_convert_fusion.refs_0_), channel_id=1, source_target_pairs={{0,4},{2,6},{4,0},{6,2},{8,12},{10,14},{12,8},{14,10},{16,20},{18,... | collective-permute-start | bytes 196616 | tf_op jit(solution)/shard_map/ppermute | solution.py:40
  145.7 1.8 %shard_map.119 = (f32[8,2048]{1,0:T(8,128)}, f32[8,1024]{1,0:T(8,128)}, f32[8,1024]{1,0:T(8,128)}) custom-call(bf16[8,4096]{1,0:T(8,128)(2,1)} %copy-done.7, bf16[8,4096]{1,0:T(8,128)(2,1)} %copy-done.8, bf16[8,4096]{1,0:T(8,128)(2,1)} %copy-done.9, bf16[8,4096]{1,0:T(8,128)(2,1)} %copy-done.10), custom_call_target="tpu_custom_call" | custom-call | tf_op jit(solution)/shard_map/pallas_call | solution.py:522
  (49 shorter events, 18.2 us)
Async XLA Ops:
  2.7 28.7 %collective-permute-start.8 = (bf16[512,1024]{1,0:T(8,128)(2,1)}, bf16[512,1024]{1,0:T(8,128)(2,1)}, u32[]{:S(2)}, u32[]{:S(2)}) collective-permute-start(bf16[512,1024]{1,0:T(8,128)(2,1)} %shard_map.116.k2.v2), channel_id=1, source_target_pairs={{0,4},{2,6},{4,8},{6,10},{8,12},{10,14},{12,16},{14,18},{16,20},{1... | collective-permute-start | bytes 3145736 | tf_op jit(solution)/shard_map/ppermute | solution.py:36
  8.6 17.5 %copy-start.1 = (bf16[512,1024]{1,0:T(8,128)(2,1)S(1)}, bf16[512,1024]{1,0:T(8,128)(2,1)}, u32[]{:S(2)}) copy-start(bf16[512,1024]{1,0:T(8,128)(2,1)} %shard_map.116.k2.v2) | copy-start | bytes 3145732
  21.1 48.5 %collective-permute-start.7 = (bf16[512,1024]{1,0:T(8,128)(2,1)}, bf16[512,1024]{1,0:T(8,128)(2,1)}, u32[]{:S(2)}, u32[]{:S(2)}) collective-permute-start(bf16[512,1024]{1,0:T(8,128)(2,1)} %get-tuple-element.12), channel_id=1, source_target_pairs={{0,1},{1,0},{2,3},{3,2},{4,5},{5,4},{6,7},{7,6},{8,9},{9,8},{10,11... | collective-permute-start | bytes 3145736 | tf_op jit(solution)/shard_map/ppermute | solution.py:447
  22.6 48.5 %collective-permute-start.1 = (bf16[512,1024]{1,0:T(8,128)(2,1)}, bf16[512,1024]{1,0:T(8,128)(2,1)}, u32[]{:S(2)}, u32[]{:S(2)}) collective-permute-start(bf16[512,1024]{1,0:T(8,128)(2,1)} %get-tuple-element.8.k2.v2), channel_id=1, source_target_pairs={{0,4},{2,6},{4,8},{6,10},{8,12},{10,14},{12,16},{14,18},{16,20},{1... | collective-permute-start | bytes 3145736 | tf_op jit(solution)/shard_map/ppermute | solution.py:36
  26.1 46.5 %collective-permute-start.10 = (bf16[512,1024]{1,0:T(8,128)(2,1)S(1)}, bf16[512,1024]{1,0:T(8,128)(2,1)}, u32[]{:S(2)}, u32[]{:S(2)}) collective-permute-start(bf16[512,1024]{1,0:T(8,128)(2,1)S(1)} %copy-done.1), channel_id=1, source_target_pairs={{0,2},{4,6},{8,10},{12,14},{16,18},{20,22},{24,26},{28,30},{1,3},{... | collective-permute-start | bytes 3145736 | tf_op jit(solution)/shard_map/ppermute | solution.py:424
  31.4 41.2 %collective-permute-start.9 = (bf16[512,1024]{1,0:T(8,128)(2,1)}, bf16[512,1024]{1,0:T(8,128)(2,1)}, u32[]{:S(2)}, u32[]{:S(2)}) collective-permute-start(bf16[512,1024]{1,0:T(8,128)(2,1)} %collective-permute-done.8.k0.v0), channel_id=1, source_target_pairs={{2,0},{6,4},{10,8},{14,12},{18,16},{22,20},{26,24},{30,28},{3,1},{... | collective-permute-start | bytes 3145736 | tf_op jit(solution)/shard_map/ppermute | solution.py:488
  32.7 14.6 %collective-permute-start.4 = (f32[32,512]{1,0:T(8,128)}, f32[32,512]{1,0:T(8,128)S(1)}, u32[]{:S(2)}, u32[]{:S(2)}) collective-permute-start(f32[32,512]{1,0:T(8,128)} %get-tuple-element.9.mine_ref), channel_id=1, source_target_pairs={{0,1},{1,0},{2,3},{3,2},{4,5},{5,4},{6,7},{7,6},{8,9},{9,8},{10,11... | collective-permute-start | bytes 196616 | tf_op jit(solution)/shard_map/ppermute | solution.py:40
  49.4 4.4 %collective-permute-start.5 = (bf16[32,512]{1,0:T(8,128)(2,1)}, bf16[32,512]{1,0:T(8,128)(2,1)S(1)}, u32[]{:S(2)}, u32[]{:S(2)}) collective-permute-start(bf16[32,512]{1,0:T(8,128)(2,1)} %shard_map.114.t0_ref.lq_ref), channel_id=1, source_target_pairs={{0,4},{2,6},{4,8},{6,10},{8,12},{10,14},{12,16},{14,18},{16,20},{1... | collective-permute-start | bytes 98312 | tf_op jit(solution)/shard_map/ppermute | solution.py:36
  53.8 8.7 %copy-start.12 = (bf16[32,512]{1,0:T(8,128)(2,1)}, bf16[32,512]{1,0:T(8,128)(2,1)S(1)}, u32[]{:S(2)}) copy-start(bf16[32,512]{1,0:T(8,128)(2,1)S(1)} %collective-permute-done.5.t2_ref) | copy-start | bytes 98308
  53.8 8.7 %collective-permute-start.6 = (bf16[32,512]{1,0:T(8,128)(2,1)}, bf16[32,512]{1,0:T(8,128)(2,1)S(1)}, u32[]{:S(2)}, u32[]{:S(2)}) collective-permute-start(bf16[32,512]{1,0:T(8,128)(2,1)} %shard_map.114.t0_ref.lq_ref), channel_id=1, source_target_pairs={{0,2},{2,4},{4,6},{6,8},{8,10},{10,12},{12,14},{14,16},{16,18},{18... | collective-permute-start | bytes 98312 | tf_op jit(solution)/shard_map/ppermute | solution.py:36
  55.1 17.5 %copy-start.2 = (bf16[32,512]{1,0:T(8,128)(2,1)S(1)}, bf16[32,512]{1,0:T(8,128)(2,1)}, u32[]{:S(2)}) copy-start(bf16[32,512]{1,0:T(8,128)(2,1)} %shard_map.114.t0_ref.lq_ref) | copy-start | bytes 98308
  62.5 4.9 %copy-start.13 = (bf16[32,512]{1,0:T(8,128)(2,1)}, bf16[32,512]{1,0:T(8,128)(2,1)S(1)}, u32[]{:S(2)}) copy-start(bf16[32,512]{1,0:T(8,128)(2,1)S(1)} %collective-permute-done.6.t1_ref) | copy-start | bytes 98308
  62.5 39.0 %collective-permute-start.3 = (bf16[512,1024]{1,0:T(8,128)(2,1)}, bf16[512,1024]{1,0:T(8,128)(2,1)S(1)}, u32[]{:S(2)}, u32[]{:S(2)}) collective-permute-start(bf16[512,1024]{1,0:T(8,128)(2,1)} %get-tuple-element.8.k2.v2), channel_id=1, source_target_pairs={{0,2},{4,6},{8,10},{12,14},{16,18},{20,22},{24,26},{28,30},{1,3},{... | collective-permute-start | bytes 3145736 | tf_op jit(solution)/shard_map/ppermute | solution.py:487
  69.6 31.9 %collective-permute-start = (bf16[512,1024]{1,0:T(8,128)(2,1)}, bf16[512,1024]{1,0:T(8,128)(2,1)S(1)}, u32[]{:S(2)}, u32[]{:S(2)}) collective-permute-start(bf16[512,1024]{1,0:T(8,128)(2,1)} %shard_map.112), channel_id=1, source_target_pairs={{0,1},{1,0},{2,3},{3,2},{4,5},{5,4},{6,7},{7,6},{8,9},{9,8},{10,11... | collective-permute-start | bytes 3145736 | tf_op jit(solution)/shard_map/ppermute | solution.py:447
  71.1 30.4 %collective-permute-start.2 = (bf16[512,1024]{1,0:T(8,128)(2,1)}, bf16[512,1024]{1,0:T(8,128)(2,1)S(1)}, u32[]{:S(2)}, u32[]{:S(2)}) collective-permute-start(bf16[512,1024]{1,0:T(8,128)(2,1)} %collective-permute-done.1.k0.v0), channel_id=1, source_target_pairs={{2,0},{6,4},{10,8},{14,12},{18,16},{22,20},{26,24},{30,28},{3,1},{... | collective-permute-start | bytes 3145736 | tf_op jit(solution)/shard_map/ppermute | solution.py:488
  78.0 23.6 %copy-start.4 = (bf16[512,1024]{1,0:T(8,128)(2,1)S(1)}, bf16[512,1024]{1,0:T(8,128)(2,1)}, u32[]{:S(2)}) copy-start(bf16[512,1024]{1,0:T(8,128)(2,1)} %get-tuple-element.8.k2.v2) | copy-start | bytes 3145732
  124.8 2.2 %collective-permute-start.11 = (bf16[8,4096]{1,0:T(8,128)(2,1)S(1)}, bf16[8,4096]{1,0:T(8,128)(2,1)S(1)}, u32[]{:S(2)}, u32[]{:S(2)}) collective-permute-start(bf16[8,4096]{1,0:T(8,128)(2,1)S(1)} %shard_map.118), channel_id=1, source_target_pairs={{0,2},{2,0},{4,6},{6,4},{8,10},{10,8},{12,14},{14,12},{16,18},{18,... | collective-permute-start | bytes 196616 | tf_op jit(solution)/shard_map/ppermute | solution.py:40
  127.0 4.4 %collective-permute-start.12 = (bf16[8,4096]{1,0:T(8,128)(2,1)S(1)}, bf16[8,4096]{1,0:T(8,128)(2,1)S(1)}, u32[]{:S(2)}, u32[]{:S(2)}) collective-permute-start(bf16[8,4096]{1,0:T(8,128)(2,1)S(1)} %add_convert_fusion.2), channel_id=1, source_target_pairs={{0,8},{2,10},{4,12},{6,14},{8,0},{10,2},{12,4},{14,6},{16,24},{18,... | collective-permute-start | bytes 196616 | tf_op jit(solution)/shard_map/ppermute | solution.py:40
  131.4 5.5 %collective-permute-start.13 = (bf16[8,4096]{1,0:T(8,128)(2,1)S(1)}, bf16[8,4096]{1,0:T(8,128)(2,1)S(1)}, u32[]{:S(2)}, u32[]{:S(2)}) collective-permute-start(bf16[8,4096]{1,0:T(8,128)(2,1)S(1)} %add_convert_fusion.1), channel_id=1, source_target_pairs={{0,16},{2,18},{4,20},{6,22},{8,24},{10,26},{12,28},{14,30},{16,0},... | collective-permute-start | bytes 196616 | tf_op jit(solution)/shard_map/ppermute | solution.py:40
  136.9 8.1 %copy-start.7 = (bf16[8,4096]{1,0:T(8,128)(2,1)}, bf16[8,4096]{1,0:T(8,128)(2,1)S(1)}, u32[]{:S(2)}) copy-start(bf16[8,4096]{1,0:T(8,128)(2,1)S(1)} %add_convert_fusion.refs_0_) | copy-start | bytes 196612
  136.9 5.3 %collective-permute-start.14 = (bf16[8,4096]{1,0:T(8,128)(2,1)S(1)}, bf16[8,4096]{1,0:T(8,128)(2,1)S(1)}, u32[]{:S(2)}, u32[]{:S(2)}) collective-permute-start(bf16[8,4096]{1,0:T(8,128)(2,1)S(1)} %add_convert_fusion.refs_0_), channel_id=1, source_target_pairs={{0,4},{2,6},{4,0},{6,2},{8,12},{10,14},{12,8},{14,10},{16,20},{18,... | collective-permute-start | bytes 196616 | tf_op jit(solution)/shard_map/ppermute | solution.py:40
  139.4 4.3 %collective-permute-start.15 = (bf16[8,4096]{1,0:T(8,128)(2,1)S(1)}, bf16[8,4096]{1,0:T(8,128)(2,1)S(1)}, u32[]{:S(2)}, u32[]{:S(2)}) collective-permute-start(bf16[8,4096]{1,0:T(8,128)(2,1)S(1)} %add_convert_fusion.refs_0_), channel_id=1, source_target_pairs={{0,1},{1,0},{2,3},{3,2},{4,5},{5,4},{6,7},{7,6},{8,9},{9,8},{10,11... | collective-permute-start | bytes 196616 | tf_op jit(solution)/shard_map/ppermute | solution.py:40
  139.9 5.2 %collective-permute-start.16 = (bf16[8,4096]{1,0:T(8,128)(2,1)S(1)}, bf16[8,4096]{1,0:T(8,128)(2,1)S(1)}, u32[]{:S(2)}, u32[]{:S(2)}) collective-permute-start(bf16[8,4096]{1,0:T(8,128)(2,1)S(1)} %add_convert_fusion.refs_0_), channel_id=1, source_target_pairs={{0,5},{1,4},{2,7},{3,6},{4,1},{5,0},{6,3},{7,2},{8,13},{9,12},{10,... | collective-permute-start | bytes 196616 | tf_op jit(solution)/shard_map/ppermute | solution.py:513
  142.2 2.8 %copy-start.8 = (bf16[8,4096]{1,0:T(8,128)(2,1)}, bf16[8,4096]{1,0:T(8,128)(2,1)S(1)}, u32[]{:S(2)}) copy-start(bf16[8,4096]{1,0:T(8,128)(2,1)S(1)} %collective-permute-done.14.refs_1_) | copy-start | bytes 196612
  (7 other events, 8.0 us)

commit v2 on v0

--- a/solution.py
+++ b/solution.py
@@ -18,6 +18,7 @@
 SCALE = float(MODEL_WIDTH // QUERY_HEADS) ** (-0.5)
 LANES = 128
 GRANT = 62 << 20
+SMALL = pltpu.CompilerParams(vmem_limit_bytes=8 << 20)
 ROW_K, ROW_V, ROW_ONE, ROW_DOC = 0, ADAPTER_RANK, 2 * ADAPTER_RANK, 2 * ADAPTER_RANK + 1
 TABLE = 4 * ADAPTER_RANK
 
@@ -67,15 +68,16 @@
     )(first_block, gradient, weight)
 
 
-def open_body(chunks, offset_ref, gradient_ref, weight_ref, x_ref, down_ref, k_ref, v_ref, out_ref, low_ref, *packs):
+def open_body(each, offset_ref, gradient_ref, weight_ref, x_ref, norm_ref, down_ref, *rest):
+    k_ref, v_ref, out_ref, low_ref, *packs = rest
     step = pl.program_id(0)
     out_ref[...] = dotf(gradient_ref[...], weight_ref[...], NT).astype(out_ref.dtype)
-    low_ref[0 : 3 * ADAPTER_RANK, :] = dotf(down_ref[...], x_ref[...], NT)
     hidden = x_ref[...].astype(jnp.float32)
+    weighted = (hidden * norm_ref[...].astype(jnp.float32)).astype(jnp.bfloat16)
+    low_ref[0 : 3 * ADAPTER_RANK, :] = dotf(down_ref[...], weighted, NT)
     ones = jnp.ones((ADAPTER_RANK, hidden.shape[1]), jnp.bfloat16)
     low_ref[3 * ADAPTER_RANK :, :] = dotf(ones, (hidden * hidden).astype(jnp.bfloat16), NT)
     wide = k_ref.shape[1]
-    each = pl.num_programs(0) // chunks
     for c, pack_ref in enumerate(packs):
 
         @pl.when(step // each == c)
@@ -84,18 +86,35 @@
             pack_ref[:, wide:] = v_ref[...]
 
 
-def open_call(gradient, weight, first_block, blocks, width, x, down, keys, values, chunks):
+def pack_body(k_ref, v_ref, out_ref):
+    wide = k_ref.shape[1]
+    out_ref[:, :wide] = k_ref[...]
+    out_ref[:, wide:] = v_ref[...]
+
+
+def pack_call(keys, values, wide, blocks):
+    rows = keys.shape[0]
+    return pl.pallas_call(
+        pack_body,
+        grid=(blocks,),
+        in_specs=[pl.BlockSpec((rows, wide), lambda i: (0, i))] * 2,
+        out_specs=pl.BlockSpec((rows, 2 * wide), lambda i: (0, i)),
+        out_shape=jax.ShapeDtypeStruct((rows, 2 * wide * blocks), keys.dtype),
+        compiler_params=pltpu.CompilerParams(vmem_limit_bytes=GRANT),
+    )(keys, values)
+
+
+def open_call(gradient, weight, first_block, blocks, width, x, norm, down, keys, values, chunks):
     rows, depth = gradient.shape
     slab = rows // blocks
     wide = keys.shape[1] // blocks
     each = blocks // chunks
-    pack_specs = [
-        pl.BlockSpec((rows, 2 * wide), lambda i, off, c=c: (0, jnp.clip(i - c * each, 0, each - 1)))
-        for c in range(chunks)
-    ]
+    skip = each
+    extra = chunks - 1
+    pack_specs = [pl.BlockSpec((rows, 2 * wide), lambda i, off: (0, jnp.minimum(i, each - 1)))] * extra
     pack_shape = jax.ShapeDtypeStruct((rows, 2 * wide * each), keys.dtype)
     return pl.pallas_call(
-        functools.partial(open_body, chunks),
+        functools.partial(open_body, each),
         grid_spec=pltpu.PrefetchScalarGridSpec(
             num_scalar_prefetch=1,
             grid=(blocks,),
@@ -103,9 +122,10 @@
                 pl.BlockSpec((rows, depth), lambda i, off: (0, 0)),
                 pl.BlockSpec((width, depth), lambda i, off: (off[0] + i, 0)),
                 pl.BlockSpec((slab, depth), lambda i, off: (i, 0)),
+                pl.BlockSpec((1, depth), lambda i, off: (0, 0)),
                 pl.BlockSpec((3 * ADAPTER_RANK, depth), lambda i, off: (0, 0)),
-                pl.BlockSpec((rows, wide), lambda i, off: (0, i)),
-                pl.BlockSpec((rows, wide), lambda i, off: (0, i)),
+                pl.BlockSpec((rows, wide), lambda i, off: (0, jnp.minimum(i + skip, blocks - 1))),
+                pl.BlockSpec((rows, wide), lambda i, off: (0, jnp.minimum(i + skip, blocks - 1))),
             ],
             out_specs=[
                 pl.BlockSpec((rows, width), lambda i, off: (0, i)),
@@ -117,14 +137,14 @@
             jax.ShapeDtypeStruct((rows, blocks * width), jnp.bfloat16),
             jax.ShapeDtypeStruct((TABLE, rows), jnp.float32),
         ]
-        + [pack_shape] * chunks,
+        + [pack_shape] * extra,
         cost_estimate=pl.CostEstimate(
             flops=2 * rows * depth * width * blocks,
             bytes_accessed=2 * (2 * rows * depth + width * blocks * depth + rows * width * blocks),
             transcendentals=0,
         ),
         compiler_params=pltpu.CompilerParams(vmem_limit_bytes=GRANT),
-    )(first_block, gradient, weight, x, down, keys, values)
+    )(first_block, gradient, weight, x, norm, down, keys, values)
 
 
 def table_body(mine_ref, theirs_ref, doc_ref, out_ref):
@@ -156,13 +176,14 @@
 
 
 def attend_body(
-    steps, step_units, base, offset_ref, q_ref, pg_ref, w_ref, recv_ref, k0, k1, k2, v0, v1, v2, ext_ref, lq_ref, st_ref, *rest
+    steps, step_units, base, offset_ref, q_ref, pg_hbm, w_hbm, recv_ref, k0, k1, k2, v0, v1, v2, ext_ref, lq_ref, st_ref, *rest
 ):
     if base:
-        before_ref, out_ref, s_scr, e_scr, ve, ke, do_scr = rest
+        before_ref, out_ref, *scratch = rest
     else:
-        out_ref, s_scr, e_scr, ve, ke, do_scr = rest
-    rows = pg_ref.shape[0]
+        out_ref, *scratch = rest
+    s_scr, e_scr, ve, ke, do_scr, pg_scr, w_scr, sems = scratch
+    rows = pg_scr.shape[0]
     tile = s_scr.shape[1] // 2
     keys = s_scr.shape[2]
     width = tile
@@ -172,6 +193,21 @@
     state = [{} for _ in units]
     columns = range(keys // width)
     step = pl.program_id(0)
+    deep = 2 * LANES
+
+    def gradient_copy():
+        return pltpu.make_async_copy(pg_hbm, pg_scr, sems.at[0])
+
+    def weight_copy(group):
+        first = pl.multiple_of((offset_ref[0] * step_units + group) * deep, deep)
+        return pltpu.make_async_copy(w_hbm.at[pl.ds(first, deep), :], w_scr.at[group], sems.at[1 + group])
+
+    @pl.when(step == 0)
+    def _():
+        gradient_copy().start()
+        for group in range(steps * step_units):
+            weight_copy(group).start()
+
     if base:
 
         @pl.when(step == 0)
@@ -181,9 +217,6 @@
     def prepare(i):
         g, t = units[i]
         if t == 0:
-            own = dotf(pg_ref[...], w_ref[2 * LANES * g : 2 * LANES * (g + 1), :], NT)
-            got = recv_ref[:, 2 * LANES * g : 2 * LANES * (g + 1)].astype(jnp.float32)
-            do_scr[g % 2] = (own + got).astype(jnp.bfloat16)
             for b, (k_ref, v_ref) in enumerate(((k0, v0), (k1, v1), (k2, v2))):
                 span = slice(b * rows, (b + 1) * rows)
                 ke[g % 2, span, :LANES] = k_ref[:, g * LANES : (g + 1) * LANES]
@@ -200,6 +233,13 @@
         s["start"] = jnp.concatenate([start, start], 0)
         s["peak"] = None
 
+    def cotangent(i):
+        g, t = units[i]
+        if t == 0:
+            own = dotf(pg_scr[...], w_scr[step * step_units + g], NT)
+            got = recv_ref[:, deep * g : deep * (g + 1)].astype(jnp.float32)
+            do_scr[g % 2] = (own + got).astype(jnp.bfloat16)
+
     def score(i, j):
         g, t = units[i]
         s = state[i]
@@ -273,11 +313,20 @@
     prepare(0)
     for j in columns:
         score(0, j)
+
+    @pl.when(step == 0)
+    def _():
+        gradient_copy().wait()
+
+    for g in range(step_units):
+        weight_copy(step * step_units + g).wait()
+    cotangent(0)
     for i in range(len(units) + 1):
         if i < len(units):
             state[i]["top"] = jnp.max(state[i]["peak"], axis=1, keepdims=True)
         if i + 1 < len(units):
             prepare(i + 1)
+            cotangent(i + 1)
         for j in columns:
             if i < len(units):
                 weigh(i, j)
@@ -304,8 +353,8 @@
     in_specs = (
         [
             col(2 * wide, lambda g, off: (0, g + skip)),
-            col(depth, lambda g, off: (0, 0)),
-            pl.BlockSpec((2 * wide, depth), lambda g, off: (g + off[0], 0)),
+            pl.BlockSpec(memory_space=pl.ANY),
+            pl.BlockSpec(memory_space=pl.ANY),
             col(2 * wide, lambda g, off: (0, g)),
         ]
         + [col(wide, lambda g, off: (0, 2 * g))] * 3
@@ -333,6 +382,9 @@
                 pltpu.VMEM((2, 3 * rows, 2 * LANES), jnp.bfloat16),
                 pltpu.VMEM((2, 3 * rows, 2 * LANES), jnp.bfloat16),
                 pltpu.VMEM((2, rows, 2 * LANES), jnp.bfloat16),
+                pltpu.VMEM((rows, depth), jnp.bfloat16),
+                pltpu.VMEM((groups, 2 * LANES, depth), jnp.bfloat16),
+                pltpu.SemaphoreType.DMA((1 + groups,)),
             ],
         ),
         out_shape=jax.ShapeDtypeStruct((ADAPTER_RANK, total), jnp.bfloat16),
@@ -348,12 +400,7 @@
 def finish_body(*refs):
     q_ref, k_ref, v_ref = refs[-3:]
     mine = refs[0][...].astype(jnp.float32) + refs[1][...].astype(jnp.float32)
-    total = jnp.sum(mine * mine, keepdims=True)
-    if len(refs) == 7:
-        theirs = refs[2][...].astype(jnp.float32) + refs[3][...].astype(jnp.float32)
-        total = total + jnp.sum(theirs * theirs, keepdims=True)
-    else:
-        total = refs[2][0:1, 0:1]
+    total = refs[2][0:1, 0:1]
     count = float(ADAPTER_RANK * (QUERY_HEADS + 2 * KEY_VALUE_HEADS) * HEAD_SIZE)
     mine = mine * jnp.sqrt(count / (total + 1e-06))
     for g in range(k_ref.shape[1] // LANES):
@@ -386,8 +433,9 @@
     half = heads_width // width
     per = half // chunks
     scalar = lambda value: jnp.asarray(value, jnp.int32).reshape(1)
-    gain = norm_weight.astype(jnp.float32)[None, :]
-    down = (adapter_down_maps.T.astype(jnp.float32) * gain).astype(jnp.bfloat16)
+
+    packs = [pack_call(stored_keys, stored_values, units * LANES, steps)]
+    fars = [shifted(packs[0], "ctx", 2)]
 
     received = []
     for c in range(chunks):
@@ -395,14 +443,15 @@
         for d in range(1, tp):
             first = scalar(((tp_at + d) % tp) * half + c * per)
             if c == 0 and d == 1:
-                part, low, *packs = open_call(
+                part, low, *more = open_call(
                     projection_gradient,
                     output_weight,
                     first,
                     per,
                     width,
                     layer_input,
-                    down,
+                    norm_weight[None, :],
+                    adapter_down_maps.T,
                     stored_keys,
                     stored_values,
                     chunks,
@@ -420,7 +469,9 @@
         low = low + xor_move(low, "tp", move)
         move *= 2
     other = xor_move(low, "tp", move)
-    table = pl.pallas_call(table_body, out_shape=jax.ShapeDtypeStruct((TABLE, rows), jnp.bfloat16))(
+    table = pl.pallas_call(
+        table_body, out_shape=jax.ShapeDtypeStruct((TABLE, rows), jnp.bfloat16), compiler_params=SMALL
+    )(
         low, other, document_index[None, :]
     )
     table2 = shifted(table, "ctx", 2)
@@ -440,22 +491,25 @@
             jax.ShapeDtypeStruct((3 * rows, LANES), jnp.bfloat16),
             jax.ShapeDtypeStruct((rows, LANES), jnp.int32),
         ],
+        compiler_params=SMALL,
     )
     ext, starts = prepare(scalar(2 * rows - ctx_at * rows), table2, table1, table)
 
     second = (ctx_at % 2) == 1
     sums = None
     for c in range(chunks):
-        own = packs[c]
-        far = shifted(own, "ctx", 2)
-        near = xor_move(jnp.where(second, far, own), "ctx", 1)
+        if c > 0:
+            packs.append(more[c - 1])
+            fars.append(shifted(packs[c], "ctx", 2))
+        picked = jnp.where(second, fars[c], packs[c])
+        near = xor_move(picked, "ctx", 1)
         first = scalar((tp_at * half + c * per) // units)
         sums = attend(
             stored_queries,
             projection_gradient,
             output_weight,
             received[c],
-            (far, near, own),
+            (fars[c], near, packs[c]),
             ext,
             table,
             starts,
@@ -470,20 +524,17 @@
     for move in order:
         sums = (sums.astype(jnp.float32) + xor_move(sums, "ctx", move).astype(jnp.float32)).astype(jnp.bfloat16)
     last = [sums, xor_move(sums, "ctx", 2)]
-    if tp == 2:
-        both = [(at, at ^ 5) for at in range(2 * ctx)]
-        last = last + [xor_move(sums, "tp", 1), lax.ppermute(sums, ("ctx", "tp"), both)]
-    else:
-        squared = jnp.sum(jnp.square(last[0].astype(jnp.float32) + last[1].astype(jnp.float32))).reshape(1, 1)
-        move = 1
-        while move < tp:
-            squared = squared + xor_move(squared, "tp", move)
-            move *= 2
-        last.append(squared)
+    squared = jnp.sum(jnp.square(last[0].astype(jnp.float32) + last[1].astype(jnp.float32))).reshape(1, 1)
+    move = 1
+    while move < tp:
+        squared = squared + xor_move(squared, "tp", move)
+        move *= 2
+    last.append(squared)
     sizes = (heads_width, groups * HEAD_SIZE, groups * HEAD_SIZE)
     return pl.pallas_call(
         finish_body,
         out_shape=[jax.ShapeDtypeStruct((ADAPTER_RANK, size), jnp.float32) for size in sizes],
+        compiler_params=SMALL,
     )(*last)
 
 

time: 148 us -> 140 us (0.946)
  starting transfers between devices: 31.6 us -> 27.4 us
  other arithmetic: 6.97 us -> 3.73 us
  Pallas kernels: 75.3 us -> 72.2 us
    ppermute x8, waiting for transfers between devices: 11.1 us -> 23.8 us  [xor_move(): lax.ppermute(value, axis, [(at, at ^ step) for at in range(lax.axis_size(...]
    ppermute x4, waiting for transfers between devices: 17.9 us -> 7.48 us  [shifted(): lax.ppermute(value, axis, [(source, source + steps) for source in range(f...]
    ppermute x1 -> x0, starting transfers between devices: 2.38 us -> none  [local(): lax.ppermute(sums, ('ctx', 'tp'), both)]
    convert_element_type x2 -> x0, other arithmetic: 2.27 us -> none  [the longest x1 1.57 us: local(): down = (adapter_down_maps.T.astype(jnp.float32) * gain).astype(jnp.bfloat16)]
    ppermute x4, starting transfers between devices: 15.1 us -> 13.1 us  [shifted(): lax.ppermute(value, axis, [(source, source + steps) for source in range(f...]
    pallas_call x1 -> x2, Pallas kernels: 10 us -> 11.8 us  [the longest x1 9.72 us: open_call(): pl.pallas_call(functools.partial(open_body, each), grid_spec=pltpu.Prefet...]
    select_n x2, other arithmetic: 3.8 us -> 2.2 us  [local(): picked = jnp.where(second, fars[c], packs[c])]
    pallas_call x1, Pallas kernels: 2.1 us -> 0.54 us  [local(): prepare(scalar(2 * rows - ctx_at * rows), table2, table1, table)]
  transfers between devices with their start and end apart: 15 -> 14, of which waited for: 8 -> 7; matrix products, arithmetic and copies ran while one was open for 3% -> 2% of each run, Pallas kernels for 25% -> 31%
where the time goes in v2:
time: 140 us
  Pallas kernels  72.2 us (52%)
  waiting for transfers between devices  31.3 us (22%)
  starting transfers between devices  27.4 us (20%)
  other arithmetic  3.73 us (3%)
  local copies, waits for them, and re-layouts  3.08 us (2%)
  between operations  2.04 us (1%)
    pallas_call x2, Pallas kernels, attend(): pl.pallas_call(functools.partial(attend_body, steps, units, base), grid_s...  51.6 us
    ppermute x8, waiting for transfers between devices, xor_move(): lax.ppermute(value, axis, [(at, at ^ step) for at in range(lax.axis_size(...  23.8 us
    ppermute x4, starting transfers between devices, shifted(): lax.ppermute(value, axis, [(source, source + steps) for source in range(f...  13.1 us
    ppermute x8, starting transfers between devices, xor_move(): lax.ppermute(value, axis, [(at, at ^ step) for at in range(lax.axis_size(...  11.2 us
    pallas_call x1, Pallas kernels, open_call(): pl.pallas_call(functools.partial(open_body, each), grid_spec=pltpu.Prefet...  9.72 us
    ppermute x4, waiting for transfers between devices, shifted(): lax.ppermute(value, axis, [(source, source + steps) for source in range(f...  7.48 us
    pallas_call x1, Pallas kernels, project(): pl.pallas_call(project_body, grid_spec=pltpu.PrefetchScalarGridSpec(num_s...  7.47 us
    ppermute x2, starting transfers between devices, local(): lax.ppermute(part, 'tp', [(at, (at + d) % tp) for at in range(tp)])  3.11 us
  transfers between devices with their start and end apart: 14, of which 7 were waited for; matrix products, arithmetic and copies ran while one was open for 2% of the time, Pallas kernels for 31%

profile of v2, /device:TPU:0, one launch (start us, length us, event | category | flops | bytes accessed | tf_op | source)
XLA Modules:
  0.0 139.6 jit_solution(10897213919908125876)
XLA Ops:
  0.6 2.1 %shard_map.116.k2.v2 = bf16[512,1024]{1,0:T(8,128)(2,1)} custom-call(bf16[512,1024]{1,0:T(8,128)(2,1)} %k_ref.1, bf16[512,1024]{1,0:T(8,128)(2,1)} %v_ref.1), custom_call_target="tpu_custom_call" | custom-call | tf_op jit(solution)/shard_map/pallas_call | solution.py:97
  2.7 5.9 %collective-permute-start.7 = (bf16[512,1024]{1,0:T(8,128)(2,1)}, bf16[512,1024]{1,0:T(8,128)(2,1)}, u32[]{:S(2)}, u32[]{:S(2)}) collective-permute-start(bf16[512,1024]{1,0:T(8,128)(2,1)} %shard_map.116.k2.v2), channel_id=1, source_target_pairs={{0,4},{2,6},{4,8},{6,10},{8,12},{10,14},{12,16},{14,18},{16,20},{1... | collective-permute-start | bytes 3145736 | tf_op jit(solution)/shard_map/ppermute | solution.py:37
  9.2 9.7 %shard_map.113 = (bf16[512,1024]{1,0:T(8,128)(2,1)}, f32[32,512]{1,0:T(8,128)}, bf16[512,1024]{1,0:T(8,128)(2,1)}) custom-call(s32[1]{0:T(128)} %bitcast.2.offset_ref, bf16[512,2688]{1,0:T(8,128)(2,1)} %pg_hbm.3, bf16[4096,2688]{1,0:T(8,128)(2,1)} %w_hbm.3, bf16[512,2688]{1,0:T(8,128)(2,1)} %x_ref.1, bf16[1,2688]{1,0:T(2,128)(2,1)} %broadcast_in_dim.6.norm_ref, ...), custom_call_target="tpu_custom_call" | custom-call | flops 2818572288 | bytes 12058624 | tf_op jit(solution)/shard_map/pallas_call | solution.py:116
  18.9 1.6 %collective-permute-start.6 = (bf16[512,1024]{1,0:T(8,128)(2,1)}, bf16[512,1024]{1,0:T(8,128)(2,1)}, u32[]{:S(2)}, u32[]{:S(2)}) collective-permute-start(bf16[512,1024]{1,0:T(8,128)(2,1)} %get-tuple-element.12), channel_id=1, source_target_pairs={{0,1},{1,0},{2,3},{3,2},{4,5},{5,4},{6,7},{7,6},{8,9},{9,8},{10,11... | collective-permute-start | bytes 3145736 | tf_op jit(solution)/shard_map/ppermute | solution.py:461
  20.5 3.5 %collective-permute-start.1 = (bf16[512,1024]{1,0:T(8,128)(2,1)}, bf16[512,1024]{1,0:T(8,128)(2,1)}, u32[]{:S(2)}, u32[]{:S(2)}) collective-permute-start(bf16[512,1024]{1,0:T(8,128)(2,1)} %get-tuple-element.8.k2.v2), channel_id=1, source_target_pairs={{0,4},{2,6},{4,8},{6,10},{8,12},{10,14},{12,16},{14,18},{16,20},{1... | collective-permute-start | bytes 3145736 | tf_op jit(solution)/shard_map/ppermute | solution.py:37
  24.0 7.5 %collective-permute-done.7.k0.v0 = bf16[512,1024]{1,0:T(8,128)(2,1)} collective-permute-done((bf16[512,1024]{1,0:T(8,128)(2,1)}, bf16[512,1024]{1,0:T(8,128)(2,1)}, u32[]{:S(2)}, u32[]{:S(2)}) %collective-permute-start.7) | collective-permute-done | bytes 1048608 | tf_op jit(solution)/shard_map/ppermute | solution.py:37
  31.4 1.1 broadcast_select_fusion
  32.5 1.5 %collective-permute-start.3 = (f32[32,512]{1,0:T(8,128)S(1)}, f32[32,512]{1,0:T(8,128)S(1)}, u32[]{:S(2)}, u32[]{:S(2)}) collective-permute-start(f32[32,512]{1,0:T(8,128)S(1)} %copy-done.1), channel_id=1, source_target_pairs={{0,1},{1,0},{2,3},{3,2},{4,5},{5,4},{6,7},{7,6},{8,9},{9,8},{10,11... | collective-permute-start | bytes 196616 | tf_op jit(solution)/shard_map/ppermute | solution.py:41
  34.1 11.2 %collective-permute-done.3.theirs_ref = f32[32,512]{1,0:T(8,128)S(1)} collective-permute-done((f32[32,512]{1,0:T(8,128)S(1)}, f32[32,512]{1,0:T(8,128)S(1)}, u32[]{:S(2)}, u32[]{:S(2)}) %collective-permute-start.3) | collective-permute-done | bytes 65568 | tf_op jit(solution)/shard_map/ppermute | solution.py:41
  45.3 2.5 %collective-permute-start.4 = (bf16[32,512]{1,0:T(8,128)(2,1)S(1)}, bf16[32,512]{1,0:T(8,128)(2,1)S(1)}, u32[]{:S(2)}, u32[]{:S(2)}) collective-permute-start(bf16[32,512]{1,0:T(8,128)(2,1)S(1)} %shard_map.114.t0_ref.lq_ref), channel_id=1, source_target_pairs={{0,4},{2,6},{4,8},{6,10},{8,12},{10,14},{12,16},{14,18},{16,20},{1... | collective-permute-start | bytes 98312 | tf_op jit(solution)/shard_map/ppermute | solution.py:37
  47.8 1.3 collective-permute-start.5
  49.1 7.5 %shard_map.112 = bf16[512,1024]{1,0:T(8,128)(2,1)} custom-call(s32[1]{0:T(128)} %bitcast.1.offset_ref, bf16[512,2688]{1,0:T(8,128)(2,1)} %pg_hbm.3, bf16[4096,2688]{1,0:T(8,128)(2,1)} %w_hbm.3), custom_call_target="tpu_custom_call" | custom-call | flops 2818572288 | bytes 9306112 | tf_op jit(solution)/shard_map/pallas_call | solution.py:50
  56.5 1.5 %collective-permute-start = (bf16[512,1024]{1,0:T(8,128)(2,1)}, bf16[512,1024]{1,0:T(8,128)(2,1)}, u32[]{:S(2)}, u32[]{:S(2)}) collective-permute-start(bf16[512,1024]{1,0:T(8,128)(2,1)} %shard_map.112), channel_id=1, source_target_pairs={{0,1},{1,0},{2,3},{3,2},{4,5},{5,4},{6,7},{7,6},{8,9},{9,8},{10,11... | collective-permute-start | bytes 3145736 | tf_op jit(solution)/shard_map/ppermute | solution.py:461
  61.2 3.2 %collective-permute-start.2 = (bf16[512,1024]{1,0:T(8,128)(2,1)}, bf16[512,1024]{1,0:T(8,128)(2,1)S(1)}, u32[]{:S(2)}, u32[]{:S(2)}) collective-permute-start(bf16[512,1024]{1,0:T(8,128)(2,1)} %broadcast_select_fusion.1), channel_id=1, source_target_pairs={{0,2},{2,0},{4,6},{6,4},{8,10},{10,8},{12,14},{14,12},{16,18},{18,... | collective-permute-start | bytes 3145736 | tf_op jit(solution)/shard_map/ppermute | solution.py:41
  64.4 25.9 %shard_map.117.rest_0_ = bf16[8,2048]{1,0:T(8,128)(2,1)} custom-call(s32[1]{0:T(128)} %bitcast.6.offset_ref, bf16[512,2048]{1,0:T(8,128)(2,1)} %q_ref.3, bf16[512,2688]{1,0:T(8,128)(2,1)} %pg_hbm.3, bf16[4096,2688]{1,0:T(8,128)(2,1)} %w_hbm.3, bf16[512,1024]{1,0:T(8,128)(2,1)} %collective-permute-done.6.recv_ref, ...), custom_call_target="tpu_custom_call" | custom-call | flops 13555990528 | bytes 10747904 | tf_op jit(solution)/shard_map/pallas_call | solution.py:372
  91.3 25.7 %shard_map.118 = bf16[8,4096]{1,0:T(8,128)(2,1)} custom-call(s32[1]{0:T(128)} %bitcast.offset_ref, bf16[512,2048]{1,0:T(8,128)(2,1)} %q_ref.3, bf16[512,2688]{1,0:T(8,128)(2,1)} %pg_hbm.3, bf16[4096,2688]{1,0:T(8,128)(2,1)} %w_hbm.3, bf16[512,1024]{1,0:T(8,128)(2,1)} %collective-permute-done.recv_ref, bf16[512,1024]{1,0:T(8,128)(2,1)} %collective-permute-done.1.k0.v0, ...), custom_call_target="tpu_custom_call" | custom-call | flops 13555990528 | bytes 10747904 | tf_op jit(solution)/shard_map/pallas_call | solution.py:372
  117.1 1.4 %collective-permute-done.9 = bf16[8,4096]{1,0:T(8,128)(2,1)S(1)} collective-permute-done((bf16[8,4096]{1,0:T(8,128)(2,1)}, bf16[8,4096]{1,0:T(8,128)(2,1)S(1)}, u32[]{:S(2)}, u32[]{:S(2)}) %collective-permute-start.9) | collective-permute-done | bytes 65568 | tf_op jit(solution)/shard_map/ppermute | solution.py:41
  119.4 1.6 %collective-permute-start.10 = (bf16[8,4096]{1,0:T(8,128)(2,1)S(1)}, bf16[8,4096]{1,0:T(8,128)(2,1)S(1)}, u32[]{:S(2)}, u32[]{:S(2)}) collective-permute-start(bf16[8,4096]{1,0:T(8,128)(2,1)S(1)} %add_convert_fusion.2), channel_id=1, source_target_pairs={{0,8},{2,10},{4,12},{6,14},{8,0},{10,2},{12,4},{14,6},{16,24},{18,... | collective-permute-start | bytes 196616 | tf_op jit(solution)/shard_map/ppermute | solution.py:41
  121.0 2.7 %collective-permute-done.10 = bf16[8,4096]{1,0:T(8,128)(2,1)S(1)} collective-permute-done((bf16[8,4096]{1,0:T(8,128)(2,1)S(1)}, bf16[8,4096]{1,0:T(8,128)(2,1)S(1)}, u32[]{:S(2)}, u32[]{:S(2)}) %collective-permute-start.10) | collective-permute-done | bytes 65568 | tf_op jit(solution)/shard_map/ppermute | solution.py:41
  123.7 2.6 %collective-permute-start.11 = (bf16[8,4096]{1,0:T(8,128)(2,1)S(1)}, bf16[8,4096]{1,0:T(8,128)(2,1)S(1)}, u32[]{:S(2)}, u32[]{:S(2)}) collective-permute-start(bf16[8,4096]{1,0:T(8,128)(2,1)S(1)} %add_convert_fusion.1), channel_id=1, source_target_pairs={{0,16},{2,18},{4,20},{6,22},{8,24},{10,26},{12,28},{14,30},{16,0},... | collective-permute-start | bytes 196616 | tf_op jit(solution)/shard_map/ppermute | solution.py:41
  126.4 2.6 %collective-permute-done.11 = bf16[8,4096]{1,0:T(8,128)(2,1)S(1)} collective-permute-done((bf16[8,4096]{1,0:T(8,128)(2,1)S(1)}, bf16[8,4096]{1,0:T(8,128)(2,1)S(1)}, u32[]{:S(2)}, u32[]{:S(2)}) %collective-permute-start.11) | collective-permute-done | bytes 65568 | tf_op jit(solution)/shard_map/ppermute | solution.py:41
  129.0 1.6 %collective-permute-start.12 = (bf16[8,4096]{1,0:T(8,128)(2,1)S(1)}, bf16[8,4096]{1,0:T(8,128)(2,1)S(1)}, u32[]{:S(2)}, u32[]{:S(2)}) collective-permute-start(bf16[8,4096]{1,0:T(8,128)(2,1)S(1)} %add_convert_fusion.refs_0_), channel_id=1, source_target_pairs={{0,4},{2,6},{4,0},{6,2},{8,12},{10,14},{12,8},{14,10},{16,20},{18,... | collective-permute-start | bytes 196616 | tf_op jit(solution)/shard_map/ppermute | solution.py:41
  130.6 2.7 %collective-permute-done.12.refs_1_ = bf16[8,4096]{1,0:T(8,128)(2,1)S(1)} collective-permute-done((bf16[8,4096]{1,0:T(8,128)(2,1)S(1)}, bf16[8,4096]{1,0:T(8,128)(2,1)S(1)}, u32[]{:S(2)}, u32[]{:S(2)}) %collective-permute-start.12) | collective-permute-done | bytes 65568 | tf_op jit(solution)/shard_map/ppermute | solution.py:41
  134.4 3.2 %collective-permute-done.13 = f32[1,1]{1,0:T(1,128)} collective-permute-done((f32[1,1]{1,0:T(1,128)}, f32[1,1]{1,0:T(1,128)}, u32[]{:S(2)}, u32[]{:S(2)}) %collective-permute-start.13) | collective-permute-done | bytes 36 | tf_op jit(solution)/shard_map/ppermute | solution.py:41
  (37 shorter events, 7.6 us)
Async XLA Ops:
  0.6 7.9 %copy-start.7 = (bf16[2688]{0:T(1024)(128)(2,1)S(1)}, bf16[2688]{0:T(1024)(128)(2,1)}, u32[]{:S(2)}) copy-start(bf16[2688]{0:T(1024)(128)(2,1)} %param.10) | copy-start | bytes 16132
  2.7 28.7 %collective-permute-start.7 = (bf16[512,1024]{1,0:T(8,128)(2,1)}, bf16[512,1024]{1,0:T(8,128)(2,1)}, u32[]{:S(2)}, u32[]{:S(2)}) collective-permute-start(bf16[512,1024]{1,0:T(8,128)(2,1)} %shard_map.116.k2.v2), channel_id=1, source_target_pairs={{0,4},{2,6},{4,8},{6,10},{8,12},{10,14},{12,16},{14,18},{16,20},{1... | collective-permute-start | bytes 3145736 | tf_op jit(solution)/shard_map/ppermute | solution.py:37
  9.2 22.2 %copy-start.5 = (bf16[512,1024]{1,0:T(8,128)(2,1)S(1)}, bf16[512,1024]{1,0:T(8,128)(2,1)}, u32[]{:S(2)}) copy-start(bf16[512,1024]{1,0:T(8,128)(2,1)} %shard_map.116.k2.v2) | copy-start | bytes 3145732
  18.9 13.6 %copy-start.1 = (f32[32,512]{1,0:T(8,128)S(1)}, f32[32,512]{1,0:T(8,128)}, u32[]{:S(2)}) copy-start(f32[32,512]{1,0:T(8,128)} %get-tuple-element.9.mine_ref) | copy-start | bytes 196612
  18.9 26.3 %copy-start.2 = (s32[512]{0:T(512)S(1)}, s32[512]{0:T(512)}, u32[]{:S(2)}) copy-start(s32[512]{0:T(512)} %param.11) | copy-start | bytes 6148
  18.9 45.5 %collective-permute-start.6 = (bf16[512,1024]{1,0:T(8,128)(2,1)}, bf16[512,1024]{1,0:T(8,128)(2,1)}, u32[]{:S(2)}, u32[]{:S(2)}) collective-permute-start(bf16[512,1024]{1,0:T(8,128)(2,1)} %get-tuple-element.12), channel_id=1, source_target_pairs={{0,1},{1,0},{2,3},{3,2},{4,5},{5,4},{6,7},{7,6},{8,9},{9,8},{10,11... | collective-permute-start | bytes 3145736 | tf_op jit(solution)/shard_map/ppermute | solution.py:461
  20.5 39.6 %collective-permute-start.1 = (bf16[512,1024]{1,0:T(8,128)(2,1)}, bf16[512,1024]{1,0:T(8,128)(2,1)}, u32[]{:S(2)}, u32[]{:S(2)}) collective-permute-start(bf16[512,1024]{1,0:T(8,128)(2,1)} %get-tuple-element.8.k2.v2), channel_id=1, source_target_pairs={{0,4},{2,6},{4,8},{6,10},{8,12},{10,14},{12,16},{14,18},{16,20},{1... | collective-permute-start | bytes 3145736 | tf_op jit(solution)/shard_map/ppermute | solution.py:37
  32.5 31.9 %collective-permute-start.8 = (bf16[512,1024]{1,0:T(8,128)(2,1)}, bf16[512,1024]{1,0:T(8,128)(2,1)}, u32[]{:S(2)}, u32[]{:S(2)}) collective-permute-start(bf16[512,1024]{1,0:T(8,128)(2,1)} %broadcast_select_fusion), channel_id=1, source_target_pairs={{0,2},{2,0},{4,6},{6,4},{8,10},{10,8},{12,14},{14,12},{16,18},{18,... | collective-permute-start | bytes 3145736 | tf_op jit(solution)/shard_map/ppermute | solution.py:41
  32.5 12.7 %collective-permute-start.3 = (f32[32,512]{1,0:T(8,128)S(1)}, f32[32,512]{1,0:T(8,128)S(1)}, u32[]{:S(2)}, u32[]{:S(2)}) collective-permute-start(f32[32,512]{1,0:T(8,128)S(1)} %copy-done.1), channel_id=1, source_target_pairs={{0,1},{1,0},{2,3},{3,2},{4,5},{5,4},{6,7},{7,6},{8,9},{9,8},{10,11... | collective-permute-start | bytes 196616 | tf_op jit(solution)/shard_map/ppermute | solution.py:41
  45.2 12.8 %copy-start = (bf16[32,512]{1,0:T(8,128)(2,1)}, bf16[32,512]{1,0:T(8,128)(2,1)S(1)}, u32[]{:S(2)}) copy-start(bf16[32,512]{1,0:T(8,128)(2,1)S(1)} %shard_map.114.t0_ref.lq_ref) | copy-start | bytes 98308
  45.3 11.3 %collective-permute-start.4 = (bf16[32,512]{1,0:T(8,128)(2,1)S(1)}, bf16[32,512]{1,0:T(8,128)(2,1)S(1)}, u32[]{:S(2)}, u32[]{:S(2)}) collective-permute-start(bf16[32,512]{1,0:T(8,128)(2,1)S(1)} %shard_map.114.t0_ref.lq_ref), channel_id=1, source_target_pairs={{0,4},{2,6},{4,8},{6,10},{8,12},{10,14},{12,16},{14,18},{16,20},{1... | collective-permute-start | bytes 98312 | tf_op jit(solution)/shard_map/ppermute | solution.py:37
  47.8 10.3 %collective-permute-start.5 = (bf16[32,512]{1,0:T(8,128)(2,1)S(1)}, bf16[32,512]{1,0:T(8,128)(2,1)S(1)}, u32[]{:S(2)}, u32[]{:S(2)}) collective-permute-start(bf16[32,512]{1,0:T(8,128)(2,1)S(1)} %shard_map.114.t0_ref.lq_ref), channel_id=1, source_target_pairs={{0,2},{2,4},{4,6},{6,8},{8,10},{10,12},{12,14},{14,16},{16,18},{18... | collective-permute-start | bytes 98312 | tf_op jit(solution)/shard_map/ppermute | solution.py:37
  49.1 11.0 %copy-start.6 = (bf16[512,1024]{1,0:T(8,128)(2,1)S(1)}, bf16[512,1024]{1,0:T(8,128)(2,1)}, u32[]{:S(2)}) copy-start(bf16[512,1024]{1,0:T(8,128)(2,1)} %get-tuple-element.8.k2.v2) | copy-start | bytes 3145732
  56.5 33.7 %collective-permute-start = (bf16[512,1024]{1,0:T(8,128)(2,1)}, bf16[512,1024]{1,0:T(8,128)(2,1)}, u32[]{:S(2)}, u32[]{:S(2)}) collective-permute-start(bf16[512,1024]{1,0:T(8,128)(2,1)} %shard_map.112), channel_id=1, source_target_pairs={{0,1},{1,0},{2,3},{3,2},{4,5},{5,4},{6,7},{7,6},{8,9},{9,8},{10,11... | collective-permute-start | bytes 3145736 | tf_op jit(solution)/shard_map/ppermute | solution.py:461
  58.6 0.8 copy-start.3
  59.4 0.7 copy-start.4
  61.2 29.1 %collective-permute-start.2 = (bf16[512,1024]{1,0:T(8,128)(2,1)}, bf16[512,1024]{1,0:T(8,128)(2,1)S(1)}, u32[]{:S(2)}, u32[]{:S(2)}) collective-permute-start(bf16[512,1024]{1,0:T(8,128)(2,1)} %broadcast_select_fusion.1), channel_id=1, source_target_pairs={{0,2},{2,0},{4,6},{6,4},{8,10},{10,8},{12,14},{14,12},{16,18},{18,... | collective-permute-start | bytes 3145736 | tf_op jit(solution)/shard_map/ppermute | solution.py:41
  90.3 1.0 copy-start.8
  117.0 1.5 %collective-permute-start.9 = (bf16[8,4096]{1,0:T(8,128)(2,1)}, bf16[8,4096]{1,0:T(8,128)(2,1)S(1)}, u32[]{:S(2)}, u32[]{:S(2)}) collective-permute-start(bf16[8,4096]{1,0:T(8,128)(2,1)} %shard_map.118), channel_id=1, source_target_pairs={{0,2},{2,0},{4,6},{6,4},{8,10},{10,8},{12,14},{14,12},{16,18},{18,... | collective-permute-start | bytes 196616 | tf_op jit(solution)/shard_map/ppermute | solution.py:41
  119.4 4.3 %collective-permute-start.10 = (bf16[8,4096]{1,0:T(8,128)(2,1)S(1)}, bf16[8,4096]{1,0:T(8,128)(2,1)S(1)}, u32[]{:S(2)}, u32[]{:S(2)}) collective-permute-start(bf16[8,4096]{1,0:T(8,128)(2,1)S(1)} %add_convert_fusion.2), channel_id=1, source_target_pairs={{0,8},{2,10},{4,12},{6,14},{8,0},{10,2},{12,4},{14,6},{16,24},{18,... | collective-permute-start | bytes 196616 | tf_op jit(solution)/shard_map/ppermute | solution.py:41
  123.7 5.2 %collective-permute-start.11 = (bf16[8,4096]{1,0:T(8,128)(2,1)S(1)}, bf16[8,4096]{1,0:T(8,128)(2,1)S(1)}, u32[]{:S(2)}, u32[]{:S(2)}) collective-permute-start(bf16[8,4096]{1,0:T(8,128)(2,1)S(1)} %add_convert_fusion.1), channel_id=1, source_target_pairs={{0,16},{2,18},{4,20},{6,22},{8,24},{10,26},{12,28},{14,30},{16,0},... | collective-permute-start | bytes 196616 | tf_op jit(solution)/shard_map/ppermute | solution.py:41
  129.0 4.3 %collective-permute-start.12 = (bf16[8,4096]{1,0:T(8,128)(2,1)S(1)}, bf16[8,4096]{1,0:T(8,128)(2,1)S(1)}, u32[]{:S(2)}, u32[]{:S(2)}) collective-permute-start(bf16[8,4096]{1,0:T(8,128)(2,1)S(1)} %add_convert_fusion.refs_0_), channel_id=1, source_target_pairs={{0,4},{2,6},{4,0},{6,2},{8,12},{10,14},{12,8},{14,10},{16,20},{18,... | collective-permute-start | bytes 196616 | tf_op jit(solution)/shard_map/ppermute | solution.py:41
  134.0 3.7 %collective-permute-start.13 = (f32[1,1]{1,0:T(1,128)}, f32[1,1]{1,0:T(1,128)}, u32[]{:S(2)}, u32[]{:S(2)}) collective-permute-start(f32[1,1]{1,0:T(1,128)} %bitcast.7), channel_id=1, source_target_pairs={{0,1},{1,0},{2,3},{3,2},{4,5},{5,4},{6,7},{7,6},{8,9},{9,8},{10,11... | collective-permute-start | bytes 20 | tf_op jit(solution)/shard_map/ppermute | solution.py:41

commit v3 on v2

--- a/solution.py
+++ b/solution.py
@@ -17,7 +17,7 @@
 LOG2E = 1.4426950408889634
 SCALE = float(MODEL_WIDTH // QUERY_HEADS) ** (-0.5)
 LANES = 128
-GRANT = 62 << 20
+GRANT = 52 << 20
 SMALL = pltpu.CompilerParams(vmem_limit_bytes=8 << 20)
 ROW_K, ROW_V, ROW_ONE, ROW_DOC = 0, ADAPTER_RANK, 2 * ADAPTER_RANK, 2 * ADAPTER_RANK + 1
 TABLE = 4 * ADAPTER_RANK
@@ -45,7 +45,7 @@
     out_ref[...] = dotf(gradient_ref[...], weight_ref[...], NT).astype(out_ref.dtype)
 
 
-def project(gradient, weight, first_block, blocks, width):
+def project(gradient, weight, first_block, blocks, width, dtype=jnp.bfloat16):
     rows, depth = gradient.shape
     return pl.pallas_call(
         project_body,
@@ -58,7 +58,7 @@
             ],
             out_specs=pl.BlockSpec((rows, width), lambda i, off: (0, i)),
         ),
-        out_shape=jax.ShapeDtypeStruct((rows, blocks * width), jnp.bfloat16),
+        out_shape=jax.ShapeDtypeStruct((rows, blocks * width), dtype),
         cost_estimate=pl.CostEstimate(
             flops=2 * rows * depth * width * blocks,
             bytes_accessed=2 * (rows * depth + width * blocks * depth + rows * width * blocks),
@@ -86,32 +86,15 @@
             pack_ref[:, wide:] = v_ref[...]
 
 
-def pack_body(k_ref, v_ref, out_ref):
-    wide = k_ref.shape[1]
-    out_ref[:, :wide] = k_ref[...]
-    out_ref[:, wide:] = v_ref[...]
-
-
-def pack_call(keys, values, wide, blocks):
-    rows = keys.shape[0]
-    return pl.pallas_call(
-        pack_body,
-        grid=(blocks,),
-        in_specs=[pl.BlockSpec((rows, wide), lambda i: (0, i))] * 2,
-        out_specs=pl.BlockSpec((rows, 2 * wide), lambda i: (0, i)),
-        out_shape=jax.ShapeDtypeStruct((rows, 2 * wide * blocks), keys.dtype),
-        compiler_params=pltpu.CompilerParams(vmem_limit_bytes=GRANT),
-    )(keys, values)
-
-
 def open_call(gradient, weight, first_block, blocks, width, x, norm, down, keys, values, chunks):
     rows, depth = gradient.shape
     slab = rows // blocks
     wide = keys.shape[1] // blocks
     each = blocks // chunks
-    skip = each
-    extra = chunks - 1
-    pack_specs = [pl.BlockSpec((rows, 2 * wide), lambda i, off: (0, jnp.minimum(i, each - 1)))] * extra
+    pack_specs = [
+        pl.BlockSpec((rows, 2 * wide), lambda i, off, c=c: (0, jnp.clip(i - c * each, 0, each - 1)))
+        for c in range(chunks)
+    ]
     pack_shape = jax.ShapeDtypeStruct((rows, 2 * wide * each), keys.dtype)
     return pl.pallas_call(
         functools.partial(open_body, each),
@@ -124,8 +107,8 @@
                 pl.BlockSpec((slab, depth), lambda i, off: (i, 0)),
                 pl.BlockSpec((1, depth), lambda i, off: (0, 0)),
                 pl.BlockSpec((3 * ADAPTER_RANK, depth), lambda i, off: (0, 0)),
-                pl.BlockSpec((rows, wide), lambda i, off: (0, jnp.minimum(i + skip, blocks - 1))),
-                pl.BlockSpec((rows, wide), lambda i, off: (0, jnp.minimum(i + skip, blocks - 1))),
+                pl.BlockSpec((rows, wide), lambda i, off: (0, i)),
+                pl.BlockSpec((rows, wide), lambda i, off: (0, i)),
             ],
             out_specs=[
                 pl.BlockSpec((rows, width), lambda i, off: (0, i)),
@@ -137,7 +120,7 @@
             jax.ShapeDtypeStruct((rows, blocks * width), jnp.bfloat16),
             jax.ShapeDtypeStruct((TABLE, rows), jnp.float32),
         ]
-        + [pack_shape] * extra,
+        + [pack_shape] * chunks,
         cost_estimate=pl.CostEstimate(
             flops=2 * rows * depth * width * blocks,
             bytes_accessed=2 * (2 * rows * depth + width * blocks * depth + rows * width * blocks),
@@ -175,15 +158,18 @@
     st_ref[...] = jnp.maximum(jnp.maximum(begin, band), first_ref[0])
 
 
-def attend_body(
-    steps, step_units, base, offset_ref, q_ref, pg_hbm, w_hbm, recv_ref, k0, k1, k2, v0, v1, v2, ext_ref, lq_ref, st_ref, *rest
-):
+def attend_body(steps, step_units, base, alone, offset_ref, q_ref, *rest):
+    if alone:
+        pg_hbm, w_hbm, *rest = rest
+    else:
+        own_ref, *rest = rest
+    recv_ref, k0, k1, k2, v0, v1, v2, ext_ref, lq_ref, st_ref, *rest = rest
     if base:
-        before_ref, out_ref, *scratch = rest
-    else:
-        out_ref, *scratch = rest
-    s_scr, e_scr, ve, ke, do_scr, pg_scr, w_scr, sems = scratch
-    rows = pg_scr.shape[0]
+        before_ref, *rest = rest
+    out_ref, s_scr, e_scr, ve, ke, do_scr, *rest = rest
+    if alone:
+        pg_scr, w_scr, sems = rest
+    rows = q_ref.shape[0]
     tile = s_scr.shape[1] // 2
     keys = s_scr.shape[2]
     width = tile
@@ -202,11 +188,13 @@
         first = pl.multiple_of((offset_ref[0] * step_units + group) * deep, deep)
         return pltpu.make_async_copy(w_hbm.at[pl.ds(first, deep), :], w_scr.at[group], sems.at[1 + group])
 
-    @pl.when(step == 0)
-    def _():
-        gradient_copy().start()
-        for group in range(steps * step_units):
-            weight_copy(group).start()
+    if alone:
+
+        @pl.when(step == 0)
+        def _():
+            gradient_copy().start()
+            for group in range(steps * step_units):
+                weight_copy(group).start()
 
     if base:
 
@@ -236,7 +224,10 @@
     def cotangent(i):
         g, t = units[i]
         if t == 0:
-            own = dotf(pg_scr[...], w_scr[step * step_units + g], NT)
+            if alone:
+                own = dotf(pg_scr[...], w_scr[step * step_units + g], NT)
+            else:
+                own = own_ref[:, deep * g : deep * (g + 1)]
             got = recv_ref[:, deep * g : deep * (g + 1)].astype(jnp.float32)
             do_scr[g % 2] = (own + got).astype(jnp.bfloat16)
 
@@ -314,12 +305,14 @@
     for j in columns:
         score(0, j)
 
-    @pl.when(step == 0)
-    def _():
-        gradient_copy().wait()
-
-    for g in range(step_units):
-        weight_copy(step * step_units + g).wait()
+    if alone:
+
+        @pl.when(step == 0)
+        def _():
+            gradient_copy().wait()
+
+        for g in range(step_units):
+            weight_copy(step * step_units + g).wait()
     cotangent(0)
     for i in range(len(units) + 1):
         if i < len(units):
@@ -340,7 +333,7 @@
             backed(i - 1)
 
 
-def attend(queries, gradient, weight, recv, packs, ext, table, starts, first, skip, steps, units, before):
+def attend(queries, gradient, weight, recv, own, packs, ext, table, starts, first, skip, steps, units, before):
     rows, depth = gradient.shape
     tile = rows // 2
     keys = LOOKBACK_SPAN + tile
@@ -349,12 +342,13 @@
     col = lambda width, fn: pl.BlockSpec((rows, width), fn)
     total = base + 4 * LANES * groups
     wide = units * LANES
-    operands = [queries, gradient, weight, recv, *packs, *packs, ext, table, starts]
+    alone = own is None
+    source = [gradient, weight] if alone else [own]
+    operands = [queries, *source, recv, *packs, *packs, ext, table, starts]
     in_specs = (
         [
             col(2 * wide, lambda g, off: (0, g + skip)),
-            pl.BlockSpec(memory_space=pl.ANY),
-            pl.BlockSpec(memory_space=pl.ANY),
+            *([pl.BlockSpec(memory_space=pl.ANY)] * 2 if alone else [col(2 * wide, lambda g, off: (0, g))]),
             col(2 * wide, lambda g, off: (0, g)),
         ]
         + [col(wide, lambda g, off: (0, 2 * g))] * 3
@@ -370,7 +364,7 @@
         in_specs.append(pl.BlockSpec((ADAPTER_RANK, base), lambda g, off: (0, 0)))
     pushes = rows * groups * 2 * keys // 256 * 4
     return pl.pallas_call(
-        functools.partial(attend_body, steps, units, base),
+        functools.partial(attend_body, steps, units, base, alone),
         grid_spec=pltpu.PrefetchScalarGridSpec(
             num_scalar_prefetch=1,
             grid=(steps,),
@@ -382,6 +376,9 @@
                 pltpu.VMEM((2, 3 * rows, 2 * LANES), jnp.bfloat16),
                 pltpu.VMEM((2, 3 * rows, 2 * LANES), jnp.bfloat16),
                 pltpu.VMEM((2, rows, 2 * LANES), jnp.bfloat16),
+            ]
+            + alone
+            * [
                 pltpu.VMEM((rows, depth), jnp.bfloat16),
                 pltpu.VMEM((groups, 2 * LANES, depth), jnp.bfloat16),
                 pltpu.SemaphoreType.DMA((1 + groups,)),
@@ -389,7 +386,7 @@
         ),
         out_shape=jax.ShapeDtypeStruct((ADAPTER_RANK, total), jnp.bfloat16),
         cost_estimate=pl.CostEstimate(
-            flops=pushes * 256 * 256 * 2 + 2 * rows * depth * 2 * LANES * groups,
+            flops=pushes * 256 * 256 * 2 + alone * 2 * rows * depth * 2 * LANES * groups,
             bytes_accessed=groups * rows * LANES * 20 + 4 * LANES * groups * depth,
             transcendentals=rows * groups * 2 * keys,
         ),
@@ -434,16 +431,13 @@
     per = half // chunks
     scalar = lambda value: jnp.asarray(value, jnp.int32).reshape(1)
 
-    packs = [pack_call(stored_keys, stored_values, units * LANES, steps)]
-    fars = [shifted(packs[0], "ctx", 2)]
-
     received = []
     for c in range(chunks):
         got = []
         for d in range(1, tp):
             first = scalar(((tp_at + d) % tp) * half + c * per)
             if c == 0 and d == 1:
-                part, low, *more = open_call(
+                part, low, *packs = open_call(
                     projection_gradient,
                     output_weight,
                     first,
@@ -498,18 +492,21 @@
     second = (ctx_at % 2) == 1
     sums = None
     for c in range(chunks):
-        if c > 0:
-            packs.append(more[c - 1])
-            fars.append(shifted(packs[c], "ctx", 2))
-        picked = jnp.where(second, fars[c], packs[c])
+        far = shifted(packs[c], "ctx", 2)
+        picked = jnp.where(second, far, packs[c])
         near = xor_move(picked, "ctx", 1)
         first = scalar((tp_at * half + c * per) // units)
+        own = None
+        if c < chunks - 1:
+            begin = scalar(tp_at * half + c * per)
+            own = project(projection_gradient, output_weight, begin, per, width, jnp.float32)
         sums = attend(
             stored_queries,
             projection_gradient,
             output_weight,
             received[c],
-            (fars[c], near, packs[c]),
+            own,
+            (far, near, packs[c]),
             ext,
             table,
             starts,

time: 140 us -> 146 us (1.043)
  waiting for transfers between devices: 31.3 us -> 34.9 us
  starting transfers between devices: 27.4 us -> 30.3 us
  other arithmetic: 3.73 us -> 5.79 us
  local copies, waits for them, and re-layouts: 3.08 us -> 1.61 us
    ppermute x4, waiting for transfers between devices: 7.48 us -> 23.9 us  [shifted(): lax.ppermute(value, axis, [(source, source + steps) for source in range(f...]
    ppermute x8, waiting for transfers between devices: 23.8 us -> 11.1 us  [xor_move(): lax.ppermute(value, axis, [(at, at ^ step) for at in range(lax.axis_size(...]
    pallas_call x3 -> x2, Pallas kernels: 53.7 us -> 45.5 us  [attend(): pl.pallas_call(functools.partial(attend_body, steps, units, base, alone),...]
    pallas_call x1 -> x2, Pallas kernels: 7.47 us -> 14.1 us  [project(): pl.pallas_call(project_body, grid_spec=pltpu.PrefetchScalarGridSpec(num_s...]
    select_n x2, other arithmetic: 2.2 us -> 5.1 us  [local(): picked = jnp.where(second, far, packs[c])]
    ppermute x4, starting transfers between devices: 13.1 us -> 15.1 us  [shifted(): lax.ppermute(value, axis, [(source, source + steps) for source in range(f...]
    ppermute x8, starting transfers between devices: 11.2 us -> 13.1 us  [xor_move(): lax.ppermute(value, axis, [(at, at ^ step) for at in range(lax.axis_size(...]
    unnamed x18 -> x6, local copies, waits for them, and re-layouts: 2.47 us -> 0.91 us
  transfers between devices with their start and end apart: 14 -> 14, of which waited for: 7 -> 7; matrix products, arithmetic and copies ran while one was open for 2% -> 4% of each run, Pallas kernels for 31% -> 24%
where the time goes in v3:
time: 146 us
  Pallas kernels  70.8 us (48%)
  waiting for transfers between devices  34.9 us (24%)
  starting transfers between devices  30.3 us (21%)
  other arithmetic  5.79 us (4%)
  between operations  2.05 us (1%)
  local copies, waits for them, and re-layouts  1.61 us (1%)
    pallas_call x2, Pallas kernels, attend(): pl.pallas_call(functools.partial(attend_body, steps, units, base, alone),...  45.5 us
    ppermute x4, waiting for transfers between devices, shifted(): lax.ppermute(value, axis, [(source, source + steps) for source in range(f...  23.9 us
    ppermute x4, starting transfers between devices, shifted(): lax.ppermute(value, axis, [(source, source + steps) for source in range(f...  15.1 us
    pallas_call x2, Pallas kernels, project(): pl.pallas_call(project_body, grid_spec=pltpu.PrefetchScalarGridSpec(num_s...  14.1 us
    ppermute x8, starting transfers between devices, xor_move(): lax.ppermute(value, axis, [(at, at ^ step) for at in range(lax.axis_size(...  13.1 us
    ppermute x8, waiting for transfers between devices, xor_move(): lax.ppermute(value, axis, [(at, at ^ step) for at in range(lax.axis_size(...  11.1 us
    pallas_call x1, Pallas kernels, open_call(): pl.pallas_call(functools.partial(open_body, each), grid_spec=pltpu.Prefet...  9.93 us
    select_n x2, other arithmetic, local(): picked = jnp.where(second, far, packs[c])  5.1 us
  transfers between devices with their start and end apart: 14, of which 7 were waited for; matrix products, arithmetic and copies ran while one was open for 4% of the time, Pallas kernels for 24%

profile of v3, /device:TPU:0, one launch (start us, length us, event | category | flops | bytes accessed | tf_op | source)
XLA Modules:
  0.0 145.5 jit_solution(2744310546374888052)
XLA Ops:
  2.2 9.9 %shard_map.113 = (bf16[512,1024]{1,0:T(8,128)(2,1)S(1)}, f32[32,512]{1,0:T(8,128)S(1)}, bf16[512,1024]{1,0:T(8,128)(2,1)}, bf16[512,1024]{1,0:T(8,128)(2,1)}) custom-call(s32[1]{0:T(128)} %bitcast.2.offset_ref, bf16[512,2688]{1,0:T(8,128)(2,1)} %rest_0_.3, bf16[4096,2688]{1,0:T(8,128)(2,1)} %rest_1_.3, bf16[512,2688]{1,0:T(8,128)(2,1)} %x_ref.1, ...), custom_call_target="tpu_custom_call" | custom-call | flops 2818572288 | bytes 12058624 | tf_op jit(solution)/shard_map/pallas_call | solution.py:99
  12.2 4.9 %collective-permute-start.7 = (bf16[512,1024]{1,0:T(8,128)(2,1)}, bf16[512,1024]{1,0:T(8,128)(2,1)S(1)}, u32[]{:S(2)}, u32[]{:S(2)}) collective-permute-start(bf16[512,1024]{1,0:T(8,128)(2,1)} %get-tuple-element.14.rest_4_.rest_7_), channel_id=1, source_target_pairs={{0,4},{2,6},{4,8},{6,10},{8,12},{10,14},{12,16},{14,18},{16,20},{1... | collective-permute-start | bytes 3145736 | tf_op jit(solution)/shard_map/ppermute | solution.py:37
  17.1 4.4 %collective-permute-start.1 = (bf16[512,1024]{1,0:T(8,128)(2,1)}, bf16[512,1024]{1,0:T(8,128)(2,1)}, u32[]{:S(2)}, u32[]{:S(2)}) collective-permute-start(bf16[512,1024]{1,0:T(8,128)(2,1)} %get-tuple-element.9.rest_5_.rest_8_), channel_id=1, source_target_pairs={{0,4},{2,6},{4,8},{6,10},{8,12},{10,14},{12,16},{14,18},{16,20},{1... | collective-permute-start | bytes 3145736 | tf_op jit(solution)/shard_map/ppermute | solution.py:37
  21.5 1.5 %collective-permute-start.6 = (bf16[512,1024]{1,0:T(8,128)(2,1)S(1)}, bf16[512,1024]{1,0:T(8,128)(2,1)S(1)}, u32[]{:S(2)}, u32[]{:S(2)}) collective-permute-start(bf16[512,1024]{1,0:T(8,128)(2,1)S(1)} %get-tuple-element.13), channel_id=1, source_target_pairs={{0,1},{1,0},{2,3},{3,2},{4,5},{5,4},{6,7},{7,6},{8,9},{9,8},{10,11... | collective-permute-start | bytes 3145736 | tf_op jit(solution)/shard_map/ppermute | solution.py:455
  23.1 17.9 %collective-permute-done.7.rest_2_.rest_5_ = bf16[512,1024]{1,0:T(8,128)(2,1)S(1)} collective-permute-done((bf16[512,1024]{1,0:T(8,128)(2,1)}, bf16[512,1024]{1,0:T(8,128)(2,1)S(1)}, u32[]{:S(2)}, u32[]{:S(2)}) %collective-permute-start.7) | collective-permute-done | bytes 1048608 | tf_op jit(solution)/shard_map/ppermute | solution.py:37
  40.9 2.7 %broadcast_select_fusion = bf16[512,1024]{1,0:T(8,128)(2,1)} fusion(bf16[512,1024]{1,0:T(8,128)(2,1)S(1)} %collective-permute-done.7.rest_2_.rest_5_, bf16[512,1024]{1,0:T(8,128)(2,1)} %get-tuple-element.14.rest_4_.rest_7_, pred[]{:T(512)S(6)} %eq.7), kind=kLoop, calls=%fused_computation | loop fusion | flops 524288 | bytes 3145729 | tf_op jit(solution)/shard_map/jit(_where)/select_n | solution.py:496
  43.6 1.5 %collective-permute-start.3 = (f32[32,512]{1,0:T(8,128)S(1)}, f32[32,512]{1,0:T(8,128)S(1)}, u32[]{:S(2)}, u32[]{:S(2)}) collective-permute-start(f32[32,512]{1,0:T(8,128)S(1)} %get-tuple-element.10.mine_ref), channel_id=1, source_target_pairs={{0,1},{1,0},{2,3},{3,2},{4,5},{5,4},{6,7},{7,6},{8,9},{9,8},{10,11... | collective-permute-start | bytes 196616 | tf_op jit(solution)/shard_map/ppermute | solution.py:41
  45.1 6.6 %shard_map.112 = bf16[512,1024]{1,0:T(8,128)(2,1)S(1)} custom-call(s32[1]{0:T(128)} %bitcast.1.offset_ref, bf16[512,2688]{1,0:T(8,128)(2,1)} %rest_0_.3, bf16[4096,2688]{1,0:T(8,128)(2,1)} %rest_1_.3), custom_call_target="tpu_custom_call" | custom-call | flops 2818572288 | bytes 9306112 | tf_op jit(solution)/shard_map/pallas_call | solution.py:50
  52.3 4.3 %collective-permute-start.4 = (bf16[32,512]{1,0:T(8,128)(2,1)S(1)}, bf16[32,512]{1,0:T(8,128)(2,1)S(1)}, u32[]{:S(2)}, u32[]{:S(2)}) collective-permute-start(bf16[32,512]{1,0:T(8,128)(2,1)S(1)} %shard_map.114.t0_ref.rest_9_.rest_10_), channel_id=1, source_target_pairs={{0,4},{2,6},{4,8},{6,10},{8,12},{10,14},{12,16},{14,18},{16,20},{1... | collective-permute-start | bytes 98312 | tf_op jit(solution)/shard_map/ppermute | solution.py:37
  56.6 6.0 %collective-permute-done.1.rest_3_.rest_6_ = bf16[512,1024]{1,0:T(8,128)(2,1)} collective-permute-done((bf16[512,1024]{1,0:T(8,128)(2,1)}, bf16[512,1024]{1,0:T(8,128)(2,1)}, u32[]{:S(2)}, u32[]{:S(2)}) %collective-permute-start.1) | collective-permute-done | bytes 1048608 | tf_op jit(solution)/shard_map/ppermute | solution.py:37
  62.6 1.5 %collective-permute-start.5 = (bf16[32,512]{1,0:T(8,128)(2,1)S(1)}, bf16[32,512]{1,0:T(8,128)(2,1)S(1)}, u32[]{:S(2)}, u32[]{:S(2)}) collective-permute-start(bf16[32,512]{1,0:T(8,128)(2,1)S(1)} %shard_map.114.t0_ref.rest_9_.rest_10_), channel_id=1, source_target_pairs={{0,2},{2,4},{4,6},{6,8},{8,10},{10,12},{12,14},{14,16},{16,18},{18... | collective-permute-start | bytes 98312 | tf_op jit(solution)/shard_map/ppermute | solution.py:37
  64.1 2.4 %broadcast_select_fusion.1 = bf16[512,1024]{1,0:T(8,128)(2,1)} fusion(bf16[512,1024]{1,0:T(8,128)(2,1)} %collective-permute-done.1.rest_3_.rest_6_, bf16[512,1024]{1,0:T(8,128)(2,1)} %get-tuple-element.9.rest_5_.rest_8_, pred[]{:T(512)S(6)} %eq.7), kind=kLoop, calls=%fused_computation.1 | loop fusion | flops 524288 | bytes 3145729 | tf_op jit(solution)/shard_map/jit(_where)/select_n | solution.py:496
  66.5 3.2 %collective-permute-start.2 = (bf16[512,1024]{1,0:T(8,128)(2,1)}, bf16[512,1024]{1,0:T(8,128)(2,1)}, u32[]{:S(2)}, u32[]{:S(2)}) collective-permute-start(bf16[512,1024]{1,0:T(8,128)(2,1)} %broadcast_select_fusion.1), channel_id=1, source_target_pairs={{0,2},{2,0},{4,6},{6,4},{8,10},{10,8},{12,14},{14,12},{16,18},{18,... | collective-permute-start | bytes 3145736 | tf_op jit(solution)/shard_map/ppermute | solution.py:41
  69.7 7.5 %shard_map.116.rest_0_ = f32[512,1024]{1,0:T(8,128)} custom-call(s32[1]{0:T(128)} %bitcast.7.offset_ref, bf16[512,2688]{1,0:T(8,128)(2,1)} %rest_0_.3, bf16[4096,2688]{1,0:T(8,128)(2,1)} %rest_1_.3), custom_call_target="tpu_custom_call" | custom-call | flops 2818572288 | bytes 9306112 | tf_op jit(solution)/shard_map/pallas_call | solution.py:50
  77.8 20.6 %shard_map.117.rest_12_ = bf16[8,2048]{1,0:T(8,128)(2,1)S(1)} custom-call(s32[1]{0:T(128)} %bitcast.6.offset_ref, bf16[512,2048]{1,0:T(8,128)(2,1)} %q_ref.3, f32[512,1024]{1,0:T(8,128)} %shard_map.116.rest_0_, bf16[512,1024]{1,0:T(8,128)(2,1)S(1)} %collective-permute-done.6.rest_1_, bf16[512,1024]{1,0:T(8,128)(2,1)} %copy-done.2, ...), custom_call_target="tpu_custom_call" | custom-call | flops 10737418240 | bytes 10747904 | tf_op jit(solution)/shard_map/pallas_call | solution.py:366
  98.4 24.9 %shard_map.118 = bf16[8,4096]{1,0:T(8,128)(2,1)S(1)} custom-call(s32[1]{0:T(128)} %bitcast.offset_ref, bf16[512,2048]{1,0:T(8,128)(2,1)} %q_ref.3, bf16[512,2688]{1,0:T(8,128)(2,1)} %rest_0_.3, bf16[4096,2688]{1,0:T(8,128)(2,1)} %rest_1_.3, bf16[512,1024]{1,0:T(8,128)(2,1)} %collective-permute-done.rest_2_, ...), custom_call_target="tpu_custom_call" | custom-call | flops 13555990528 | bytes 10747904 | tf_op jit(solution)/shard_map/pallas_call | solution.py:366
  124.7 1.7 %collective-permute-start.10 = (bf16[8,4096]{1,0:T(8,128)(2,1)S(1)}, bf16[8,4096]{1,0:T(8,128)(2,1)S(1)}, u32[]{:S(2)}, u32[]{:S(2)}) collective-permute-start(bf16[8,4096]{1,0:T(8,128)(2,1)S(1)} %add_convert_fusion.2), channel_id=1, source_target_pairs={{0,8},{2,10},{4,12},{6,14},{8,0},{10,2},{12,4},{14,6},{16,24},{18,... | collective-permute-start | bytes 196616 | tf_op jit(solution)/shard_map/ppermute | solution.py:41
  126.3 2.7 %collective-permute-done.10 = bf16[8,4096]{1,0:T(8,128)(2,1)S(1)} collective-permute-done((bf16[8,4096]{1,0:T(8,128)(2,1)S(1)}, bf16[8,4096]{1,0:T(8,128)(2,1)S(1)}, u32[]{:S(2)}, u32[]{:S(2)}) %collective-permute-start.10) | collective-permute-done | bytes 65568 | tf_op jit(solution)/shard_map/ppermute | solution.py:41
  129.0 2.6 %collective-permute-start.11 = (bf16[8,4096]{1,0:T(8,128)(2,1)S(1)}, bf16[8,4096]{1,0:T(8,128)(2,1)S(1)}, u32[]{:S(2)}, u32[]{:S(2)}) collective-permute-start(bf16[8,4096]{1,0:T(8,128)(2,1)S(1)} %add_convert_fusion.1), channel_id=1, source_target_pairs={{0,16},{2,18},{4,20},{6,22},{8,24},{10,26},{12,28},{14,30},{16,0},... | collective-permute-start | bytes 196616 | tf_op jit(solution)/shard_map/ppermute | solution.py:41
  131.7 2.6 %collective-permute-done.11 = bf16[8,4096]{1,0:T(8,128)(2,1)S(1)} collective-permute-done((bf16[8,4096]{1,0:T(8,128)(2,1)S(1)}, bf16[8,4096]{1,0:T(8,128)(2,1)S(1)}, u32[]{:S(2)}, u32[]{:S(2)}) %collective-permute-start.11) | collective-permute-done | bytes 65568 | tf_op jit(solution)/shard_map/ppermute | solution.py:41
  134.3 2.5 %collective-permute-start.12 = (bf16[8,4096]{1,0:T(8,128)(2,1)S(1)}, bf16[8,4096]{1,0:T(8,128)(2,1)S(1)}, u32[]{:S(2)}, u32[]{:S(2)}) collective-permute-start(bf16[8,4096]{1,0:T(8,128)(2,1)S(1)} %add_convert_fusion.refs_0_), channel_id=1, source_target_pairs={{0,4},{2,6},{4,0},{6,2},{8,12},{10,14},{12,8},{14,10},{16,20},{18,... | collective-permute-start | bytes 196616 | tf_op jit(solution)/shard_map/ppermute | solution.py:41
  136.8 2.2 %collective-permute-done.12.refs_1_ = bf16[8,4096]{1,0:T(8,128)(2,1)S(1)} collective-permute-done((bf16[8,4096]{1,0:T(8,128)(2,1)S(1)}, bf16[8,4096]{1,0:T(8,128)(2,1)S(1)}, u32[]{:S(2)}, u32[]{:S(2)}) %collective-permute-start.12) | collective-permute-done | bytes 65568 | tf_op jit(solution)/shard_map/ppermute | solution.py:41
  139.7 1.5 %collective-permute-start.13 = (f32[1,1]{1,0:T(1,128)}, f32[1,1]{1,0:T(1,128)}, u32[]{:S(2)}, u32[]{:S(2)}) collective-permute-start(f32[1,1]{1,0:T(1,128)} %bitcast.8), channel_id=1, source_target_pairs={{0,1},{1,0},{2,3},{3,2},{4,5},{5,4},{6,7},{7,6},{8,9},{9,8},{10,11... | collective-permute-start | bytes 20 | tf_op jit(solution)/shard_map/ppermute | solution.py:41
  141.2 2.3 %collective-permute-done.13 = f32[1,1]{1,0:T(1,128)} collective-permute-done((f32[1,1]{1,0:T(1,128)}, f32[1,1]{1,0:T(1,128)}, u32[]{:S(2)}, u32[]{:S(2)}) %collective-permute-start.13) | collective-permute-done | bytes 36 | tf_op jit(solution)/shard_map/ppermute | solution.py:41
  (25 shorter events, 5.5 us)
Async XLA Ops:
  1.3 0.9 copy-start
  12.2 28.7 %collective-permute-start.7 = (bf16[512,1024]{1,0:T(8,128)(2,1)}, bf16[512,1024]{1,0:T(8,128)(2,1)S(1)}, u32[]{:S(2)}, u32[]{:S(2)}) collective-permute-start(bf16[512,1024]{1,0:T(8,128)(2,1)} %get-tuple-element.14.rest_4_.rest_7_), channel_id=1, source_target_pairs={{0,4},{2,6},{4,8},{6,10},{8,12},{10,14},{12,16},{14,18},{16,20},{1... | collective-permute-start | bytes 3145736 | tf_op jit(solution)/shard_map/ppermute | solution.py:37
  17.1 45.5 %collective-permute-start.1 = (bf16[512,1024]{1,0:T(8,128)(2,1)}, bf16[512,1024]{1,0:T(8,128)(2,1)}, u32[]{:S(2)}, u32[]{:S(2)}) collective-permute-start(bf16[512,1024]{1,0:T(8,128)(2,1)} %get-tuple-element.9.rest_5_.rest_8_), channel_id=1, source_target_pairs={{0,4},{2,6},{4,8},{6,10},{8,12},{10,14},{12,16},{14,18},{16,20},{1... | collective-permute-start | bytes 3145736 | tf_op jit(solution)/shard_map/ppermute | solution.py:37
  21.5 56.2 %collective-permute-start.6 = (bf16[512,1024]{1,0:T(8,128)(2,1)S(1)}, bf16[512,1024]{1,0:T(8,128)(2,1)S(1)}, u32[]{:S(2)}, u32[]{:S(2)}) collective-permute-start(bf16[512,1024]{1,0:T(8,128)(2,1)S(1)} %get-tuple-element.13), channel_id=1, source_target_pairs={{0,1},{1,0},{2,3},{3,2},{4,5},{5,4},{6,7},{7,6},{8,9},{9,8},{10,11... | collective-permute-start | bytes 3145736 | tf_op jit(solution)/shard_map/ppermute | solution.py:455
  40.9 4.2 %copy-start.2 = (bf16[512,1024]{1,0:T(8,128)(2,1)}, bf16[512,1024]{1,0:T(8,128)(2,1)S(1)}, u32[]{:S(2)}) copy-start(bf16[512,1024]{1,0:T(8,128)(2,1)S(1)} %collective-permute-done.7.rest_2_.rest_5_) | copy-start | bytes 3145732
  43.6 34.2 %collective-permute-start.8 = (bf16[512,1024]{1,0:T(8,128)(2,1)}, bf16[512,1024]{1,0:T(8,128)(2,1)}, u32[]{:S(2)}, u32[]{:S(2)}) collective-permute-start(bf16[512,1024]{1,0:T(8,128)(2,1)} %broadcast_select_fusion), channel_id=1, source_target_pairs={{0,2},{2,0},{4,6},{6,4},{8,10},{10,8},{12,14},{14,12},{16,18},{18,... | collective-permute-start | bytes 3145736 | tf_op jit(solution)/shard_map/ppermute | solution.py:41
  43.6 8.7 %collective-permute-start.3 = (f32[32,512]{1,0:T(8,128)S(1)}, f32[32,512]{1,0:T(8,128)S(1)}, u32[]{:S(2)}, u32[]{:S(2)}) collective-permute-start(f32[32,512]{1,0:T(8,128)S(1)} %get-tuple-element.10.mine_ref), channel_id=1, source_target_pairs={{0,1},{1,0},{2,3},{3,2},{4,5},{5,4},{6,7},{7,6},{8,9},{9,8},{10,11... | collective-permute-start | bytes 196616 | tf_op jit(solution)/shard_map/ppermute | solution.py:41
  45.1 7.2 %copy-start.1 = (s32[512]{0:T(512)S(1)}, s32[512]{0:T(512)}, u32[]{:S(2)}) copy-start(s32[512]{0:T(512)} %param.11) | copy-start | bytes 6148
  51.7 46.7 %collective-permute-start = (bf16[512,1024]{1,0:T(8,128)(2,1)S(1)}, bf16[512,1024]{1,0:T(8,128)(2,1)}, u32[]{:S(2)}, u32[]{:S(2)}) collective-permute-start(bf16[512,1024]{1,0:T(8,128)(2,1)S(1)} %shard_map.112), channel_id=1, source_target_pairs={{0,1},{1,0},{2,3},{3,2},{4,5},{5,4},{6,7},{7,6},{8,9},{9,8},{10,11... | collective-permute-start | bytes 3145736 | tf_op jit(solution)/shard_map/ppermute | solution.py:455
  52.3 14.2 %collective-permute-start.4 = (bf16[32,512]{1,0:T(8,128)(2,1)S(1)}, bf16[32,512]{1,0:T(8,128)(2,1)S(1)}, u32[]{:S(2)}, u32[]{:S(2)}) collective-permute-start(bf16[32,512]{1,0:T(8,128)(2,1)S(1)} %shard_map.114.t0_ref.rest_9_.rest_10_), channel_id=1, source_target_pairs={{0,4},{2,6},{4,8},{6,10},{8,12},{10,14},{12,16},{14,18},{16,20},{1... | collective-permute-start | bytes 98312 | tf_op jit(solution)/shard_map/ppermute | solution.py:37
  62.6 14.6 %collective-permute-start.5 = (bf16[32,512]{1,0:T(8,128)(2,1)S(1)}, bf16[32,512]{1,0:T(8,128)(2,1)S(1)}, u32[]{:S(2)}, u32[]{:S(2)}) collective-permute-start(bf16[32,512]{1,0:T(8,128)(2,1)S(1)} %shard_map.114.t0_ref.rest_9_.rest_10_), channel_id=1, source_target_pairs={{0,2},{2,4},{4,6},{6,8},{8,10},{10,12},{12,14},{14,16},{16,18},{18... | collective-permute-start | bytes 98312 | tf_op jit(solution)/shard_map/ppermute | solution.py:37
  66.5 32.0 %collective-permute-start.2 = (bf16[512,1024]{1,0:T(8,128)(2,1)}, bf16[512,1024]{1,0:T(8,128)(2,1)}, u32[]{:S(2)}, u32[]{:S(2)}) collective-permute-start(bf16[512,1024]{1,0:T(8,128)(2,1)} %broadcast_select_fusion.1), channel_id=1, source_target_pairs={{0,2},{2,0},{4,6},{6,4},{8,10},{10,8},{12,14},{14,12},{16,18},{18,... | collective-permute-start | bytes 3145736 | tf_op jit(solution)/shard_map/ppermute | solution.py:41
  123.3 1.3 collective-permute-start.9
  124.7 4.3 %collective-permute-start.10 = (bf16[8,4096]{1,0:T(8,128)(2,1)S(1)}, bf16[8,4096]{1,0:T(8,128)(2,1)S(1)}, u32[]{:S(2)}, u32[]{:S(2)}) collective-permute-start(bf16[8,4096]{1,0:T(8,128)(2,1)S(1)} %add_convert_fusion.2), channel_id=1, source_target_pairs={{0,8},{2,10},{4,12},{6,14},{8,0},{10,2},{12,4},{14,6},{16,24},{18,... | collective-permute-start | bytes 196616 | tf_op jit(solution)/shard_map/ppermute | solution.py:41
  129.0 5.2 %collective-permute-start.11 = (bf16[8,4096]{1,0:T(8,128)(2,1)S(1)}, bf16[8,4096]{1,0:T(8,128)(2,1)S(1)}, u32[]{:S(2)}, u32[]{:S(2)}) collective-permute-start(bf16[8,4096]{1,0:T(8,128)(2,1)S(1)} %add_convert_fusion.1), channel_id=1, source_target_pairs={{0,16},{2,18},{4,20},{6,22},{8,24},{10,26},{12,28},{14,30},{16,0},... | collective-permute-start | bytes 196616 | tf_op jit(solution)/shard_map/ppermute | solution.py:41
  134.3 4.8 %collective-permute-start.12 = (bf16[8,4096]{1,0:T(8,128)(2,1)S(1)}, bf16[8,4096]{1,0:T(8,128)(2,1)S(1)}, u32[]{:S(2)}, u32[]{:S(2)}) collective-permute-start(bf16[8,4096]{1,0:T(8,128)(2,1)S(1)} %add_convert_fusion.refs_0_), channel_id=1, source_target_pairs={{0,4},{2,6},{4,0},{6,2},{8,12},{10,14},{12,8},{14,10},{16,20},{18,... | collective-permute-start | bytes 196616 | tf_op jit(solution)/shard_map/ppermute | solution.py:41
  139.7 3.8 %collective-permute-start.13 = (f32[1,1]{1,0:T(1,128)}, f32[1,1]{1,0:T(1,128)}, u32[]{:S(2)}, u32[]{:S(2)}) collective-permute-start(f32[1,1]{1,0:T(1,128)} %bitcast.8), channel_id=1, source_target_pairs={{0,1},{1,0},{2,3},{3,2},{4,5},{5,4},{6,7},{7,6},{8,9},{9,8},{10,11... | collective-permute-start | bytes 20 | tf_op jit(solution)/shard_map/ppermute | solution.py:41

commit v4 on v3

--- a/solution.py
+++ b/solution.py
@@ -41,63 +41,78 @@
     return lax.ppermute(value, axis, [(at, at ^ step) for at in range(lax.axis_size(axis))])
 
 
-def project_body(offset_ref, gradient_ref, weight_ref, out_ref):
+def project_body(offset_ref, gradient_ref, weight_ref, *rest):
+    if len(rest) > 1:
+        k_ref, v_ref, out_ref, pack_ref = rest
+        wide = k_ref.shape[1]
+        pack_ref[:, :wide] = k_ref[...]
+        pack_ref[:, wide:] = v_ref[...]
+    else:
+        (out_ref,) = rest
     out_ref[...] = dotf(gradient_ref[...], weight_ref[...], NT).astype(out_ref.dtype)
 
 
-def project(gradient, weight, first_block, blocks, width, dtype=jnp.bfloat16):
+def pack_body(k_ref, v_ref, out_ref):
+    wide = k_ref.shape[1]
+    out_ref[:, :wide] = k_ref[...]
+    out_ref[:, wide:] = v_ref[...]
+
+
+def pack_call(keys, values, wide, blocks):
+    rows = keys.shape[0]
+    return pl.pallas_call(
+        pack_body,
+        grid=(blocks,),
+        in_specs=[pl.BlockSpec((rows, wide), lambda i: (0, i))] * 2,
+        out_specs=pl.BlockSpec((rows, 2 * wide), lambda i: (0, i)),
+        out_shape=jax.ShapeDtypeStruct((rows, 2 * wide * blocks), keys.dtype),
+        compiler_params=pltpu.CompilerParams(vmem_limit_bytes=62 << 20),
+    )(keys, values)
+
+
+def project(gradient, weight, first_block, blocks, width, keys=None, values=None, wide=0, skip=0):
     rows, depth = gradient.shape
+    out_specs = [pl.BlockSpec((rows, width), lambda i, off: (0, i))]
+    out_shape = [jax.ShapeDtypeStruct((rows, blocks * width), jnp.bfloat16)]
+    in_specs = [
+        pl.BlockSpec((rows, depth), lambda i, off: (0, 0)),
+        pl.BlockSpec((width, depth), lambda i, off: (off[0] + i, 0)),
+    ]
+    operands = [gradient, weight]
+    if keys is not None:
+        operands += [keys, values]
+        in_specs += [pl.BlockSpec((rows, wide), lambda i, off: (0, i // 2 + skip))] * 2
+        out_specs.append(pl.BlockSpec((rows, 2 * wide), lambda i, off: (0, i // 2)))
+        out_shape.append(jax.ShapeDtypeStruct((rows, blocks * wide), keys.dtype))
     return pl.pallas_call(
         project_body,
         grid_spec=pltpu.PrefetchScalarGridSpec(
-            num_scalar_prefetch=1,
-            grid=(blocks,),
-            in_specs=[
-                pl.BlockSpec((rows, depth), lambda i, off: (0, 0)),
-                pl.BlockSpec((width, depth), lambda i, off: (off[0] + i, 0)),
-            ],
-            out_specs=pl.BlockSpec((rows, width), lambda i, off: (0, i)),
-        ),
-        out_shape=jax.ShapeDtypeStruct((rows, blocks * width), dtype),
+            num_scalar_prefetch=1, grid=(blocks,), in_specs=in_specs, out_specs=out_specs
+        ),
+        out_shape=out_shape,
         cost_estimate=pl.CostEstimate(
             flops=2 * rows * depth * width * blocks,
             bytes_accessed=2 * (rows * depth + width * blocks * depth + rows * width * blocks),
             transcendentals=0,
         ),
         compiler_params=pltpu.CompilerParams(vmem_limit_bytes=GRANT),
-    )(first_block, gradient, weight)
-
-
-def open_body(each, offset_ref, gradient_ref, weight_ref, x_ref, norm_ref, down_ref, *rest):
-    k_ref, v_ref, out_ref, low_ref, *packs = rest
-    step = pl.program_id(0)
+    )(first_block, *operands)
+
+
+def open_body(offset_ref, gradient_ref, weight_ref, x_ref, norm_ref, down_ref, out_ref, low_ref):
     out_ref[...] = dotf(gradient_ref[...], weight_ref[...], NT).astype(out_ref.dtype)
     hidden = x_ref[...].astype(jnp.float32)
     weighted = (hidden * norm_ref[...].astype(jnp.float32)).astype(jnp.bfloat16)
     low_ref[0 : 3 * ADAPTER_RANK, :] = dotf(down_ref[...], weighted, NT)
     ones = jnp.ones((ADAPTER_RANK, hidden.shape[1]), jnp.bfloat16)
     low_ref[3 * ADAPTER_RANK :, :] = dotf(ones, (hidden * hidden).astype(jnp.bfloat16), NT)
-    wide = k_ref.shape[1]
-    for c, pack_ref in enumerate(packs):
-
-        @pl.when(step // each == c)
-        def _(pack_ref=pack_ref):
-            pack_ref[:, :wide] = k_ref[...]
-            pack_ref[:, wide:] = v_ref[...]
-
-
-def open_call(gradient, weight, first_block, blocks, width, x, norm, down, keys, values, chunks):
+
+
+def open_call(gradient, weight, first_block, blocks, width, x, norm, down):
     rows, depth = gradient.shape
     slab = rows // blocks
-    wide = keys.shape[1] // blocks
-    each = blocks // chunks
-    pack_specs = [
-        pl.BlockSpec((rows, 2 * wide), lambda i, off, c=c: (0, jnp.clip(i - c * each, 0, each - 1)))
-        for c in range(chunks)
-    ]
-    pack_shape = jax.ShapeDtypeStruct((rows, 2 * wide * each), keys.dtype)
     return pl.pallas_call(
-        functools.partial(open_body, each),
+        open_body,
         grid_spec=pltpu.PrefetchScalarGridSpec(
             num_scalar_prefetch=1,
             grid=(blocks,),
@@ -107,27 +122,23 @@
                 pl.BlockSpec((slab, depth), lambda i, off: (i, 0)),
                 pl.BlockSpec((1, depth), lambda i, off: (0, 0)),
                 pl.BlockSpec((3 * ADAPTER_RANK, depth), lambda i, off: (0, 0)),
-                pl.BlockSpec((rows, wide), lambda i, off: (0, i)),
-                pl.BlockSpec((rows, wide), lambda i, off: (0, i)),
             ],
             out_specs=[
                 pl.BlockSpec((rows, width), lambda i, off: (0, i)),
                 pl.BlockSpec((TABLE, slab), lambda i, off: (0, i)),
-            ]
-            + pack_specs,
+            ],
         ),
         out_shape=[
             jax.ShapeDtypeStruct((rows, blocks * width), jnp.bfloat16),
             jax.ShapeDtypeStruct((TABLE, rows), jnp.float32),
-        ]
-        + [pack_shape] * chunks,
+        ],
         cost_estimate=pl.CostEstimate(
             flops=2 * rows * depth * width * blocks,
             bytes_accessed=2 * (2 * rows * depth + width * blocks * depth + rows * width * blocks),
             transcendentals=0,
         ),
         compiler_params=pltpu.CompilerParams(vmem_limit_bytes=GRANT),
-    )(first_block, gradient, weight, x, norm, down, keys, values)
+    )(first_block, gradient, weight, x, norm, down)
 
 
 def table_body(mine_ref, theirs_ref, doc_ref, out_ref):
@@ -397,7 +408,7 @@
 def finish_body(*refs):
     q_ref, k_ref, v_ref = refs[-3:]
     mine = refs[0][...].astype(jnp.float32) + refs[1][...].astype(jnp.float32)
-    total = refs[2][0:1, 0:1]
+    total = refs[2][0:1, 0:1] + refs[3][0:1, 0:1]
     count = float(ADAPTER_RANK * (QUERY_HEADS + 2 * KEY_VALUE_HEADS) * HEAD_SIZE)
     mine = mine * jnp.sqrt(count / (total + 1e-06))
     for g in range(k_ref.shape[1] // LANES):
@@ -431,13 +442,15 @@
     per = half // chunks
     scalar = lambda value: jnp.asarray(value, jnp.int32).reshape(1)
 
+    packs = [pack_call(stored_keys, stored_values, units * LANES, steps)]
+
     received = []
     for c in range(chunks):
         got = []
         for d in range(1, tp):
             first = scalar(((tp_at + d) % tp) * half + c * per)
             if c == 0 and d == 1:
-                part, low, *packs = open_call(
+                part, low = open_call(
                     projection_gradient,
                     output_weight,
                     first,
@@ -446,12 +459,23 @@
                     layer_input,
                     norm_weight[None, :],
                     adapter_down_maps.T,
-                    stored_keys,
-                    stored_values,
-                    chunks,
                 )
             else:
-                part = project(projection_gradient, output_weight, first, per, width)
+                if d == 1:
+                    part, pack = project(
+                        projection_gradient,
+                        output_weight,
+                        first,
+                        per,
+                        width,
+                        stored_keys,
+                        stored_values,
+                        units * LANES,
+                        c * steps,
+                    )
+                    packs.append(pack)
+                else:
+                    (part,) = project(projection_gradient, output_weight, first, per, width)
             got.append(lax.ppermute(part, "tp", [(at, (at + d) % tp) for at in range(tp)]))
         total = got[0]
         if len(got) > 1:
@@ -493,19 +517,18 @@
     sums = None
     for c in range(chunks):
         far = shifted(packs[c], "ctx", 2)
-        picked = jnp.where(second, far, packs[c])
-        near = xor_move(picked, "ctx", 1)
+        if c == 0:
+            picked = jnp.where(second, far, packs[c])
+            near = xor_move(picked, "ctx", 1)
+        else:
+            near = shifted(packs[c], "ctx", 1)
         first = scalar((tp_at * half + c * per) // units)
-        own = None
-        if c < chunks - 1:
-            begin = scalar(tp_at * half + c * per)
-            own = project(projection_gradient, output_weight, begin, per, width, jnp.float32)
         sums = attend(
             stored_queries,
             projection_gradient,
             output_weight,
             received[c],
-            own,
+            None,
             (far, near, packs[c]),
             ext,
             table,
@@ -517,16 +540,24 @@
             sums,
         )
 
-    order = [1] + [1 << at for at in range(2, ctx.bit_length() - 1)]
-    for move in order:
-        sums = (sums.astype(jnp.float32) + xor_move(sums, "ctx", move).astype(jnp.float32)).astype(jnp.bfloat16)
-    last = [sums, xor_move(sums, "ctx", 2)]
-    squared = jnp.sum(jnp.square(last[0].astype(jnp.float32) + last[1].astype(jnp.float32))).reshape(1, 1)
+    def joined(*parts):
+        wide = [part.astype(jnp.float32) for part in parts]
+        total = wide[0] + wide[1]
+        return total if len(parts) == 2 else total + (wide[2] + wide[3])
+
+    sums = joined(sums, xor_move(sums, "ctx", 1)).astype(jnp.bfloat16)
+    sums = joined(sums, *[xor_move(sums, "ctx", move) for move in (2, 4, 6)]).astype(jnp.bfloat16)
+    move = 8
+    while 2 * move < ctx:
+        sums = joined(sums, xor_move(sums, "ctx", move)).astype(jnp.bfloat16)
+        move *= 2
+    last = [sums, xor_move(sums, "ctx", move)]
+    squared = jnp.sum(jnp.square(joined(*last))).reshape(1, 1)
     move = 1
-    while move < tp:
+    while 2 * move < tp:
         squared = squared + xor_move(squared, "tp", move)
         move *= 2
-    last.append(squared)
+    last += [squared, xor_move(squared, "tp", move)]
     sizes = (heads_width, groups * HEAD_SIZE, groups * HEAD_SIZE)
     return pl.pallas_call(
         finish_body,

time: 146 us -> 143 us (0.979)
  starting transfers between devices: 30.3 us -> 35.7 us
  other arithmetic: 5.79 us -> 1.81 us
  waiting for transfers between devices: 34.9 us -> 33.1 us
    ppermute x4 -> x5, waiting for transfers between devices: 23.9 us -> 12 us  [shifted(): lax.ppermute(value, axis, [(source, source + steps) for source in range(f...]
    ppermute x8, waiting for transfers between devices: 11.1 us -> 21.2 us  [xor_move(): lax.ppermute(value, axis, [(at, at ^ step) for at in range(lax.axis_size(...]
    pallas_call x2 -> x1, Pallas kernels: 14.1 us -> 7.99 us  [project(): pl.pallas_call(project_body, grid_spec=pltpu.PrefetchScalarGridSpec(num_s...]
    select_n x2 -> x1, other arithmetic: 5.1 us -> 1.12 us  [local(): picked = jnp.where(second, far, packs[c])]
    pallas_call x2, Pallas kernels: 45.5 us -> 49 us  [attend(): pl.pallas_call(functools.partial(attend_body, steps, units, base, alone),...]
    ppermute x4 -> x5, starting transfers between devices: 15.1 us -> 18.2 us  [shifted(): lax.ppermute(value, axis, [(source, source + steps) for source in range(f...]
    pallas_call x1 -> x2, Pallas kernels: 9.93 us -> 10.3 us  [the longest x1 8.11 us: open_call(): pl.pallas_call(open_body, grid_spec=pltpu.PrefetchScalarGridSpec(num_scal...]
  transfers between devices with their start and end apart: 14 -> 15, of which waited for: 7 -> 7; matrix products, arithmetic and copies ran while one was open for 4% -> 1% of each run, Pallas kernels for 24% -> 29%
where the time goes in v4:
time: 143 us; the launch traced here: 142 us
  Pallas kernels  69.7 us (49%)
  starting transfers between devices  35.7 us (25%)
  waiting for transfers between devices  33.1 us (23%)
  other arithmetic  1.81 us (1%)
    pallas_call x2, Pallas kernels, attend(): pl.pallas_call(functools.partial(attend_body, steps, units, base, alone),...  49 us
    ppermute x8, waiting for transfers between devices, xor_move(): lax.ppermute(value, axis, [(at, at ^ step) for at in range(lax.axis_size(...  21.2 us
    ppermute x5, starting transfers between devices, shifted(): lax.ppermute(value, axis, [(source, source + steps) for source in range(f...  18.2 us
    ppermute x8, starting transfers between devices, xor_move(): lax.ppermute(value, axis, [(at, at ^ step) for at in range(lax.axis_size(...  14.3 us
    ppermute x5, waiting for transfers between devices, shifted(): lax.ppermute(value, axis, [(source, source + steps) for source in range(f...  12 us
    pallas_call x1, Pallas kernels, open_call(): pl.pallas_call(open_body, grid_spec=pltpu.PrefetchScalarGridSpec(num_scal...  8.11 us
    pallas_call x1, Pallas kernels, project(): pl.pallas_call(project_body, grid_spec=pltpu.PrefetchScalarGridSpec(num_s...  7.99 us
    ppermute x2, starting transfers between devices, local(): lax.ppermute(part, 'tp', [(at, (at + d) % tp) for at in range(tp)])  3.18 us
  transfers between devices with their start and end apart: 15, of which 7 were waited for; matrix products, arithmetic and copies ran while one was open for 1% of the time, Pallas kernels for 29%

profile of v4, /device:TPU:0, one launch (start us, length us, event | category | flops | bytes accessed | tf_op | source)
XLA Modules:
  0.0 142.2 jit_solution(7976973525750371402)
XLA Ops:
  0.7 2.1 %shard_map.116.rest_5_.rest_8_ = bf16[512,1024]{1,0:T(8,128)(2,1)} custom-call(bf16[512,1024]{1,0:T(8,128)(2,1)} %k_ref.1, bf16[512,1024]{1,0:T(8,128)(2,1)} %v_ref.1), custom_call_target="tpu_custom_call" | custom-call | tf_op jit(solution)/shard_map/pallas_call | solution.py:63
  2.8 5.9 %collective-permute-start.7 = (bf16[512,1024]{1,0:T(8,128)(2,1)}, bf16[512,1024]{1,0:T(8,128)(2,1)}, u32[]{:S(2)}, u32[]{:S(2)}) collective-permute-start(bf16[512,1024]{1,0:T(8,128)(2,1)} %shard_map.116.rest_5_.rest_8_), channel_id=1, source_target_pairs={{0,4},{2,6},{4,8},{6,10},{8,12},{10,14},{12,16},{14,18},{16,20},{1... | collective-permute-start | bytes 3145736 | tf_op jit(solution)/shard_map/ppermute | solution.py:37
  8.7 8.1 %shard_map.113 = (bf16[512,1024]{1,0:T(8,128)(2,1)S(1)}, f32[32,512]{1,0:T(8,128)S(1)}) custom-call(s32[1]{0:T(128)} %bitcast.3.offset_ref, bf16[512,2688]{1,0:T(8,128)(2,1)} %rest_0_.5, bf16[4096,2688]{1,0:T(8,128)(2,1)} %rest_1_.5, bf16[512,2688]{1,0:T(8,128)(2,1)} %x_ref.1, bf16[1,2688]{1,0:T(2,128)(2,1)S(1)} %broadcast_in_dim.6.norm_ref, ...), custom_call_target="tpu_custom_call" | custom-call | flops 2818572288 | bytes 12058624 | tf_op jit(solution)/shard_map/pallas_call | solution.py:114
  16.8 1.6 %collective-permute-start.6 = (bf16[512,1024]{1,0:T(8,128)(2,1)S(1)}, bf16[512,1024]{1,0:T(8,128)(2,1)S(1)}, u32[]{:S(2)}, u32[]{:S(2)}) collective-permute-start(bf16[512,1024]{1,0:T(8,128)(2,1)S(1)} %get-tuple-element.14), channel_id=1, source_target_pairs={{0,1},{1,0},{2,3},{3,2},{4,5},{5,4},{6,7},{7,6},{8,9},{9,8},{10,11... | collective-permute-start | bytes 3145736 | tf_op jit(solution)/shard_map/ppermute | solution.py:479
  18.4 12.0 %collective-permute-done.7.rest_3_.rest_6_ = bf16[512,1024]{1,0:T(8,128)(2,1)} collective-permute-done((bf16[512,1024]{1,0:T(8,128)(2,1)}, bf16[512,1024]{1,0:T(8,128)(2,1)}, u32[]{:S(2)}, u32[]{:S(2)}) %collective-permute-start.7) | collective-permute-done | bytes 1048608 | tf_op jit(solution)/shard_map/ppermute | solution.py:37
  31.7 1.5 %collective-permute-start.3 = (f32[32,512]{1,0:T(8,128)S(1)}, f32[32,512]{1,0:T(8,128)S(1)}, u32[]{:S(2)}, u32[]{:S(2)}) collective-permute-start(f32[32,512]{1,0:T(8,128)S(1)} %get-tuple-element.11.mine_ref), channel_id=1, source_target_pairs={{0,1},{1,0},{2,3},{3,2},{4,5},{5,4},{6,7},{7,6},{8,9},{9,8},{10,11... | collective-permute-start | bytes 196616 | tf_op jit(solution)/shard_map/ppermute | solution.py:41
  33.2 9.7 %collective-permute-done.3.theirs_ref = f32[32,512]{1,0:T(8,128)S(1)} collective-permute-done((f32[32,512]{1,0:T(8,128)S(1)}, f32[32,512]{1,0:T(8,128)S(1)}, u32[]{:S(2)}, u32[]{:S(2)}) %collective-permute-start.3) | collective-permute-done | bytes 65568 | tf_op jit(solution)/shard_map/ppermute | solution.py:41
  42.9 2.5 %collective-permute-start.4 = (bf16[32,512]{1,0:T(8,128)(2,1)S(1)}, bf16[32,512]{1,0:T(8,128)(2,1)S(1)}, u32[]{:S(2)}, u32[]{:S(2)}) collective-permute-start(bf16[32,512]{1,0:T(8,128)(2,1)S(1)} %shard_map.114.t0_ref.rest_10_), channel_id=1, source_target_pairs={{0,4},{2,6},{4,8},{6,10},{8,12},{10,14},{12,16},{14,18},{16,20},{1... | collective-permute-start | bytes 98312 | tf_op jit(solution)/shard_map/ppermute | solution.py:37
  46.7 8.0 %shard_map.112 = (bf16[512,1024]{1,0:T(8,128)(2,1)S(1)}, bf16[512,1024]{1,0:T(8,128)(2,1)}) custom-call(s32[1]{0:T(128)} %bitcast.1.offset_ref, bf16[512,2688]{1,0:T(8,128)(2,1)} %rest_0_.5, bf16[4096,2688]{1,0:T(8,128)(2,1)} %rest_1_.5, bf16[512,1024]{1,0:T(8,128)(2,1)} %k_ref.1, bf16[512,1024]{1,0:T(8,128)(2,1)} %v_ref.1), custom_call_target="tpu_custom_call" | custom-call | flops 2818572288 | bytes 9306112 | tf_op jit(solution)/shard_map/pallas_call | solution.py:87
  54.7 5.0 %collective-permute-start.1 = (bf16[512,1024]{1,0:T(8,128)(2,1)}, bf16[512,1024]{1,0:T(8,128)(2,1)}, u32[]{:S(2)}, u32[]{:S(2)}) collective-permute-start(bf16[512,1024]{1,0:T(8,128)(2,1)} %get-tuple-element.10.rest_5_.rest_8_), channel_id=1, source_target_pairs={{0,4},{2,6},{4,8},{6,10},{8,12},{10,14},{12,16},{14,18},{16,20},{1... | collective-permute-start | bytes 3145736 | tf_op jit(solution)/shard_map/ppermute | solution.py:37
  59.7 3.5 %collective-permute-start.2 = (bf16[512,1024]{1,0:T(8,128)(2,1)}, bf16[512,1024]{1,0:T(8,128)(2,1)S(1)}, u32[]{:S(2)}, u32[]{:S(2)}) collective-permute-start(bf16[512,1024]{1,0:T(8,128)(2,1)} %get-tuple-element.10.rest_5_.rest_8_), channel_id=1, source_target_pairs={{0,2},{2,4},{4,6},{6,8},{8,10},{10,12},{12,14},{14,16},{16,18},{18... | collective-permute-start | bytes 3145736 | tf_op jit(solution)/shard_map/ppermute | solution.py:37
  63.3 1.6 %collective-permute-start = (bf16[512,1024]{1,0:T(8,128)(2,1)S(1)}, bf16[512,1024]{1,0:T(8,128)(2,1)S(1)}, u32[]{:S(2)}, u32[]{:S(2)}) collective-permute-start(bf16[512,1024]{1,0:T(8,128)(2,1)S(1)} %get-tuple-element.9), channel_id=1, source_target_pairs={{0,1},{1,0},{2,3},{3,2},{4,5},{5,4},{6,7},{7,6},{8,9},{9,8},{10,11... | collective-permute-start | bytes 3145736 | tf_op jit(solution)/shard_map/ppermute | solution.py:479
  65.4 24.6 %shard_map.117.rest_12_ = bf16[8,2048]{1,0:T(8,128)(2,1)S(1)} custom-call(s32[1]{0:T(128)} %bitcast.6.offset_ref, bf16[512,2048]{1,0:T(8,128)(2,1)} %q_ref.3, bf16[512,2688]{1,0:T(8,128)(2,1)} %rest_0_.5, bf16[4096,2688]{1,0:T(8,128)(2,1)} %rest_1_.5, bf16[512,1024]{1,0:T(8,128)(2,1)S(1)} %collective-permute-done.6.rest_2_, ...), custom_call_target="tpu_custom_call" | custom-call | flops 13555990528 | bytes 10747904 | tf_op jit(solution)/shard_map/pallas_call | solution.py:377
  91.1 24.4 %shard_map.118 = bf16[8,4096]{1,0:T(8,128)(2,1)S(1)} custom-call(s32[1]{0:T(128)} %bitcast.offset_ref, bf16[512,2048]{1,0:T(8,128)(2,1)} %q_ref.3, bf16[512,2688]{1,0:T(8,128)(2,1)} %rest_0_.5, bf16[4096,2688]{1,0:T(8,128)(2,1)} %rest_1_.5, bf16[512,1024]{1,0:T(8,128)(2,1)S(1)} %collective-permute-done.rest_2_, ...), custom_call_target="tpu_custom_call" | custom-call | flops 13555990528 | bytes 10747904 | tf_op jit(solution)/shard_map/pallas_call | solution.py:377
  115.5 3.9 %collective-permute-start.9 = (bf16[8,4096]{1,0:T(8,128)(2,1)S(1)}, bf16[8,4096]{1,0:T(8,128)(2,1)S(1)}, u32[]{:S(2)}, u32[]{:S(2)}) collective-permute-start(bf16[8,4096]{1,0:T(8,128)(2,1)S(1)} %shard_map.118), channel_id=1, source_target_pairs={{0,2},{2,0},{4,6},{6,4},{8,10},{10,8},{12,14},{14,12},{16,18},{18,... | collective-permute-start | bytes 196616 | tf_op jit(solution)/shard_map/ppermute | solution.py:41
  120.3 2.7 %collective-permute-start.10 = (bf16[8,4096]{1,0:T(8,128)(2,1)S(1)}, bf16[8,4096]{1,0:T(8,128)(2,1)S(1)}, u32[]{:S(2)}, u32[]{:S(2)}) collective-permute-start(bf16[8,4096]{1,0:T(8,128)(2,1)S(1)} %add_convert_fusion.1), channel_id=1, source_target_pairs={{0,4},{2,6},{4,0},{6,2},{8,12},{10,14},{12,8},{14,10},{16,20},{18,... | collective-permute-start | bytes 196616 | tf_op jit(solution)/shard_map/ppermute | solution.py:41
  123.0 1.6 %collective-permute-start.11 = (bf16[8,4096]{1,0:T(8,128)(2,1)S(1)}, bf16[8,4096]{1,0:T(8,128)(2,1)S(1)}, u32[]{:S(2)}, u32[]{:S(2)}) collective-permute-start(bf16[8,4096]{1,0:T(8,128)(2,1)S(1)} %add_convert_fusion.1), channel_id=1, source_target_pairs={{0,8},{2,10},{4,12},{6,14},{8,0},{10,2},{12,4},{14,6},{16,24},{18,... | collective-permute-start | bytes 196616 | tf_op jit(solution)/shard_map/ppermute | solution.py:41
  125.5 1.8 %collective-permute-done.11 = bf16[8,4096]{1,0:T(8,128)(2,1)S(1)} collective-permute-done((bf16[8,4096]{1,0:T(8,128)(2,1)S(1)}, bf16[8,4096]{1,0:T(8,128)(2,1)S(1)}, u32[]{:S(2)}, u32[]{:S(2)}) %collective-permute-start.11) | collective-permute-done | bytes 65568 | tf_op jit(solution)/shard_map/ppermute | solution.py:41
  127.3 2.5 %collective-permute-done.12 = bf16[8,4096]{1,0:T(8,128)(2,1)S(1)} collective-permute-done((bf16[8,4096]{1,0:T(8,128)(2,1)S(1)}, bf16[8,4096]{1,0:T(8,128)(2,1)S(1)}, u32[]{:S(2)}, u32[]{:S(2)}) %collective-permute-start.12) | collective-permute-done | bytes 65568 | tf_op jit(solution)/shard_map/ppermute | solution.py:41
  129.8 2.1 %collective-permute-start.13 = (bf16[8,4096]{1,0:T(8,128)(2,1)S(1)}, bf16[8,4096]{1,0:T(8,128)(2,1)S(1)}, u32[]{:S(2)}, u32[]{:S(2)}) collective-permute-start(bf16[8,4096]{1,0:T(8,128)(2,1)S(1)} %add_convert_fusion.refs_0_), channel_id=1, source_target_pairs={{0,16},{2,18},{4,20},{6,22},{8,24},{10,26},{12,28},{14,30},{16,0},... | collective-permute-start | bytes 196616 | tf_op jit(solution)/shard_map/ppermute | solution.py:41
  131.9 3.9 %collective-permute-done.13.refs_1_ = bf16[8,4096]{1,0:T(8,128)(2,1)S(1)} collective-permute-done((bf16[8,4096]{1,0:T(8,128)(2,1)S(1)}, bf16[8,4096]{1,0:T(8,128)(2,1)S(1)}, u32[]{:S(2)}, u32[]{:S(2)}) %collective-permute-start.13) | collective-permute-done | bytes 65568 | tf_op jit(solution)/shard_map/ppermute | solution.py:41
  136.4 1.5 %collective-permute-start.14 = (f32[1,1]{1,0:T(1,128)}, f32[1,1]{1,0:T(1,128)}, u32[]{:S(2)}, u32[]{:S(2)}) collective-permute-start(f32[1,1]{1,0:T(1,128)} %bitcast.7.refs_2_), channel_id=1, source_target_pairs={{0,1},{1,0},{2,3},{3,2},{4,5},{5,4},{6,7},{7,6},{8,9},{9,8},{10,11... | collective-permute-start | bytes 20 | tf_op jit(solution)/shard_map/ppermute | solution.py:41
  137.9 2.4 %collective-permute-done.14.refs_3_ = f32[1,1]{1,0:T(1,128)} collective-permute-done((f32[1,1]{1,0:T(1,128)}, f32[1,1]{1,0:T(1,128)}, u32[]{:S(2)}, u32[]{:S(2)}) %collective-permute-start.14) | collective-permute-done | bytes 36 | tf_op jit(solution)/shard_map/ppermute | solution.py:41
  140.3 1.9 %shard_map.119 = (f32[8,2048]{1,0:T(8,128)}, f32[8,1024]{1,0:T(8,128)}, f32[8,1024]{1,0:T(8,128)}) custom-call(bf16[8,4096]{1,0:T(8,128)(2,1)S(1)} %add_convert_fusion.refs_0_, bf16[8,4096]{1,0:T(8,128)(2,1)S(1)} %collective-permute-done.13.refs_1_, f32[1,1]{1,0:T(1,128)} %bitcast.7.refs_2_, f32[1,1]{1,0:T(1,128)} %collective-permute-done.14.refs_3_), custom_call_target="tpu_custom_call" | custom-call | tf_op jit(solution)/shard_map/pallas_call | solution.py:562
  (29 shorter events, 6.6 us)
Async XLA Ops:
  0.6 8.0 %copy-start.3 = (bf16[2688]{0:T(1024)(128)(2,1)S(1)}, bf16[2688]{0:T(1024)(128)(2,1)}, u32[]{:S(2)}) copy-start(bf16[2688]{0:T(1024)(128)(2,1)} %param.10) | copy-start | bytes 16132
  0.6 8.0 %copy-start = (bf16[2688,24]{0,1:T(8,128)(2,1)S(1)}, bf16[2688,24]{0,1:T(8,128)(2,1)}, u32[]{:S(2)}) copy-start(bf16[2688,24]{0,1:T(8,128)(2,1)} %param.17) | copy-start | bytes 387076
  2.8 27.6 %collective-permute-start.7 = (bf16[512,1024]{1,0:T(8,128)(2,1)}, bf16[512,1024]{1,0:T(8,128)(2,1)}, u32[]{:S(2)}, u32[]{:S(2)}) collective-permute-start(bf16[512,1024]{1,0:T(8,128)(2,1)} %shard_map.116.rest_5_.rest_8_), channel_id=1, source_target_pairs={{0,4},{2,6},{4,8},{6,10},{8,12},{10,14},{12,16},{14,18},{16,20},{1... | collective-permute-start | bytes 3145736 | tf_op jit(solution)/shard_map/ppermute | solution.py:37
  8.7 21.7 %copy-start.2 = (bf16[512,1024]{1,0:T(8,128)(2,1)S(1)}, bf16[512,1024]{1,0:T(8,128)(2,1)}, u32[]{:S(2)}) copy-start(bf16[512,1024]{1,0:T(8,128)(2,1)} %shard_map.116.rest_5_.rest_8_) | copy-start | bytes 3145732
  16.8 26.1 %copy-start.1 = (s32[512]{0:T(512)S(1)}, s32[512]{0:T(512)}, u32[]{:S(2)}) copy-start(s32[512]{0:T(512)} %param.11) | copy-start | bytes 6148
  16.8 48.6 %collective-permute-start.6 = (bf16[512,1024]{1,0:T(8,128)(2,1)S(1)}, bf16[512,1024]{1,0:T(8,128)(2,1)S(1)}, u32[]{:S(2)}, u32[]{:S(2)}) collective-permute-start(bf16[512,1024]{1,0:T(8,128)(2,1)S(1)} %get-tuple-element.14), channel_id=1, source_target_pairs={{0,1},{1,0},{2,3},{3,2},{4,5},{5,4},{6,7},{7,6},{8,9},{9,8},{10,11... | collective-permute-start | bytes 3145736 | tf_op jit(solution)/shard_map/ppermute | solution.py:479
  31.5 33.9 %collective-permute-start.8 = (bf16[512,1024]{1,0:T(8,128)(2,1)}, bf16[512,1024]{1,0:T(8,128)(2,1)}, u32[]{:S(2)}, u32[]{:S(2)}) collective-permute-start(bf16[512,1024]{1,0:T(8,128)(2,1)} %broadcast_select_fusion), channel_id=1, source_target_pairs={{0,2},{2,0},{4,6},{6,4},{8,10},{10,8},{12,14},{14,12},{16,18},{18,... | collective-permute-start | bytes 3145736 | tf_op jit(solution)/shard_map/ppermute | solution.py:41
  31.7 11.2 %collective-permute-start.3 = (f32[32,512]{1,0:T(8,128)S(1)}, f32[32,512]{1,0:T(8,128)S(1)}, u32[]{:S(2)}, u32[]{:S(2)}) collective-permute-start(f32[32,512]{1,0:T(8,128)S(1)} %get-tuple-element.11.mine_ref), channel_id=1, source_target_pairs={{0,1},{1,0},{2,3},{3,2},{4,5},{5,4},{6,7},{7,6},{8,9},{9,8},{10,11... | collective-permute-start | bytes 196616 | tf_op jit(solution)/shard_map/ppermute | solution.py:41
  42.9 16.8 %collective-permute-start.4 = (bf16[32,512]{1,0:T(8,128)(2,1)S(1)}, bf16[32,512]{1,0:T(8,128)(2,1)S(1)}, u32[]{:S(2)}, u32[]{:S(2)}) collective-permute-start(bf16[32,512]{1,0:T(8,128)(2,1)S(1)} %shard_map.114.t0_ref.rest_10_), channel_id=1, source_target_pairs={{0,4},{2,6},{4,8},{6,10},{8,12},{10,14},{12,16},{14,18},{16,20},{1... | collective-permute-start | bytes 98312 | tf_op jit(solution)/shard_map/ppermute | solution.py:37
  45.4 17.8 %collective-permute-start.5 = (bf16[32,512]{1,0:T(8,128)(2,1)S(1)}, bf16[32,512]{1,0:T(8,128)(2,1)S(1)}, u32[]{:S(2)}, u32[]{:S(2)}) collective-permute-start(bf16[32,512]{1,0:T(8,128)(2,1)S(1)} %shard_map.114.t0_ref.rest_10_), channel_id=1, source_target_pairs={{0,2},{2,4},{4,6},{6,8},{8,10},{10,12},{12,14},{14,16},{16,18},{18... | collective-permute-start | bytes 98312 | tf_op jit(solution)/shard_map/ppermute | solution.py:37
  54.7 35.3 %collective-permute-start.1 = (bf16[512,1024]{1,0:T(8,128)(2,1)}, bf16[512,1024]{1,0:T(8,128)(2,1)}, u32[]{:S(2)}, u32[]{:S(2)}) collective-permute-start(bf16[512,1024]{1,0:T(8,128)(2,1)} %get-tuple-element.10.rest_5_.rest_8_), channel_id=1, source_target_pairs={{0,4},{2,6},{4,8},{6,10},{8,12},{10,14},{12,16},{14,18},{16,20},{1... | collective-permute-start | bytes 3145736 | tf_op jit(solution)/shard_map/ppermute | solution.py:37
  59.7 30.3 %collective-permute-start.2 = (bf16[512,1024]{1,0:T(8,128)(2,1)}, bf16[512,1024]{1,0:T(8,128)(2,1)S(1)}, u32[]{:S(2)}, u32[]{:S(2)}) collective-permute-start(bf16[512,1024]{1,0:T(8,128)(2,1)} %get-tuple-element.10.rest_5_.rest_8_), channel_id=1, source_target_pairs={{0,2},{2,4},{4,6},{6,8},{8,10},{10,12},{12,14},{14,16},{16,18},{18... | collective-permute-start | bytes 3145736 | tf_op jit(solution)/shard_map/ppermute | solution.py:37
  63.3 26.8 %collective-permute-start = (bf16[512,1024]{1,0:T(8,128)(2,1)S(1)}, bf16[512,1024]{1,0:T(8,128)(2,1)S(1)}, u32[]{:S(2)}, u32[]{:S(2)}) collective-permute-start(bf16[512,1024]{1,0:T(8,128)(2,1)S(1)} %get-tuple-element.9), channel_id=1, source_target_pairs={{0,1},{1,0},{2,3},{3,2},{4,5},{5,4},{6,7},{7,6},{8,9},{9,8},{10,11... | collective-permute-start | bytes 3145736 | tf_op jit(solution)/shard_map/ppermute | solution.py:479
  90.1 1.0 copy-start.4
  115.5 4.8 %collective-permute-start.9 = (bf16[8,4096]{1,0:T(8,128)(2,1)S(1)}, bf16[8,4096]{1,0:T(8,128)(2,1)S(1)}, u32[]{:S(2)}, u32[]{:S(2)}) collective-permute-start(bf16[8,4096]{1,0:T(8,128)(2,1)S(1)} %shard_map.118), channel_id=1, source_target_pairs={{0,2},{2,0},{4,6},{6,4},{8,10},{10,8},{12,14},{14,12},{16,18},{18,... | collective-permute-start | bytes 196616 | tf_op jit(solution)/shard_map/ppermute | solution.py:41
  120.3 5.1 %collective-permute-start.10 = (bf16[8,4096]{1,0:T(8,128)(2,1)S(1)}, bf16[8,4096]{1,0:T(8,128)(2,1)S(1)}, u32[]{:S(2)}, u32[]{:S(2)}) collective-permute-start(bf16[8,4096]{1,0:T(8,128)(2,1)S(1)} %add_convert_fusion.1), channel_id=1, source_target_pairs={{0,4},{2,6},{4,0},{6,2},{8,12},{10,14},{12,8},{14,10},{16,20},{18,... | collective-permute-start | bytes 196616 | tf_op jit(solution)/shard_map/ppermute | solution.py:41
  123.0 4.3 %collective-permute-start.11 = (bf16[8,4096]{1,0:T(8,128)(2,1)S(1)}, bf16[8,4096]{1,0:T(8,128)(2,1)S(1)}, u32[]{:S(2)}, u32[]{:S(2)}) collective-permute-start(bf16[8,4096]{1,0:T(8,128)(2,1)S(1)} %add_convert_fusion.1), channel_id=1, source_target_pairs={{0,8},{2,10},{4,12},{6,14},{8,0},{10,2},{12,4},{14,6},{16,24},{18,... | collective-permute-start | bytes 196616 | tf_op jit(solution)/shard_map/ppermute | solution.py:41
  124.6 5.2 %collective-permute-start.12 = (bf16[8,4096]{1,0:T(8,128)(2,1)S(1)}, bf16[8,4096]{1,0:T(8,128)(2,1)S(1)}, u32[]{:S(2)}, u32[]{:S(2)}) collective-permute-start(bf16[8,4096]{1,0:T(8,128)(2,1)S(1)} %add_convert_fusion.1), channel_id=1, source_target_pairs={{0,12},{2,14},{4,8},{6,10},{8,4},{10,6},{12,0},{14,2},{16,28},{18,... | collective-permute-start | bytes 196616 | tf_op jit(solution)/shard_map/ppermute | solution.py:41
  129.8 5.9 %collective-permute-start.13 = (bf16[8,4096]{1,0:T(8,128)(2,1)S(1)}, bf16[8,4096]{1,0:T(8,128)(2,1)S(1)}, u32[]{:S(2)}, u32[]{:S(2)}) collective-permute-start(bf16[8,4096]{1,0:T(8,128)(2,1)S(1)} %add_convert_fusion.refs_0_), channel_id=1, source_target_pairs={{0,16},{2,18},{4,20},{6,22},{8,24},{10,26},{12,28},{14,30},{16,0},... | collective-permute-start | bytes 196616 | tf_op jit(solution)/shard_map/ppermute | solution.py:41
  136.4 3.9 %collective-permute-start.14 = (f32[1,1]{1,0:T(1,128)}, f32[1,1]{1,0:T(1,128)}, u32[]{:S(2)}, u32[]{:S(2)}) collective-permute-start(f32[1,1]{1,0:T(1,128)} %bitcast.7.refs_2_), channel_id=1, source_target_pairs={{0,1},{1,0},{2,3},{3,2},{4,5},{5,4},{6,7},{7,6},{8,9},{9,8},{10,11... | collective-permute-start | bytes 20 | tf_op jit(solution)/shard_map/ppermute | solution.py:41

commit v5 on v4

--- a/solution.py
+++ b/solution.py
@@ -52,19 +52,19 @@
     out_ref[...] = dotf(gradient_ref[...], weight_ref[...], NT).astype(out_ref.dtype)
 
 
-def pack_body(k_ref, v_ref, out_ref):
-    wide = k_ref.shape[1]
-    out_ref[:, :wide] = k_ref[...]
-    out_ref[:, wide:] = v_ref[...]
+def pack_body(wide, k_ref, v_ref, out_ref):
+    for at in range(0, k_ref.shape[1], wide):
+        out_ref[:, 2 * at : 2 * at + wide] = k_ref[:, at : at + wide]
+        out_ref[:, 2 * at + wide : 2 * at + 2 * wide] = v_ref[:, at : at + wide]
 
 
 def pack_call(keys, values, wide, blocks):
     rows = keys.shape[0]
     return pl.pallas_call(
-        pack_body,
-        grid=(blocks,),
-        in_specs=[pl.BlockSpec((rows, wide), lambda i: (0, i))] * 2,
-        out_specs=pl.BlockSpec((rows, 2 * wide), lambda i: (0, i)),
+        functools.partial(pack_body, wide),
+        grid=(1,),
+        in_specs=[pl.BlockSpec((rows, wide * blocks), lambda i: (0, 0))] * 2,
+        out_specs=pl.BlockSpec((rows, 2 * wide * blocks), lambda i: (0, 0)),
         out_shape=jax.ShapeDtypeStruct((rows, 2 * wide * blocks), keys.dtype),
         compiler_params=pltpu.CompilerParams(vmem_limit_bytes=62 << 20),
     )(keys, values)
@@ -103,9 +103,10 @@
     out_ref[...] = dotf(gradient_ref[...], weight_ref[...], NT).astype(out_ref.dtype)
     hidden = x_ref[...].astype(jnp.float32)
     weighted = (hidden * norm_ref[...].astype(jnp.float32)).astype(jnp.bfloat16)
-    low_ref[0 : 3 * ADAPTER_RANK, :] = dotf(down_ref[...], weighted, NT)
-    ones = jnp.ones((ADAPTER_RANK, hidden.shape[1]), jnp.bfloat16)
-    low_ref[3 * ADAPTER_RANK :, :] = dotf(ones, (hidden * hidden).astype(jnp.bfloat16), NT)
+    reduced = dotf(weighted, down_ref[...], NT)
+    squares = jnp.sum(hidden * hidden, axis=1, keepdims=True)
+    squares = jnp.broadcast_to(squares, (squares.shape[0], LANES - 3 * ADAPTER_RANK))
+    low_ref[...] = jnp.concatenate([reduced, squares], 1).T[:TABLE]
 
 
 def open_call(gradient, weight, first_block, blocks, width, x, norm, down):
@@ -279,7 +280,7 @@
         s["delta"] = (
             jnp.sum(s["do"].astype(jnp.float32) * acc[:, :LANES], axis=1, keepdims=True) * s["inverse"]
         )
-        s["uv"] = (acc[:, LANES:] * s["inverse"]).astype(jnp.bfloat16)
+        s["uv"] = (acc[:, LANES : LANES + ROW_ONE] * s["inverse"]).astype(jnp.bfloat16)
 
     def back(i, j):
         g, t = units[i]
@@ -297,7 +298,7 @@
         fin = (s["back"] * (s["inverse"] * SCALE)).astype(jnp.bfloat16)
         dq = jnp.concatenate([fin[:tile, :LANES], fin[tile:, :LANES]], 1)
         low_q = lq_ref[2 * ADAPTER_RANK :, t * tile : (t + 1) * tile]
-        out = (dotf(low_q, dq, NN), dotf(fin[:, LANES:], s["q"], TN), dotf(s["uv"], s["do"], TN))
+        out = (dotf(low_q, dq, NN), dotf(fin[:, LANES : LANES + ROW_ONE], s["q"], TN), dotf(s["uv"], s["do"], TN))
         if t > 0:
             out = tuple(a + b for a, b in zip(out, state[i - 1]["out"]))
             state[i - 1].clear()
@@ -405,10 +406,15 @@
     )(first, *operands)
 
 
+def square_body(mine_ref, theirs_ref, out_ref):
+    mine = mine_ref[...].astype(jnp.float32) + theirs_ref[...].astype(jnp.float32)
+    out_ref[...] = sum(jnp.square(mine[:, at : at + LANES]) for at in range(0, mine.shape[1], LANES))
+
+
 def finish_body(*refs):
     q_ref, k_ref, v_ref = refs[-3:]
     mine = refs[0][...].astype(jnp.float32) + refs[1][...].astype(jnp.float32)
-    total = refs[2][0:1, 0:1] + refs[3][0:1, 0:1]
+    total = jnp.sum(refs[2][...] + refs[3][...], keepdims=True)
     count = float(ADAPTER_RANK * (QUERY_HEADS + 2 * KEY_VALUE_HEADS) * HEAD_SIZE)
     mine = mine * jnp.sqrt(count / (total + 1e-06))
     for g in range(k_ref.shape[1] // LANES):
@@ -552,7 +558,9 @@
         sums = joined(sums, xor_move(sums, "ctx", move)).astype(jnp.bfloat16)
         move *= 2
     last = [sums, xor_move(sums, "ctx", move)]
-    squared = jnp.sum(jnp.square(joined(*last))).reshape(1, 1)
+    squared = pl.pallas_call(
+        square_body, out_shape=jax.ShapeDtypeStruct((ADAPTER_RANK, LANES), jnp.float32), compiler_params=SMALL
+    )(*last)
     move = 1
     while 2 * move < tp:
         squared = squared + xor_move(squared, "tp", move)

time: 143 us -> 141 us (0.986)
    ppermute x8, waiting for transfers between devices: 21.2 us -> 19.4 us  [xor_move(): lax.ppermute(value, axis, [(at, at ^ step) for at in range(lax.axis_size(...]
  transfers between devices with their start and end apart: 15 -> 15, of which waited for: 7 -> 7; matrix products, arithmetic and copies ran while one was open for 1% -> 2% of each run, Pallas kernels for 29% -> 29%
where the time goes in v5:
time: 141 us
  Pallas kernels  68.5 us (49%)
  starting transfers between devices  35.5 us (25%)
  waiting for transfers between devices  31.8 us (23%)
  other arithmetic  2.36 us (2%)
  local copies, waits for them, and re-layouts  1.99 us (1%)
    pallas_call x2, Pallas kernels, attend(): pl.pallas_call(functools.partial(attend_body, steps, units, base, alone),...  49.2 us
    ppermute x8, waiting for transfers between devices, xor_move(): lax.ppermute(value, axis, [(at, at ^ step) for at in range(lax.axis_size(...  19.4 us
    ppermute x5, starting transfers between devices, shifted(): lax.ppermute(value, axis, [(source, source + steps) for source in range(f...  18.1 us
    ppermute x8, starting transfers between devices, xor_move(): lax.ppermute(value, axis, [(at, at ^ step) for at in range(lax.axis_size(...  14.2 us
    ppermute x5, waiting for transfers between devices, shifted(): lax.ppermute(value, axis, [(source, source + steps) for source in range(f...  12.5 us
    pallas_call x1, Pallas kernels, project(): pl.pallas_call(project_body, grid_spec=pltpu.PrefetchScalarGridSpec(num_s...  7.98 us
    pallas_call x1, Pallas kernels, open_call(): pl.pallas_call(open_body, grid_spec=pltpu.PrefetchScalarGridSpec(num_scal...  7.63 us
    ppermute x2, starting transfers between devices, local(): lax.ppermute(part, 'tp', [(at, (at + d) % tp) for at in range(tp)])  3.18 us
  transfers between devices with their start and end apart: 15, of which 7 were waited for; matrix products, arithmetic and copies ran while one was open for 2% of the time, Pallas kernels for 29%

profile of v5, /device:TPU:0, one launch (start us, length us, event | category | flops | bytes accessed | tf_op | source)
XLA Modules:
  0.0 141.0 jit_solution(13770000223790903415)
XLA Ops:
  0.7 2.4 %shard_map.116.rest_5_.rest_8_ = bf16[512,1024]{1,0:T(8,128)(2,1)} custom-call(bf16[512,1024]{1,0:T(8,128)(2,1)} %k_ref.1, bf16[512,1024]{1,0:T(8,128)(2,1)} %v_ref.1), custom_call_target="tpu_custom_call" | custom-call | tf_op jit(solution)/shard_map/pallas_call | solution.py:63
  3.0 5.8 %collective-permute-start.7 = (bf16[512,1024]{1,0:T(8,128)(2,1)}, bf16[512,1024]{1,0:T(8,128)(2,1)}, u32[]{:S(2)}, u32[]{:S(2)}) collective-permute-start(bf16[512,1024]{1,0:T(8,128)(2,1)} %shard_map.116.rest_5_.rest_8_), channel_id=1, source_target_pairs={{0,4},{2,6},{4,8},{6,10},{8,12},{10,14},{12,16},{14,18},{16,20},{1... | collective-permute-start | bytes 3145736 | tf_op jit(solution)/shard_map/ppermute | solution.py:37
  8.9 7.6 %shard_map.113 = (bf16[512,1024]{1,0:T(8,128)(2,1)S(1)}, f32[32,512]{1,0:T(8,128)S(1)}) custom-call(s32[1]{0:T(128)} %bitcast.3.offset_ref, bf16[512,2688]{1,0:T(8,128)(2,1)} %rest_0_.5, bf16[4096,2688]{1,0:T(8,128)(2,1)} %rest_1_.5, bf16[512,2688]{1,0:T(8,128)(2,1)} %x_ref.1, bf16[1,2688]{1,0:T(2,128)(2,1)S(1)} %broadcast_in_dim.6.norm_ref, ...), custom_call_target="tpu_custom_call" | custom-call | flops 2818572288 | bytes 12058624 | tf_op jit(solution)/shard_map/pallas_call | solution.py:115
  16.5 1.6 %collective-permute-start.6 = (bf16[512,1024]{1,0:T(8,128)(2,1)S(1)}, bf16[512,1024]{1,0:T(8,128)(2,1)S(1)}, u32[]{:S(2)}, u32[]{:S(2)}) collective-permute-start(bf16[512,1024]{1,0:T(8,128)(2,1)S(1)} %get-tuple-element.14), channel_id=1, source_target_pairs={{0,1},{1,0},{2,3},{3,2},{4,5},{5,4},{6,7},{7,6},{8,9},{9,8},{10,11... | collective-permute-start | bytes 3145736 | tf_op jit(solution)/shard_map/ppermute | solution.py:485
  18.1 12.4 %collective-permute-done.7.rest_3_.rest_6_ = bf16[512,1024]{1,0:T(8,128)(2,1)} collective-permute-done((bf16[512,1024]{1,0:T(8,128)(2,1)}, bf16[512,1024]{1,0:T(8,128)(2,1)}, u32[]{:S(2)}, u32[]{:S(2)}) %collective-permute-start.7) | collective-permute-done | bytes 1048608 | tf_op jit(solution)/shard_map/ppermute | solution.py:37
  30.6 2.3 %broadcast_select_fusion = bf16[512,1024]{1,0:T(8,128)(2,1)} fusion(bf16[512,1024]{1,0:T(8,128)(2,1)} %collective-permute-done.7.rest_3_.rest_6_, bf16[512,1024]{1,0:T(8,128)(2,1)} %shard_map.116.rest_5_.rest_8_, pred[]{:T(512)S(6)} %eq.7), kind=kLoop, calls=%fused_computation | loop fusion | flops 524288 | bytes 3145729 | tf_op jit(solution)/shard_map/jit(_where)/select_n | solution.py:527
  32.9 1.5 %collective-permute-start.3 = (f32[32,512]{1,0:T(8,128)S(1)}, f32[32,512]{1,0:T(8,128)S(1)}, u32[]{:S(2)}, u32[]{:S(2)}) collective-permute-start(f32[32,512]{1,0:T(8,128)S(1)} %get-tuple-element.11.mine_ref), channel_id=1, source_target_pairs={{0,1},{1,0},{2,3},{3,2},{4,5},{5,4},{6,7},{7,6},{8,9},{9,8},{10,11... | collective-permute-start | bytes 196616 | tf_op jit(solution)/shard_map/ppermute | solution.py:41
  34.4 8.2 %collective-permute-done.3.theirs_ref = f32[32,512]{1,0:T(8,128)S(1)} collective-permute-done((f32[32,512]{1,0:T(8,128)S(1)}, f32[32,512]{1,0:T(8,128)S(1)}, u32[]{:S(2)}, u32[]{:S(2)}) %collective-permute-start.3) | collective-permute-done | bytes 65568 | tf_op jit(solution)/shard_map/ppermute | solution.py:41
  42.6 2.5 %collective-permute-start.4 = (bf16[32,512]{1,0:T(8,128)(2,1)S(1)}, bf16[32,512]{1,0:T(8,128)(2,1)S(1)}, u32[]{:S(2)}, u32[]{:S(2)}) collective-permute-start(bf16[32,512]{1,0:T(8,128)(2,1)S(1)} %shard_map.114.t0_ref.rest_10_), channel_id=1, source_target_pairs={{0,4},{2,6},{4,8},{6,10},{8,12},{10,14},{12,16},{14,18},{16,20},{1... | collective-permute-start | bytes 98312 | tf_op jit(solution)/shard_map/ppermute | solution.py:37
  46.5 8.0 %shard_map.112 = (bf16[512,1024]{1,0:T(8,128)(2,1)S(1)}, bf16[512,1024]{1,0:T(8,128)(2,1)}) custom-call(s32[1]{0:T(128)} %bitcast.1.offset_ref, bf16[512,2688]{1,0:T(8,128)(2,1)} %rest_0_.5, bf16[4096,2688]{1,0:T(8,128)(2,1)} %rest_1_.5, bf16[512,1024]{1,0:T(8,128)(2,1)} %k_ref.1, bf16[512,1024]{1,0:T(8,128)(2,1)} %v_ref.1), custom_call_target="tpu_custom_call" | custom-call | flops 2818572288 | bytes 9306112 | tf_op jit(solution)/shard_map/pallas_call | solution.py:87
  55.4 5.0 %collective-permute-start.1 = (bf16[512,1024]{1,0:T(8,128)(2,1)}, bf16[512,1024]{1,0:T(8,128)(2,1)}, u32[]{:S(2)}, u32[]{:S(2)}) collective-permute-start(bf16[512,1024]{1,0:T(8,128)(2,1)} %get-tuple-element.10.rest_5_.rest_8_), channel_id=1, source_target_pairs={{0,4},{2,6},{4,8},{6,10},{8,12},{10,14},{12,16},{14,18},{16,20},{1... | collective-permute-start | bytes 3145736 | tf_op jit(solution)/shard_map/ppermute | solution.py:37
  60.5 3.5 %collective-permute-start.2 = (bf16[512,1024]{1,0:T(8,128)(2,1)}, bf16[512,1024]{1,0:T(8,128)(2,1)S(1)}, u32[]{:S(2)}, u32[]{:S(2)}) collective-permute-start(bf16[512,1024]{1,0:T(8,128)(2,1)} %get-tuple-element.10.rest_5_.rest_8_), channel_id=1, source_target_pairs={{0,2},{2,4},{4,6},{6,8},{8,10},{10,12},{12,14},{14,16},{16,18},{18... | collective-permute-start | bytes 3145736 | tf_op jit(solution)/shard_map/ppermute | solution.py:37
  64.0 1.6 %collective-permute-start = (bf16[512,1024]{1,0:T(8,128)(2,1)}, bf16[512,1024]{1,0:T(8,128)(2,1)S(1)}, u32[]{:S(2)}, u32[]{:S(2)}) collective-permute-start(bf16[512,1024]{1,0:T(8,128)(2,1)} %copy-done.2), channel_id=1, source_target_pairs={{0,1},{1,0},{2,3},{3,2},{4,5},{5,4},{6,7},{7,6},{8,9},{9,8},{10,11... | collective-permute-start | bytes 3145736 | tf_op jit(solution)/shard_map/ppermute | solution.py:485
  66.1 24.7 %shard_map.117.rest_12_ = bf16[8,2048]{1,0:T(8,128)(2,1)S(1)} custom-call(s32[1]{0:T(128)} %bitcast.6.offset_ref, bf16[512,2048]{1,0:T(8,128)(2,1)} %q_ref.3, bf16[512,2688]{1,0:T(8,128)(2,1)} %rest_0_.5, bf16[4096,2688]{1,0:T(8,128)(2,1)} %rest_1_.5, bf16[512,1024]{1,0:T(8,128)(2,1)S(1)} %collective-permute-done.6.rest_2_, ...), custom_call_target="tpu_custom_call" | custom-call | flops 13555990528 | bytes 10747904 | tf_op jit(solution)/shard_map/pallas_call | solution.py:378
  91.9 24.4 %shard_map.118 = bf16[8,4096]{1,0:T(8,128)(2,1)S(1)} custom-call(s32[1]{0:T(128)} %bitcast.offset_ref, bf16[512,2048]{1,0:T(8,128)(2,1)} %q_ref.3, bf16[512,2688]{1,0:T(8,128)(2,1)} %rest_0_.5, bf16[4096,2688]{1,0:T(8,128)(2,1)} %rest_1_.5, bf16[512,1024]{1,0:T(8,128)(2,1)S(1)} %collective-permute-done.rest_2_, ...), custom_call_target="tpu_custom_call" | custom-call | flops 13555990528 | bytes 10747904 | tf_op jit(solution)/shard_map/pallas_call | solution.py:378
  116.3 3.9 %collective-permute-start.9 = (bf16[8,4096]{1,0:T(8,128)(2,1)S(1)}, bf16[8,4096]{1,0:T(8,128)(2,1)S(1)}, u32[]{:S(2)}, u32[]{:S(2)}) collective-permute-start(bf16[8,4096]{1,0:T(8,128)(2,1)S(1)} %shard_map.118), channel_id=1, source_target_pairs={{0,2},{2,0},{4,6},{6,4},{8,10},{10,8},{12,14},{14,12},{16,18},{18,... | collective-permute-start | bytes 196616 | tf_op jit(solution)/shard_map/ppermute | solution.py:41
  121.1 2.7 %collective-permute-start.10 = (bf16[8,4096]{1,0:T(8,128)(2,1)S(1)}, bf16[8,4096]{1,0:T(8,128)(2,1)S(1)}, u32[]{:S(2)}, u32[]{:S(2)}) collective-permute-start(bf16[8,4096]{1,0:T(8,128)(2,1)S(1)} %add_convert_fusion.1), channel_id=1, source_target_pairs={{0,4},{2,6},{4,0},{6,2},{8,12},{10,14},{12,8},{14,10},{16,20},{18,... | collective-permute-start | bytes 196616 | tf_op jit(solution)/shard_map/ppermute | solution.py:41
  123.8 1.6 %collective-permute-start.11 = (bf16[8,4096]{1,0:T(8,128)(2,1)S(1)}, bf16[8,4096]{1,0:T(8,128)(2,1)S(1)}, u32[]{:S(2)}, u32[]{:S(2)}) collective-permute-start(bf16[8,4096]{1,0:T(8,128)(2,1)S(1)} %add_convert_fusion.1), channel_id=1, source_target_pairs={{0,8},{2,10},{4,12},{6,14},{8,0},{10,2},{12,4},{14,6},{16,24},{18,... | collective-permute-start | bytes 196616 | tf_op jit(solution)/shard_map/ppermute | solution.py:41
  126.2 1.8 %collective-permute-done.11 = bf16[8,4096]{1,0:T(8,128)(2,1)S(1)} collective-permute-done((bf16[8,4096]{1,0:T(8,128)(2,1)S(1)}, bf16[8,4096]{1,0:T(8,128)(2,1)S(1)}, u32[]{:S(2)}, u32[]{:S(2)}) %collective-permute-start.11) | collective-permute-done | bytes 65568 | tf_op jit(solution)/shard_map/ppermute | solution.py:41
  128.0 2.5 %collective-permute-done.12 = bf16[8,4096]{1,0:T(8,128)(2,1)S(1)} collective-permute-done((bf16[8,4096]{1,0:T(8,128)(2,1)S(1)}, bf16[8,4096]{1,0:T(8,128)(2,1)S(1)}, u32[]{:S(2)}, u32[]{:S(2)}) %collective-permute-start.12) | collective-permute-done | bytes 65568 | tf_op jit(solution)/shard_map/ppermute | solution.py:41
  130.5 2.1 %collective-permute-start.13 = (bf16[8,4096]{1,0:T(8,128)(2,1)S(1)}, bf16[8,4096]{1,0:T(8,128)(2,1)S(1)}, u32[]{:S(2)}, u32[]{:S(2)}) collective-permute-start(bf16[8,4096]{1,0:T(8,128)(2,1)S(1)} %add_convert_fusion.mine_ref.refs_0_), channel_id=1, source_target_pairs={{0,16},{2,18},{4,20},{6,22},{8,24},{10,26},{12,28},{14,30},{16,0},... | collective-permute-start | bytes 196616 | tf_op jit(solution)/shard_map/ppermute | solution.py:41
  132.6 3.9 %collective-permute-done.13.theirs_ref.refs_1_ = bf16[8,4096]{1,0:T(8,128)(2,1)S(1)} collective-permute-done((bf16[8,4096]{1,0:T(8,128)(2,1)S(1)}, bf16[8,4096]{1,0:T(8,128)(2,1)S(1)}, u32[]{:S(2)}, u32[]{:S(2)}) %collective-permute-start.13) | collective-permute-done | bytes 65568 | tf_op jit(solution)/shard_map/ppermute | solution.py:41
  136.5 1.6 %collective-permute-start.14 = (f32[8,128]{1,0:T(8,128)S(1)}, f32[8,128]{1,0:T(8,128)S(1)}, u32[]{:S(2)}, u32[]{:S(2)}) collective-permute-start(f32[8,128]{1,0:T(8,128)S(1)} %shard_map.119.refs_2_), channel_id=1, source_target_pairs={{0,1},{1,0},{2,3},{3,2},{4,5},{5,4},{6,7},{7,6},{8,9},{9,8},{10,11... | collective-permute-start | bytes 12296 | tf_op jit(solution)/shard_map/ppermute | solution.py:41
  138.1 2.1 %collective-permute-done.14.refs_3_ = f32[8,128]{1,0:T(8,128)S(1)} collective-permute-done((f32[8,128]{1,0:T(8,128)S(1)}, f32[8,128]{1,0:T(8,128)S(1)}, u32[]{:S(2)}, u32[]{:S(2)}) %collective-permute-start.14) | collective-permute-done | bytes 4128 | tf_op jit(solution)/shard_map/ppermute | solution.py:41
  (29 shorter events, 6.5 us)
Async XLA Ops:
  0.6 8.2 %copy-start.3 = (bf16[2688]{0:T(1024)(128)(2,1)S(1)}, bf16[2688]{0:T(1024)(128)(2,1)}, u32[]{:S(2)}) copy-start(bf16[2688]{0:T(1024)(128)(2,1)} %param.10) | copy-start | bytes 16132
  0.6 8.2 %copy-start = (bf16[2688,24]{0,1:T(8,128)(2,1)S(1)}, bf16[2688,24]{0,1:T(8,128)(2,1)}, u32[]{:S(2)}) copy-start(bf16[2688,24]{0,1:T(8,128)(2,1)} %param.17) | copy-start | bytes 387076
  3.0 27.6 %collective-permute-start.7 = (bf16[512,1024]{1,0:T(8,128)(2,1)}, bf16[512,1024]{1,0:T(8,128)(2,1)}, u32[]{:S(2)}, u32[]{:S(2)}) collective-permute-start(bf16[512,1024]{1,0:T(8,128)(2,1)} %shard_map.116.rest_5_.rest_8_), channel_id=1, source_target_pairs={{0,4},{2,6},{4,8},{6,10},{8,12},{10,14},{12,16},{14,18},{16,20},{1... | collective-permute-start | bytes 3145736 | tf_op jit(solution)/shard_map/ppermute | solution.py:37
  16.5 26.1 %copy-start.1 = (s32[512]{0:T(512)S(1)}, s32[512]{0:T(512)}, u32[]{:S(2)}) copy-start(s32[512]{0:T(512)} %param.11) | copy-start | bytes 6148
  16.5 49.6 %collective-permute-start.6 = (bf16[512,1024]{1,0:T(8,128)(2,1)S(1)}, bf16[512,1024]{1,0:T(8,128)(2,1)S(1)}, u32[]{:S(2)}, u32[]{:S(2)}) collective-permute-start(bf16[512,1024]{1,0:T(8,128)(2,1)S(1)} %get-tuple-element.14), channel_id=1, source_target_pairs={{0,1},{1,0},{2,3},{3,2},{4,5},{5,4},{6,7},{7,6},{8,9},{9,8},{10,11... | collective-permute-start | bytes 3145736 | tf_op jit(solution)/shard_map/ppermute | solution.py:485
  32.9 33.2 %collective-permute-start.8 = (bf16[512,1024]{1,0:T(8,128)(2,1)}, bf16[512,1024]{1,0:T(8,128)(2,1)}, u32[]{:S(2)}, u32[]{:S(2)}) collective-permute-start(bf16[512,1024]{1,0:T(8,128)(2,1)} %broadcast_select_fusion), channel_id=1, source_target_pairs={{0,2},{2,0},{4,6},{6,4},{8,10},{10,8},{12,14},{14,12},{16,18},{18,... | collective-permute-start | bytes 3145736 | tf_op jit(solution)/shard_map/ppermute | solution.py:41
  32.9 9.7 %collective-permute-start.3 = (f32[32,512]{1,0:T(8,128)S(1)}, f32[32,512]{1,0:T(8,128)S(1)}, u32[]{:S(2)}, u32[]{:S(2)}) collective-permute-start(f32[32,512]{1,0:T(8,128)S(1)} %get-tuple-element.11.mine_ref), channel_id=1, source_target_pairs={{0,1},{1,0},{2,3},{3,2},{4,5},{5,4},{6,7},{7,6},{8,9},{9,8},{10,11... | collective-permute-start | bytes 196616 | tf_op jit(solution)/shard_map/ppermute | solution.py:41
  42.6 17.8 %collective-permute-start.4 = (bf16[32,512]{1,0:T(8,128)(2,1)S(1)}, bf16[32,512]{1,0:T(8,128)(2,1)S(1)}, u32[]{:S(2)}, u32[]{:S(2)}) collective-permute-start(bf16[32,512]{1,0:T(8,128)(2,1)S(1)} %shard_map.114.t0_ref.rest_10_), channel_id=1, source_target_pairs={{0,4},{2,6},{4,8},{6,10},{8,12},{10,14},{12,16},{14,18},{16,20},{1... | collective-permute-start | bytes 98312 | tf_op jit(solution)/shard_map/ppermute | solution.py:37
  45.2 18.8 %collective-permute-start.5 = (bf16[32,512]{1,0:T(8,128)(2,1)S(1)}, bf16[32,512]{1,0:T(8,128)(2,1)S(1)}, u32[]{:S(2)}, u32[]{:S(2)}) collective-permute-start(bf16[32,512]{1,0:T(8,128)(2,1)S(1)} %shard_map.114.t0_ref.rest_10_), channel_id=1, source_target_pairs={{0,2},{2,4},{4,6},{6,8},{8,10},{10,12},{12,14},{14,16},{16,18},{18... | collective-permute-start | bytes 98312 | tf_op jit(solution)/shard_map/ppermute | solution.py:37
  54.4 1.0 copy-start.2
  55.4 35.4 %collective-permute-start.1 = (bf16[512,1024]{1,0:T(8,128)(2,1)}, bf16[512,1024]{1,0:T(8,128)(2,1)}, u32[]{:S(2)}, u32[]{:S(2)}) collective-permute-start(bf16[512,1024]{1,0:T(8,128)(2,1)} %get-tuple-element.10.rest_5_.rest_8_), channel_id=1, source_target_pairs={{0,4},{2,6},{4,8},{6,10},{8,12},{10,14},{12,16},{14,18},{16,20},{1... | collective-permute-start | bytes 3145736 | tf_op jit(solution)/shard_map/ppermute | solution.py:37
  60.5 30.4 %collective-permute-start.2 = (bf16[512,1024]{1,0:T(8,128)(2,1)}, bf16[512,1024]{1,0:T(8,128)(2,1)S(1)}, u32[]{:S(2)}, u32[]{:S(2)}) collective-permute-start(bf16[512,1024]{1,0:T(8,128)(2,1)} %get-tuple-element.10.rest_5_.rest_8_), channel_id=1, source_target_pairs={{0,2},{2,4},{4,6},{6,8},{8,10},{10,12},{12,14},{14,16},{16,18},{18... | collective-permute-start | bytes 3145736 | tf_op jit(solution)/shard_map/ppermute | solution.py:37
  64.0 26.9 %collective-permute-start = (bf16[512,1024]{1,0:T(8,128)(2,1)}, bf16[512,1024]{1,0:T(8,128)(2,1)S(1)}, u32[]{:S(2)}, u32[]{:S(2)}) collective-permute-start(bf16[512,1024]{1,0:T(8,128)(2,1)} %copy-done.2), channel_id=1, source_target_pairs={{0,1},{1,0},{2,3},{3,2},{4,5},{5,4},{6,7},{7,6},{8,9},{9,8},{10,11... | collective-permute-start | bytes 3145736 | tf_op jit(solution)/shard_map/ppermute | solution.py:485
  90.9 1.0 copy-start.4
  116.3 4.8 %collective-permute-start.9 = (bf16[8,4096]{1,0:T(8,128)(2,1)S(1)}, bf16[8,4096]{1,0:T(8,128)(2,1)S(1)}, u32[]{:S(2)}, u32[]{:S(2)}) collective-permute-start(bf16[8,4096]{1,0:T(8,128)(2,1)S(1)} %shard_map.118), channel_id=1, source_target_pairs={{0,2},{2,0},{4,6},{6,4},{8,10},{10,8},{12,14},{14,12},{16,18},{18,... | collective-permute-start | bytes 196616 | tf_op jit(solution)/shard_map/ppermute | solution.py:41
  121.1 5.1 %collective-permute-start.10 = (bf16[8,4096]{1,0:T(8,128)(2,1)S(1)}, bf16[8,4096]{1,0:T(8,128)(2,1)S(1)}, u32[]{:S(2)}, u32[]{:S(2)}) collective-permute-start(bf16[8,4096]{1,0:T(8,128)(2,1)S(1)} %add_convert_fusion.1), channel_id=1, source_target_pairs={{0,4},{2,6},{4,0},{6,2},{8,12},{10,14},{12,8},{14,10},{16,20},{18,... | collective-permute-start | bytes 196616 | tf_op jit(solution)/shard_map/ppermute | solution.py:41
  123.8 4.3 %collective-permute-start.11 = (bf16[8,4096]{1,0:T(8,128)(2,1)S(1)}, bf16[8,4096]{1,0:T(8,128)(2,1)S(1)}, u32[]{:S(2)}, u32[]{:S(2)}) collective-permute-start(bf16[8,4096]{1,0:T(8,128)(2,1)S(1)} %add_convert_fusion.1), channel_id=1, source_target_pairs={{0,8},{2,10},{4,12},{6,14},{8,0},{10,2},{12,4},{14,6},{16,24},{18,... | collective-permute-start | bytes 196616 | tf_op jit(solution)/shard_map/ppermute | solution.py:41
  125.3 5.2 %collective-permute-start.12 = (bf16[8,4096]{1,0:T(8,128)(2,1)S(1)}, bf16[8,4096]{1,0:T(8,128)(2,1)S(1)}, u32[]{:S(2)}, u32[]{:S(2)}) collective-permute-start(bf16[8,4096]{1,0:T(8,128)(2,1)S(1)} %add_convert_fusion.1), channel_id=1, source_target_pairs={{0,12},{2,14},{4,8},{6,10},{8,4},{10,6},{12,0},{14,2},{16,28},{18,... | collective-permute-start | bytes 196616 | tf_op jit(solution)/shard_map/ppermute | solution.py:41
  130.5 5.9 %collective-permute-start.13 = (bf16[8,4096]{1,0:T(8,128)(2,1)S(1)}, bf16[8,4096]{1,0:T(8,128)(2,1)S(1)}, u32[]{:S(2)}, u32[]{:S(2)}) collective-permute-start(bf16[8,4096]{1,0:T(8,128)(2,1)S(1)} %add_convert_fusion.mine_ref.refs_0_), channel_id=1, source_target_pairs={{0,16},{2,18},{4,20},{6,22},{8,24},{10,26},{12,28},{14,30},{16,0},... | collective-permute-start | bytes 196616 | tf_op jit(solution)/shard_map/ppermute | solution.py:41
  136.5 3.7 %collective-permute-start.14 = (f32[8,128]{1,0:T(8,128)S(1)}, f32[8,128]{1,0:T(8,128)S(1)}, u32[]{:S(2)}, u32[]{:S(2)}) collective-permute-start(f32[8,128]{1,0:T(8,128)S(1)} %shard_map.119.refs_2_), channel_id=1, source_target_pairs={{0,1},{1,0},{2,3},{3,2},{4,5},{5,4},{6,7},{7,6},{8,9},{9,8},{10,11... | collective-permute-start | bytes 12296 | tf_op jit(solution)/shard_map/ppermute | solution.py:41

commit v6 on v5

--- a/solution.py
+++ b/solution.py
@@ -62,9 +62,9 @@
     rows = keys.shape[0]
     return pl.pallas_call(
         functools.partial(pack_body, wide),
-        grid=(1,),
-        in_specs=[pl.BlockSpec((rows, wide * blocks), lambda i: (0, 0))] * 2,
-        out_specs=pl.BlockSpec((rows, 2 * wide * blocks), lambda i: (0, 0)),
+        grid=(blocks,),
+        in_specs=[pl.BlockSpec((rows, wide), lambda i: (0, i))] * 2,
+        out_specs=pl.BlockSpec((rows, 2 * wide), lambda i: (0, i)),
         out_shape=jax.ShapeDtypeStruct((rows, 2 * wide * blocks), keys.dtype),
         compiler_params=pltpu.CompilerParams(vmem_limit_bytes=62 << 20),
     )(keys, values)
@@ -150,6 +150,43 @@
     row = lax.broadcasted_iota(jnp.int32, (rank, low.shape[1]), 0)
     extra = jnp.where(row == 0, 1.0, jnp.where(row == 1, doc_ref[...].astype(jnp.float32), 0.0))
     out_ref[...] = jnp.concatenate([low[rank : 3 * rank], extra, low[:rank]], 0).astype(out_ref.dtype)
+
+
+def pick_body(second_ref, far_ref, own_ref, there_ref, here_ref, out_ref):
+    rows = far_ref.shape[0]
+
+    @pl.when(second_ref[0] == 1)
+    def _():
+        out_ref[:rows, :] = far_ref[...]
+        out_ref[rows:, :] = there_ref[...]
+
+    @pl.when(second_ref[0] != 1)
+    def _():
+        out_ref[:rows, :] = own_ref[...]
+        out_ref[rows:, :] = here_ref[...]
+
+
+def pick_call(second, far, own, there, here):
+    rows, span = own.shape
+    width = 2 * LANES
+    last = here.shape[1] // width - 1
+    side = pl.BlockSpec((TABLE, width), lambda i, sec: (0, jnp.minimum(i, last)))
+    return pl.pallas_call(
+        pick_body,
+        grid_spec=pltpu.PrefetchScalarGridSpec(
+            num_scalar_prefetch=1,
+            grid=(span // width,),
+            in_specs=[
+                pl.BlockSpec((rows, width), lambda i, sec: (0, i * sec[0])),
+                pl.BlockSpec((rows, width), lambda i, sec: (0, i * (1 - sec[0]))),
+                side,
+                side,
+            ],
+            out_specs=pl.BlockSpec((rows + TABLE, width), lambda i, sec: (0, i)),
+        ),
+        out_shape=jax.ShapeDtypeStruct((rows + TABLE, span), own.dtype),
+        compiler_params=pltpu.CompilerParams(vmem_limit_bytes=GRANT),
+    )(second, far, own, there, here)
 
 
 def prep_body(first_ref, t2_ref, t1_ref, t0_ref, ext_ref, st_ref):
@@ -499,13 +536,16 @@
         low, other, document_index[None, :]
     )
     table2 = shifted(table, "ctx", 2)
-    table1 = shifted(table, "ctx", 1)
     prepare = pl.pallas_call(
         prep_body,
         grid_spec=pltpu.PrefetchScalarGridSpec(
             num_scalar_prefetch=1,
             grid=(1,),
-            in_specs=[pl.BlockSpec((TABLE, rows), lambda i, off: (0, 0))] * 3,
+            in_specs=[
+                pl.BlockSpec((TABLE, rows), lambda i, off: (0, 0)),
+                pl.BlockSpec((TABLE, rows), lambda i, off: (rows // TABLE, 0)),
+                pl.BlockSpec((TABLE, rows), lambda i, off: (0, 0)),
+            ],
             out_specs=[
                 pl.BlockSpec((3 * rows, LANES), lambda i, off: (0, 0)),
                 pl.BlockSpec((rows, LANES), lambda i, off: (0, 0)),
@@ -517,15 +557,15 @@
         ],
         compiler_params=SMALL,
     )
-    ext, starts = prepare(scalar(2 * rows - ctx_at * rows), table2, table1, table)
-
-    second = (ctx_at % 2) == 1
+
+    second = scalar(ctx_at % 2)
     sums = None
     for c in range(chunks):
         far = shifted(packs[c], "ctx", 2)
         if c == 0:
-            picked = jnp.where(second, far, packs[c])
+            picked = pick_call(second, far, packs[c], table2, table)
             near = xor_move(picked, "ctx", 1)
+            ext, starts = prepare(scalar(2 * rows - ctx_at * rows), table2, near, table)
         else:
             near = shifted(packs[c], "ctx", 1)
         first = scalar((tp_at * half + c * per) // units)

time: 141 us -> 130 us (0.922)
  starting transfers between devices: 35.5 us -> 28.9 us
  waiting for transfers between devices: 31.8 us -> 28 us
  Pallas kernels: 68.5 us -> 72.3 us
  other arithmetic: 2.36 us -> 0.06 us
  local copies, waits for them, and re-layouts: 1.99 us -> 0.03 us
    ppermute x2, waiting for transfers between devices: 0.01 us -> 8.14 us  [local(): lax.ppermute(part, 'tp', [(at, (at + d) % tp) for at in range(tp)])]
    ppermute x8, waiting for transfers between devices: 19.4 us -> 12.1 us  [xor_move(): lax.ppermute(value, axis, [(at, at ^ step) for at in range(lax.axis_size(...]
    ppermute x5 -> x4, waiting for transfers between devices: 12.5 us -> 7.78 us  [shifted(): lax.ppermute(value, axis, [(source, source + steps) for source in range(f...]
    pallas_call x2 -> x3, Pallas kernels: 2.9 us -> 6.35 us  [the longest x1 3.64 us: pick_call(): pl.pallas_call(pick_body, grid_spec=pltpu.PrefetchScalarGridSpec(num_scal...]
    ppermute x8, starting transfers between devices: 14.2 us -> 11 us  [xor_move(): lax.ppermute(value, axis, [(at, at ^ step) for at in range(lax.axis_size(...]
    ppermute x5 -> x4, starting transfers between devices: 18.1 us -> 15.8 us  [shifted(): lax.ppermute(value, axis, [(source, source + steps) for source in range(f...]
    select_n x1 -> x0, other arithmetic: 2.31 us -> none  [local(): picked = jnp.where(second, far, packs[c])]
    unnamed x10, local copies, waits for them, and re-layouts: 1.99 us -> 0.02 us
  transfers between devices with their start and end apart: 15 -> 14, of which waited for: 7 -> 9; matrix products, arithmetic and copies ran while one was open for 2% -> 0% of each run, Pallas kernels for 29% -> 32%
where the time goes in v6:
time: 130 us
  Pallas kernels  72.3 us (56%)
  starting transfers between devices  28.9 us (22%)
  waiting for transfers between devices  28 us (22%)
    pallas_call x2, Pallas kernels, attend(): pl.pallas_call(functools.partial(attend_body, steps, units, base, alone),...  49.5 us
    ppermute x4, starting transfers between devices, shifted(): lax.ppermute(value, axis, [(source, source + steps) for source in range(f...  15.8 us
    ppermute x8, waiting for transfers between devices, xor_move(): lax.ppermute(value, axis, [(at, at ^ step) for at in range(lax.axis_size(...  12.1 us
    ppermute x8, starting transfers between devices, xor_move(): lax.ppermute(value, axis, [(at, at ^ step) for at in range(lax.axis_size(...  11 us
    ppermute x2, waiting for transfers between devices, local(): lax.ppermute(part, 'tp', [(at, (at + d) % tp) for at in range(tp)])  8.14 us
    pallas_call x1, Pallas kernels, project(): pl.pallas_call(project_body, grid_spec=pltpu.PrefetchScalarGridSpec(num_s...  7.91 us
    ppermute x4, waiting for transfers between devices, shifted(): lax.ppermute(value, axis, [(source, source + steps) for source in range(f...  7.78 us
    pallas_call x1, Pallas kernels, open_call(): pl.pallas_call(open_body, grid_spec=pltpu.PrefetchScalarGridSpec(num_scal...  7.64 us
  transfers between devices with their start and end apart: 14, of which 9 were waited for; matrix products, arithmetic and copies ran while one was open for 0% of the time, Pallas kernels for 32%

profile of v6, /device:TPU:0, one launch (start us, length us, event | category | flops | bytes accessed | tf_op | source)
XLA Modules:
  0.0 130.1 jit_solution(6675712799944584298)
XLA Ops:
  0.7 2.2 %shard_map.115.own_ref.rest_5_.rest_8_ = bf16[512,1024]{1,0:T(8,128)(2,1)} custom-call(bf16[512,1024]{1,0:T(8,128)(2,1)} %k_ref.1, bf16[512,1024]{1,0:T(8,128)(2,1)} %v_ref.1), custom_call_target="tpu_custom_call" | custom-call | tf_op jit(solution)/shard_map/pallas_call | solution.py:63
  2.8 4.9 %collective-permute-start.5 = (bf16[512,1024]{1,0:T(8,128)(2,1)}, bf16[512,1024]{1,0:T(8,128)(2,1)S(1)}, u32[]{:S(2)}, u32[]{:S(2)}) collective-permute-start(bf16[512,1024]{1,0:T(8,128)(2,1)} %shard_map.115.own_ref.rest_5_.rest_8_), channel_id=1, source_target_pairs={{0,4},{2,6},{4,8},{6,10},{8,12},{10,14},{12,16},{14,18},{16,20},{1... | collective-permute-start | bytes 3145736 | tf_op jit(solution)/shard_map/ppermute | solution.py:37
  7.8 7.6 %shard_map.113 = (bf16[512,1024]{1,0:T(8,128)(2,1)S(1)}, f32[32,512]{1,0:T(8,128)S(1)}) custom-call(s32[1]{0:T(128)} %bitcast.3.offset_ref, bf16[512,2688]{1,0:T(8,128)(2,1)} %rest_0_.5, bf16[4096,2688]{1,0:T(8,128)(2,1)} %rest_1_.5, bf16[512,2688]{1,0:T(8,128)(2,1)} %x_ref.1, bf16[1,2688]{1,0:T(2,128)(2,1)S(1)} %broadcast_in_dim.6.norm_ref, ...), custom_call_target="tpu_custom_call" | custom-call | flops 2818572288 | bytes 12058624 | tf_op jit(solution)/shard_map/pallas_call | solution.py:115
  15.5 1.6 %collective-permute-start.3 = (f32[32,512]{1,0:T(8,128)S(1)}, f32[32,512]{1,0:T(8,128)S(1)}, u32[]{:S(2)}, u32[]{:S(2)}) collective-permute-start(f32[32,512]{1,0:T(8,128)S(1)} %get-tuple-element.11.mine_ref), channel_id=1, source_target_pairs={{0,1},{1,0},{2,3},{3,2},{4,5},{5,4},{6,7},{7,6},{8,9},{9,8},{10,11... | collective-permute-start | bytes 196616 | tf_op jit(solution)/shard_map/ppermute | solution.py:41
  17.1 2.7 %collective-permute-done.3.theirs_ref = f32[32,512]{1,0:T(8,128)S(1)} collective-permute-done((f32[32,512]{1,0:T(8,128)S(1)}, f32[32,512]{1,0:T(8,128)S(1)}, u32[]{:S(2)}, u32[]{:S(2)}) %collective-permute-start.3) | collective-permute-done | bytes 65568 | tf_op jit(solution)/shard_map/ppermute | solution.py:41
  19.8 3.4 %collective-permute-start.4 = (bf16[32,512]{1,0:T(8,128)(2,1)S(1)}, bf16[32,512]{1,0:T(8,128)(2,1)S(1)}, u32[]{:S(2)}, u32[]{:S(2)}) collective-permute-start(bf16[32,512]{1,0:T(8,128)(2,1)S(1)} %shard_map.114.here_ref.t0_ref.rest_10_), channel_id=1, source_target_pairs={{0,4},{2,6},{4,8},{6,10},{8,12},{10,14},{12,16},{14,18},{16,20},{1... | collective-permute-start | bytes 98312 | tf_op jit(solution)/shard_map/ppermute | solution.py:37
  23.2 7.8 %collective-permute-done.4.there_ref.t2_ref = bf16[32,512]{1,0:T(8,128)(2,1)S(1)} collective-permute-done((bf16[32,512]{1,0:T(8,128)(2,1)S(1)}, bf16[32,512]{1,0:T(8,128)(2,1)S(1)}, u32[]{:S(2)}, u32[]{:S(2)}) %collective-permute-start.4) | collective-permute-done | bytes 32800 | tf_op jit(solution)/shard_map/ppermute | solution.py:37
  31.0 3.6 %shard_map.116 = bf16[544,1024]{1,0:T(8,128)(2,1)} custom-call(s32[1]{0:T(128)} %bitcast.6.second_ref, bf16[512,1024]{1,0:T(8,128)(2,1)S(1)} %collective-permute-done.5.far_ref.rest_3_.rest_6_, bf16[512,1024]{1,0:T(8,128)(2,1)} %shard_map.115.own_ref.rest_5_.rest_8_, bf16[32,512]{1,0:T(8,128)(2,1)S(1)} %collective-permute-done.4.there_ref.t2_ref, ...), custom_call_target="tpu_custom_call" | custom-call | tf_op jit(solution)/shard_map/pallas_call | solution.py:174
  34.6 1.5 %collective-permute-start.7 = (bf16[512,1024]{1,0:T(8,128)(2,1)S(1)}, bf16[512,1024]{1,0:T(8,128)(2,1)}, u32[]{:S(2)}, u32[]{:S(2)}) collective-permute-start(bf16[512,1024]{1,0:T(8,128)(2,1)S(1)} %get-tuple-element.14), channel_id=1, source_target_pairs={{0,1},{1,0},{2,3},{3,2},{4,5},{5,4},{6,7},{7,6},{8,9},{9,8},{10,11... | collective-permute-start | bytes 3145736 | tf_op jit(solution)/shard_map/ppermute | solution.py:522
  36.2 7.9 %shard_map.112 = (bf16[512,1024]{1,0:T(8,128)(2,1)}, bf16[512,1024]{1,0:T(8,128)(2,1)}) custom-call(s32[1]{0:T(128)} %bitcast.1.offset_ref, bf16[512,2688]{1,0:T(8,128)(2,1)} %rest_0_.5, bf16[4096,2688]{1,0:T(8,128)(2,1)} %rest_1_.5, bf16[512,1024]{1,0:T(8,128)(2,1)} %k_ref.1, bf16[512,1024]{1,0:T(8,128)(2,1)} %v_ref.1), custom_call_target="tpu_custom_call" | custom-call | flops 2818572288 | bytes 9306112 | tf_op jit(solution)/shard_map/pallas_call | solution.py:87
  44.1 3.1 %collective-permute-start.2 = (bf16[512,1024]{1,0:T(8,128)(2,1)}, bf16[512,1024]{1,0:T(8,128)(2,1)}, u32[]{:S(2)}, u32[]{:S(2)}) collective-permute-start(bf16[512,1024]{1,0:T(8,128)(2,1)} %get-tuple-element.10.rest_5_.rest_8_), channel_id=1, source_target_pairs={{0,2},{2,4},{4,6},{6,8},{8,10},{10,12},{12,14},{14,16},{16,18},{18... | collective-permute-start | bytes 3145736 | tf_op jit(solution)/shard_map/ppermute | solution.py:37
  47.2 4.4 %collective-permute-start.1 = (bf16[512,1024]{1,0:T(8,128)(2,1)}, bf16[512,1024]{1,0:T(8,128)(2,1)}, u32[]{:S(2)}, u32[]{:S(2)}) collective-permute-start(bf16[512,1024]{1,0:T(8,128)(2,1)} %get-tuple-element.10.rest_5_.rest_8_), channel_id=1, source_target_pairs={{0,4},{2,6},{4,8},{6,10},{8,12},{10,14},{12,16},{14,18},{16,20},{1... | collective-permute-start | bytes 3145736 | tf_op jit(solution)/shard_map/ppermute | solution.py:37
  52.7 8.1 %collective-permute-done.7.rest_2_ = bf16[512,1024]{1,0:T(8,128)(2,1)} collective-permute-done((bf16[512,1024]{1,0:T(8,128)(2,1)S(1)}, bf16[512,1024]{1,0:T(8,128)(2,1)}, u32[]{:S(2)}, u32[]{:S(2)}) %collective-permute-start.7) | collective-permute-done | bytes 1048608 | tf_op jit(solution)/shard_map/ppermute | solution.py:522
  60.8 24.9 %shard_map.118.rest_12_ = bf16[8,2048]{1,0:T(8,128)(2,1)S(1)} custom-call(s32[1]{0:T(128)} %bitcast.7.offset_ref, bf16[512,2048]{1,0:T(8,128)(2,1)} %q_ref.3, bf16[512,2688]{1,0:T(8,128)(2,1)} %rest_0_.5, bf16[4096,2688]{1,0:T(8,128)(2,1)} %rest_1_.5, bf16[512,1024]{1,0:T(8,128)(2,1)} %collective-permute-done.7.rest_2_, bf16[512,1024]{1,0:T(8,128)(2,1)} %copy-done.1, ...), custom_call_target="tpu_custom_call" | custom-call | flops 13555990528 | bytes 10747904 | tf_op jit(solution)/shard_map/pallas_call | solution.py:415
  85.7 24.6 %shard_map.119 = bf16[8,4096]{1,0:T(8,128)(2,1)S(1)} custom-call(s32[1]{0:T(128)} %bitcast.offset_ref, bf16[512,2048]{1,0:T(8,128)(2,1)} %q_ref.3, bf16[512,2688]{1,0:T(8,128)(2,1)} %rest_0_.5, bf16[4096,2688]{1,0:T(8,128)(2,1)} %rest_1_.5, bf16[512,1024]{1,0:T(8,128)(2,1)S(1)} %collective-permute-done.rest_2_, ...), custom_call_target="tpu_custom_call" | custom-call | flops 13555990528 | bytes 10747904 | tf_op jit(solution)/shard_map/pallas_call | solution.py:415
  110.5 1.2 collective-permute-done.8
  111.7 3.6 %collective-permute-start.11 = (bf16[8,4096]{1,0:T(8,128)(2,1)S(1)}, bf16[8,4096]{1,0:T(8,128)(2,1)S(1)}, u32[]{:S(2)}, u32[]{:S(2)}) collective-permute-start(bf16[8,4096]{1,0:T(8,128)(2,1)S(1)} %add_convert_fusion.1), channel_id=1, source_target_pairs={{0,12},{2,14},{4,8},{6,10},{8,4},{10,6},{12,0},{14,2},{16,28},{18,... | collective-permute-start | bytes 196616 | tf_op jit(solution)/shard_map/ppermute | solution.py:41
  115.8 1.0 collective-permute-start.9
  116.7 1.0 collective-permute-done.11
  117.7 1.9 %collective-permute-done.10 = bf16[8,4096]{1,0:T(8,128)(2,1)S(1)} collective-permute-done((bf16[8,4096]{1,0:T(8,128)(2,1)S(1)}, bf16[8,4096]{1,0:T(8,128)(2,1)S(1)}, u32[]{:S(2)}, u32[]{:S(2)}) %collective-permute-start.10) | collective-permute-done | bytes 65568 | tf_op jit(solution)/shard_map/ppermute | solution.py:41
  120.1 2.8 %collective-permute-start.12 = (bf16[8,4096]{1,0:T(8,128)(2,1)S(1)}, bf16[8,4096]{1,0:T(8,128)(2,1)S(1)}, u32[]{:S(2)}, u32[]{:S(2)}) collective-permute-start(bf16[8,4096]{1,0:T(8,128)(2,1)S(1)} %add_convert_fusion.mine_ref.refs_0_), channel_id=1, source_target_pairs={{0,16},{2,18},{4,20},{6,22},{8,24},{10,26},{12,28},{14,30},{16,0},... | collective-permute-start | bytes 196616 | tf_op jit(solution)/shard_map/ppermute | solution.py:41
  122.8 2.7 %collective-permute-done.12.theirs_ref.refs_1_ = bf16[8,4096]{1,0:T(8,128)(2,1)S(1)} collective-permute-done((bf16[8,4096]{1,0:T(8,128)(2,1)S(1)}, bf16[8,4096]{1,0:T(8,128)(2,1)S(1)}, u32[]{:S(2)}, u32[]{:S(2)}) %collective-permute-start.12) | collective-permute-done | bytes 65568 | tf_op jit(solution)/shard_map/ppermute | solution.py:41
  125.6 1.6 %collective-permute-start.13 = (f32[8,128]{1,0:T(8,128)S(1)}, f32[8,128]{1,0:T(8,128)S(1)}, u32[]{:S(2)}, u32[]{:S(2)}) collective-permute-start(f32[8,128]{1,0:T(8,128)S(1)} %shard_map.120.refs_2_), channel_id=1, source_target_pairs={{0,1},{1,0},{2,3},{3,2},{4,5},{5,4},{6,7},{7,6},{8,9},{9,8},{10,11... | collective-permute-start | bytes 12296 | tf_op jit(solution)/shard_map/ppermute | solution.py:41
  127.2 2.1 %collective-permute-done.13.refs_3_ = f32[8,128]{1,0:T(8,128)S(1)} collective-permute-done((f32[8,128]{1,0:T(8,128)S(1)}, f32[8,128]{1,0:T(8,128)S(1)}, u32[]{:S(2)}, u32[]{:S(2)}) %collective-permute-start.13) | collective-permute-done | bytes 4128 | tf_op jit(solution)/shard_map/ppermute | solution.py:41
  (27 shorter events, 3.0 us)
Async XLA Ops:
  0.6 7.1 %copy-start.4 = (bf16[2688]{0:T(1024)(128)(2,1)S(1)}, bf16[2688]{0:T(1024)(128)(2,1)}, u32[]{:S(2)}) copy-start(bf16[2688]{0:T(1024)(128)(2,1)} %param.10) | copy-start | bytes 16132
  0.6 7.2 %copy-start.2 = (bf16[2688,24]{0,1:T(8,128)(2,1)S(1)}, bf16[2688,24]{0,1:T(8,128)(2,1)}, u32[]{:S(2)}) copy-start(bf16[2688,24]{0,1:T(8,128)(2,1)} %param.17) | copy-start | bytes 387076
  2.8 28.2 %collective-permute-start.5 = (bf16[512,1024]{1,0:T(8,128)(2,1)}, bf16[512,1024]{1,0:T(8,128)(2,1)S(1)}, u32[]{:S(2)}, u32[]{:S(2)}) collective-permute-start(bf16[512,1024]{1,0:T(8,128)(2,1)} %shard_map.115.own_ref.rest_5_.rest_8_), channel_id=1, source_target_pairs={{0,4},{2,6},{4,8},{6,10},{8,12},{10,14},{12,16},{14,18},{16,20},{1... | collective-permute-start | bytes 3145736 | tf_op jit(solution)/shard_map/ppermute | solution.py:37
  7.8 12.0 %copy-start.3 = (s32[512]{0:T(512)S(1)}, s32[512]{0:T(512)}, u32[]{:S(2)}) copy-start(s32[512]{0:T(512)} %param.11) | copy-start | bytes 6148
  15.5 4.3 %collective-permute-start.3 = (f32[32,512]{1,0:T(8,128)S(1)}, f32[32,512]{1,0:T(8,128)S(1)}, u32[]{:S(2)}, u32[]{:S(2)}) collective-permute-start(f32[32,512]{1,0:T(8,128)S(1)} %get-tuple-element.11.mine_ref), channel_id=1, source_target_pairs={{0,1},{1,0},{2,3},{3,2},{4,5},{5,4},{6,7},{7,6},{8,9},{9,8},{10,11... | collective-permute-start | bytes 196616 | tf_op jit(solution)/shard_map/ppermute | solution.py:41
  19.8 11.2 %collective-permute-start.4 = (bf16[32,512]{1,0:T(8,128)(2,1)S(1)}, bf16[32,512]{1,0:T(8,128)(2,1)S(1)}, u32[]{:S(2)}, u32[]{:S(2)}) collective-permute-start(bf16[32,512]{1,0:T(8,128)(2,1)S(1)} %shard_map.114.here_ref.t0_ref.rest_10_), channel_id=1, source_target_pairs={{0,4},{2,6},{4,8},{6,10},{8,12},{10,14},{12,16},{14,18},{16,20},{1... | collective-permute-start | bytes 98312 | tf_op jit(solution)/shard_map/ppermute | solution.py:37
  31.0 13.1 %copy-start.1 = (bf16[512,1024]{1,0:T(8,128)(2,1)}, bf16[512,1024]{1,0:T(8,128)(2,1)S(1)}, u32[]{:S(2)}) copy-start(bf16[512,1024]{1,0:T(8,128)(2,1)S(1)} %collective-permute-done.5.far_ref.rest_3_.rest_6_) | copy-start | bytes 3145732
  34.6 17.5 %collective-permute-start.6 = (bf16[544,1024]{1,0:T(8,128)(2,1)}, bf16[544,1024]{1,0:T(8,128)(2,1)S(1)}, u32[]{:S(2)}, u32[]{:S(2)}) collective-permute-start(bf16[544,1024]{1,0:T(8,128)(2,1)} %shard_map.116), channel_id=1, source_target_pairs={{0,2},{2,0},{4,6},{6,4},{8,10},{10,8},{12,14},{14,12},{16,18},{18,... | collective-permute-start | bytes 3342344 | tf_op jit(solution)/shard_map/ppermute | solution.py:41
  34.6 26.1 %collective-permute-start.7 = (bf16[512,1024]{1,0:T(8,128)(2,1)S(1)}, bf16[512,1024]{1,0:T(8,128)(2,1)}, u32[]{:S(2)}, u32[]{:S(2)}) collective-permute-start(bf16[512,1024]{1,0:T(8,128)(2,1)S(1)} %get-tuple-element.14), channel_id=1, source_target_pairs={{0,1},{1,0},{2,3},{3,2},{4,5},{5,4},{6,7},{7,6},{8,9},{9,8},{10,11... | collective-permute-start | bytes 3145736 | tf_op jit(solution)/shard_map/ppermute | solution.py:522
  44.1 41.6 %collective-permute-start.2 = (bf16[512,1024]{1,0:T(8,128)(2,1)}, bf16[512,1024]{1,0:T(8,128)(2,1)}, u32[]{:S(2)}, u32[]{:S(2)}) collective-permute-start(bf16[512,1024]{1,0:T(8,128)(2,1)} %get-tuple-element.10.rest_5_.rest_8_), channel_id=1, source_target_pairs={{0,2},{2,4},{4,6},{6,8},{8,10},{10,12},{12,14},{14,16},{16,18},{18... | collective-permute-start | bytes 3145736 | tf_op jit(solution)/shard_map/ppermute | solution.py:37
  47.2 38.5 %collective-permute-start.1 = (bf16[512,1024]{1,0:T(8,128)(2,1)}, bf16[512,1024]{1,0:T(8,128)(2,1)}, u32[]{:S(2)}, u32[]{:S(2)}) collective-permute-start(bf16[512,1024]{1,0:T(8,128)(2,1)} %get-tuple-element.10.rest_5_.rest_8_), channel_id=1, source_target_pairs={{0,4},{2,6},{4,8},{6,10},{8,12},{10,14},{12,16},{14,18},{16,20},{1... | collective-permute-start | bytes 3145736 | tf_op jit(solution)/shard_map/ppermute | solution.py:37
  51.6 34.1 %collective-permute-start = (bf16[512,1024]{1,0:T(8,128)(2,1)}, bf16[512,1024]{1,0:T(8,128)(2,1)S(1)}, u32[]{:S(2)}, u32[]{:S(2)}) collective-permute-start(bf16[512,1024]{1,0:T(8,128)(2,1)} %get-tuple-element.9), channel_id=1, source_target_pairs={{0,1},{1,0},{2,3},{3,2},{4,5},{5,4},{6,7},{7,6},{8,9},{9,8},{10,11... | collective-permute-start | bytes 3145736 | tf_op jit(solution)/shard_map/ppermute | solution.py:522
  52.1 8.7 %copy-start = (bf16[544,1024]{1,0:T(8,128)(2,1)}, bf16[544,1024]{1,0:T(8,128)(2,1)S(1)}, u32[]{:S(2)}) copy-start(bf16[544,1024]{1,0:T(8,128)(2,1)S(1)} %collective-permute-done.6.t1_ref.rest_4_.rest_7_) | copy-start | bytes 3342340
  110.4 1.3 %collective-permute-start.8 = (bf16[8,4096]{1,0:T(8,128)(2,1)S(1)}, bf16[8,4096]{1,0:T(8,128)(2,1)S(1)}, u32[]{:S(2)}, u32[]{:S(2)}) collective-permute-start(bf16[8,4096]{1,0:T(8,128)(2,1)S(1)} %shard_map.119), channel_id=1, source_target_pairs={{0,2},{2,0},{4,6},{6,4},{8,10},{10,8},{12,14},{14,12},{16,18},{18,... | collective-permute-start | bytes 196616 | tf_op jit(solution)/shard_map/ppermute | solution.py:41
  111.7 6.0 %collective-permute-start.11 = (bf16[8,4096]{1,0:T(8,128)(2,1)S(1)}, bf16[8,4096]{1,0:T(8,128)(2,1)S(1)}, u32[]{:S(2)}, u32[]{:S(2)}) collective-permute-start(bf16[8,4096]{1,0:T(8,128)(2,1)S(1)} %add_convert_fusion.1), channel_id=1, source_target_pairs={{0,12},{2,14},{4,8},{6,10},{8,4},{10,6},{12,0},{14,2},{16,28},{18,... | collective-permute-start | bytes 196616 | tf_op jit(solution)/shard_map/ppermute | solution.py:41
  115.3 4.3 %collective-permute-start.10 = (bf16[8,4096]{1,0:T(8,128)(2,1)S(1)}, bf16[8,4096]{1,0:T(8,128)(2,1)S(1)}, u32[]{:S(2)}, u32[]{:S(2)}) collective-permute-start(bf16[8,4096]{1,0:T(8,128)(2,1)S(1)} %add_convert_fusion.1), channel_id=1, source_target_pairs={{0,8},{2,10},{4,12},{6,14},{8,0},{10,2},{12,4},{14,6},{16,24},{18,... | collective-permute-start | bytes 196616 | tf_op jit(solution)/shard_map/ppermute | solution.py:41
  115.8 4.3 %collective-permute-start.9 = (bf16[8,4096]{1,0:T(8,128)(2,1)S(1)}, bf16[8,4096]{1,0:T(8,128)(2,1)S(1)}, u32[]{:S(2)}, u32[]{:S(2)}) collective-permute-start(bf16[8,4096]{1,0:T(8,128)(2,1)S(1)} %add_convert_fusion.1), channel_id=1, source_target_pairs={{0,4},{2,6},{4,0},{6,2},{8,12},{10,14},{12,8},{14,10},{16,20},{18,... | collective-permute-start | bytes 196616 | tf_op jit(solution)/shard_map/ppermute | solution.py:41
  120.1 5.5 %collective-permute-start.12 = (bf16[8,4096]{1,0:T(8,128)(2,1)S(1)}, bf16[8,4096]{1,0:T(8,128)(2,1)S(1)}, u32[]{:S(2)}, u32[]{:S(2)}) collective-permute-start(bf16[8,4096]{1,0:T(8,128)(2,1)S(1)} %add_convert_fusion.mine_ref.refs_0_), channel_id=1, source_target_pairs={{0,16},{2,18},{4,20},{6,22},{8,24},{10,26},{12,28},{14,30},{16,0},... | collective-permute-start | bytes 196616 | tf_op jit(solution)/shard_map/ppermute | solution.py:41
  125.6 3.7 %collective-permute-start.13 = (f32[8,128]{1,0:T(8,128)S(1)}, f32[8,128]{1,0:T(8,128)S(1)}, u32[]{:S(2)}, u32[]{:S(2)}) collective-permute-start(f32[8,128]{1,0:T(8,128)S(1)} %shard_map.120.refs_2_), channel_id=1, source_target_pairs={{0,1},{1,0},{2,3},{3,2},{4,5},{5,4},{6,7},{7,6},{8,9},{9,8},{10,11... | collective-permute-start | bytes 12296 | tf_op jit(solution)/shard_map/ppermute | solution.py:41

commit v7 on v6

--- a/solution.py
+++ b/solution.py
@@ -448,17 +448,40 @@
     out_ref[...] = sum(jnp.square(mine[:, at : at + LANES]) for at in range(0, mine.shape[1], LANES))
 
 
+def union_body(mine_ref, other_ref, there_ref, beyond_ref, out_ref):
+    mine = mine_ref[...].astype(jnp.float32) + other_ref[...].astype(jnp.float32)
+    theirs = there_ref[...].astype(jnp.float32) + beyond_ref[...].astype(jnp.float32)
+    span = mine.shape[1]
+    tile = lambda value: sum(jnp.square(value[:, at : at + LANES]) for at in range(0, span, LANES))
+    out_ref[:, :span] = mine
+    out_ref[:, span:] = tile(mine) + tile(theirs)
+
+
+def place(mine, total, q_ref, k_ref, v_ref, skip, groups):
+    count = float(ADAPTER_RANK * (QUERY_HEADS + 2 * KEY_VALUE_HEADS) * HEAD_SIZE)
+    mine = mine * jnp.sqrt(count / (total + 1e-06))
+    for g in range(groups):
+        at, to = 4 * LANES * g, g + skip
+        q_ref[:, 2 * LANES * to : 2 * LANES * (to + 1)] = mine[:, at : at + 2 * LANES]
+        k_ref[:, LANES * to : LANES * (to + 1)] = mine[:, at + 2 * LANES : at + 3 * LANES]
+        v_ref[:, LANES * to : LANES * (to + 1)] = mine[:, at + 3 * LANES : at + 4 * LANES]
+
+
+def halves_body(second_ref, mine_ref, other_ref, q_ref, k_ref, v_ref):
+    span = mine_ref.shape[1] - LANES
+    groups = span // (4 * LANES)
+    total = jnp.sum(mine_ref[:, span:] + other_ref[:, span:], keepdims=True)
+    second = second_ref[0] == 1
+    mine, other = mine_ref[:, :span], other_ref[:, :span]
+    place(jnp.where(second, other, mine), total, q_ref, k_ref, v_ref, 0, groups)
+    place(jnp.where(second, mine, other), total, q_ref, k_ref, v_ref, groups, groups)
+
+
 def finish_body(*refs):
     q_ref, k_ref, v_ref = refs[-3:]
     mine = refs[0][...].astype(jnp.float32) + refs[1][...].astype(jnp.float32)
     total = jnp.sum(refs[2][...] + refs[3][...], keepdims=True)
-    count = float(ADAPTER_RANK * (QUERY_HEADS + 2 * KEY_VALUE_HEADS) * HEAD_SIZE)
-    mine = mine * jnp.sqrt(count / (total + 1e-06))
-    for g in range(k_ref.shape[1] // LANES):
-        at = 4 * LANES * g
-        q_ref[:, 2 * LANES * g : 2 * LANES * (g + 1)] = mine[:, at : at + 2 * LANES]
-        k_ref[:, LANES * g : LANES * (g + 1)] = mine[:, at + 2 * LANES : at + 3 * LANES]
-        v_ref[:, LANES * g : LANES * (g + 1)] = mine[:, at + 3 * LANES : at + 4 * LANES]
+    place(mine, total, q_ref, k_ref, v_ref, 0, k_ref.shape[1] // LANES)
 
 
 def local(
@@ -591,6 +614,36 @@
         total = wide[0] + wide[1]
         return total if len(parts) == 2 else total + (wide[2] + wide[3])
 
+    sizes = (heads_width, groups * HEAD_SIZE, groups * HEAD_SIZE)
+    results = [jax.ShapeDtypeStruct((ADAPTER_RANK, size), jnp.float32) for size in sizes]
+    if chunks == 2 and tp == 2:
+        span = sums.shape[1] // 2
+        flip = second[0] == 1
+        lower, upper = sums[:, :span], sums[:, span:]
+        kept = jnp.where(flip, upper, lower)
+        mine = joined(kept, xor_move(jnp.where(flip, lower, upper), "ctx", 1)).astype(jnp.bfloat16)
+        mine = joined(mine, *[xor_move(mine, "ctx", move) for move in (2, 4, 6)]).astype(jnp.bfloat16)
+        move = 8
+        while 2 * move < ctx:
+            mine = joined(mine, xor_move(mine, "ctx", move)).astype(jnp.bfloat16)
+            move *= 2
+        both = [(at, at ^ (2 * move + 1)) for at in range(2 * ctx)]
+        union = pl.pallas_call(
+            union_body,
+            out_shape=jax.ShapeDtypeStruct((ADAPTER_RANK, span + LANES), jnp.float32),
+            compiler_params=SMALL,
+        )(mine, xor_move(mine, "ctx", move), xor_move(mine, "tp", 1), lax.ppermute(mine, ("ctx", "tp"), both))
+        return pl.pallas_call(
+            halves_body,
+            grid_spec=pltpu.PrefetchScalarGridSpec(
+                num_scalar_prefetch=1,
+                grid=(1,),
+                in_specs=[pl.BlockSpec(union.shape, lambda i, sec: (0, 0))] * 2,
+                out_specs=[pl.BlockSpec(one.shape, lambda i, sec: (0, 0)) for one in results],
+            ),
+            out_shape=results,
+            compiler_params=SMALL,
+        )(second, union, xor_move(union, "ctx", 1))
     sums = joined(sums, xor_move(sums, "ctx", 1)).astype(jnp.bfloat16)
     sums = joined(sums, *[xor_move(sums, "ctx", move) for move in (2, 4, 6)]).astype(jnp.bfloat16)
     move = 8
@@ -606,10 +659,9 @@
         squared = squared + xor_move(squared, "tp", move)
         move *= 2
     last += [squared, xor_move(squared, "tp", move)]
-    sizes = (heads_width, groups * HEAD_SIZE, groups * HEAD_SIZE)
     return pl.pallas_call(
         finish_body,
-        out_shape=[jax.ShapeDtypeStruct((ADAPTER_RANK, size), jnp.float32) for size in sizes],
+        out_shape=results,
         compiler_params=SMALL,
     )(*last)
 

time: 130 us -> 131 us (level)
    ppermute x0 -> x1, starting transfers between devices: none -> 3.61 us  [local(): lax.ppermute(mine, ('ctx', 'tp'), both)]
    ppermute x8 -> x9, starting transfers between devices: 11 us -> 7.57 us  [xor_move(): lax.ppermute(value, axis, [(at, at ^ step) for at in range(lax.axis_size(...]
    ppermute x0 -> x1, waiting for transfers between devices: none -> 1.32 us  [local(): lax.ppermute(mine, ('ctx', 'tp'), both)]
    ppermute x8 -> x9, waiting for transfers between devices: 12.1 us -> 11.3 us  [xor_move(): lax.ppermute(value, axis, [(at, at ^ step) for at in range(lax.axis_size(...]
  transfers between devices with their start and end apart: 14 -> 16, of which waited for: 9 -> 11; matrix products, arithmetic and copies ran while one was open for 0% -> 0% of each run, Pallas kernels for 32% -> 31%
where the time goes in v7:
time: 131 us
  Pallas kernels  72.2 us (55%)
  starting transfers between devices  29.1 us (22%)
  waiting for transfers between devices  28.5 us (22%)
    pallas_call x2, Pallas kernels, attend(): pl.pallas_call(functools.partial(attend_body, steps, units, base, alone),...  49.5 us
    ppermute x4, starting transfers between devices, shifted(): lax.ppermute(value, axis, [(source, source + steps) for source in range(f...  15.9 us
    ppermute x9, waiting for transfers between devices, xor_move(): lax.ppermute(value, axis, [(at, at ^ step) for at in range(lax.axis_size(...  11.3 us
    ppermute x2, waiting for transfers between devices, local(): lax.ppermute(part, 'tp', [(at, (at + d) % tp) for at in range(tp)])  8.13 us
    pallas_call x1, Pallas kernels, project(): pl.pallas_call(project_body, grid_spec=pltpu.PrefetchScalarGridSpec(num_s...  7.87 us
    ppermute x4, waiting for transfers between devices, shifted(): lax.ppermute(value, axis, [(source, source + steps) for source in range(f...  7.77 us
    pallas_call x1, Pallas kernels, open_call(): pl.pallas_call(open_body, grid_spec=pltpu.PrefetchScalarGridSpec(num_scal...  7.63 us
    ppermute x9, starting transfers between devices, xor_move(): lax.ppermute(value, axis, [(at, at ^ step) for at in range(lax.axis_size(...  7.57 us
  transfers between devices with their start and end apart: 16, of which 11 were waited for; matrix products, arithmetic and copies ran while one was open for 0% of the time, Pallas kernels for 31%

profile of v7, /device:TPU:0, one launch (start us, length us, event | category | flops | bytes accessed | tf_op | source)
XLA Modules:
  0.0 130.7 jit_solution(14574232230313223020)
XLA Ops:
  0.7 2.1 %shard_map.115.own_ref.rest_5_.rest_8_ = bf16[512,1024]{1,0:T(8,128)(2,1)} custom-call(bf16[512,1024]{1,0:T(8,128)(2,1)} %k_ref.1, bf16[512,1024]{1,0:T(8,128)(2,1)} %v_ref.1), custom_call_target="tpu_custom_call" | custom-call | tf_op jit(solution)/shard_map/pallas_call | solution.py:63
  2.8 4.9 %collective-permute-start.5 = (bf16[512,1024]{1,0:T(8,128)(2,1)}, bf16[512,1024]{1,0:T(8,128)(2,1)S(1)}, u32[]{:S(2)}, u32[]{:S(2)}) collective-permute-start(bf16[512,1024]{1,0:T(8,128)(2,1)} %shard_map.115.own_ref.rest_5_.rest_8_), channel_id=1, source_target_pairs={{0,4},{2,6},{4,8},{6,10},{8,12},{10,14},{12,16},{14,18},{16,20},{1... | collective-permute-start | bytes 3145736 | tf_op jit(solution)/shard_map/ppermute | solution.py:37
  7.8 7.6 %shard_map.113 = (bf16[512,1024]{1,0:T(8,128)(2,1)S(1)}, f32[32,512]{1,0:T(8,128)S(1)}) custom-call(s32[1]{0:T(128)} %bitcast.4.offset_ref, bf16[512,2688]{1,0:T(8,128)(2,1)} %rest_0_.5, bf16[4096,2688]{1,0:T(8,128)(2,1)} %rest_1_.5, bf16[512,2688]{1,0:T(8,128)(2,1)} %x_ref.1, bf16[1,2688]{1,0:T(2,128)(2,1)S(1)} %broadcast_in_dim.6.norm_ref, ...), custom_call_target="tpu_custom_call" | custom-call | flops 2818572288 | bytes 12058624 | tf_op jit(solution)/shard_map/pallas_call | solution.py:115
  15.4 1.6 %collective-permute-start.3 = (f32[32,512]{1,0:T(8,128)S(1)}, f32[32,512]{1,0:T(8,128)S(1)}, u32[]{:S(2)}, u32[]{:S(2)}) collective-permute-start(f32[32,512]{1,0:T(8,128)S(1)} %get-tuple-element.11.mine_ref), channel_id=1, source_target_pairs={{0,1},{1,0},{2,3},{3,2},{4,5},{5,4},{6,7},{7,6},{8,9},{9,8},{10,11... | collective-permute-start | bytes 196616 | tf_op jit(solution)/shard_map/ppermute | solution.py:41
  17.0 2.7 %collective-permute-done.3.theirs_ref = f32[32,512]{1,0:T(8,128)S(1)} collective-permute-done((f32[32,512]{1,0:T(8,128)S(1)}, f32[32,512]{1,0:T(8,128)S(1)}, u32[]{:S(2)}, u32[]{:S(2)}) %collective-permute-start.3) | collective-permute-done | bytes 65568 | tf_op jit(solution)/shard_map/ppermute | solution.py:41
  19.8 3.4 %collective-permute-start.4 = (bf16[32,512]{1,0:T(8,128)(2,1)S(1)}, bf16[32,512]{1,0:T(8,128)(2,1)S(1)}, u32[]{:S(2)}, u32[]{:S(2)}) collective-permute-start(bf16[32,512]{1,0:T(8,128)(2,1)S(1)} %shard_map.114.here_ref.t0_ref.rest_10_), channel_id=1, source_target_pairs={{0,4},{2,6},{4,8},{6,10},{8,12},{10,14},{12,16},{14,18},{16,20},{1... | collective-permute-start | bytes 98312 | tf_op jit(solution)/shard_map/ppermute | solution.py:37
  23.2 7.8 %collective-permute-done.4.there_ref.t2_ref = bf16[32,512]{1,0:T(8,128)(2,1)S(1)} collective-permute-done((bf16[32,512]{1,0:T(8,128)(2,1)S(1)}, bf16[32,512]{1,0:T(8,128)(2,1)S(1)}, u32[]{:S(2)}, u32[]{:S(2)}) %collective-permute-start.4) | collective-permute-done | bytes 32800 | tf_op jit(solution)/shard_map/ppermute | solution.py:37
  31.0 3.7 %shard_map.116 = bf16[544,1024]{1,0:T(8,128)(2,1)} custom-call(s32[1]{0:T(128)} %bitcast.second_ref, bf16[512,1024]{1,0:T(8,128)(2,1)S(1)} %collective-permute-done.5.far_ref.rest_3_.rest_6_, bf16[512,1024]{1,0:T(8,128)(2,1)} %shard_map.115.own_ref.rest_5_.rest_8_, bf16[32,512]{1,0:T(8,128)(2,1)S(1)} %collective-permute-done.4.there_ref.t2_ref, ...), custom_call_target="tpu_custom_call" | custom-call | tf_op jit(solution)/shard_map/pallas_call | solution.py:174
  34.6 1.5 %collective-permute-start.7 = (bf16[512,1024]{1,0:T(8,128)(2,1)S(1)}, bf16[512,1024]{1,0:T(8,128)(2,1)}, u32[]{:S(2)}, u32[]{:S(2)}) collective-permute-start(bf16[512,1024]{1,0:T(8,128)(2,1)S(1)} %get-tuple-element.14), channel_id=1, source_target_pairs={{0,1},{1,0},{2,3},{3,2},{4,5},{5,4},{6,7},{7,6},{8,9},{9,8},{10,11... | collective-permute-start | bytes 3145736 | tf_op jit(solution)/shard_map/ppermute | solution.py:545
  36.2 7.9 %shard_map.112 = (bf16[512,1024]{1,0:T(8,128)(2,1)}, bf16[512,1024]{1,0:T(8,128)(2,1)}) custom-call(s32[1]{0:T(128)} %bitcast.2.offset_ref, bf16[512,2688]{1,0:T(8,128)(2,1)} %rest_0_.5, bf16[4096,2688]{1,0:T(8,128)(2,1)} %rest_1_.5, bf16[512,1024]{1,0:T(8,128)(2,1)} %k_ref.1, bf16[512,1024]{1,0:T(8,128)(2,1)} %v_ref.1), custom_call_target="tpu_custom_call" | custom-call | flops 2818572288 | bytes 9306112 | tf_op jit(solution)/shard_map/pallas_call | solution.py:87
  44.0 3.1 %collective-permute-start.2 = (bf16[512,1024]{1,0:T(8,128)(2,1)}, bf16[512,1024]{1,0:T(8,128)(2,1)}, u32[]{:S(2)}, u32[]{:S(2)}) collective-permute-start(bf16[512,1024]{1,0:T(8,128)(2,1)} %get-tuple-element.10.rest_5_.rest_8_), channel_id=1, source_target_pairs={{0,2},{2,4},{4,6},{6,8},{8,10},{10,12},{12,14},{14,16},{16,18},{18... | collective-permute-start | bytes 3145736 | tf_op jit(solution)/shard_map/ppermute | solution.py:37
  47.1 4.5 %collective-permute-start.1 = (bf16[512,1024]{1,0:T(8,128)(2,1)}, bf16[512,1024]{1,0:T(8,128)(2,1)}, u32[]{:S(2)}, u32[]{:S(2)}) collective-permute-start(bf16[512,1024]{1,0:T(8,128)(2,1)} %get-tuple-element.10.rest_5_.rest_8_), channel_id=1, source_target_pairs={{0,4},{2,6},{4,8},{6,10},{8,12},{10,14},{12,16},{14,18},{16,20},{1... | collective-permute-start | bytes 3145736 | tf_op jit(solution)/shard_map/ppermute | solution.py:37
  52.6 8.1 %collective-permute-done.7.rest_2_ = bf16[512,1024]{1,0:T(8,128)(2,1)} collective-permute-done((bf16[512,1024]{1,0:T(8,128)(2,1)S(1)}, bf16[512,1024]{1,0:T(8,128)(2,1)}, u32[]{:S(2)}, u32[]{:S(2)}) %collective-permute-start.7) | collective-permute-done | bytes 1048608 | tf_op jit(solution)/shard_map/ppermute | solution.py:545
  60.8 24.9 %shard_map.118.rest_12_ = bf16[8,2048]{1,0:T(8,128)(2,1)S(1)} custom-call(s32[1]{0:T(128)} %bitcast.7.offset_ref, bf16[512,2048]{1,0:T(8,128)(2,1)} %q_ref.3, bf16[512,2688]{1,0:T(8,128)(2,1)} %rest_0_.5, bf16[4096,2688]{1,0:T(8,128)(2,1)} %rest_1_.5, bf16[512,1024]{1,0:T(8,128)(2,1)} %collective-permute-done.7.rest_2_, bf16[512,1024]{1,0:T(8,128)(2,1)} %copy-done.1, ...), custom_call_target="tpu_custom_call" | custom-call | flops 13555990528 | bytes 10747904 | tf_op jit(solution)/shard_map/pallas_call | solution.py:415
  85.7 24.6 %shard_map.119 = bf16[8,4096]{1,0:T(8,128)(2,1)S(1)} custom-call(s32[1]{0:T(128)} %bitcast.1.offset_ref, bf16[512,2048]{1,0:T(8,128)(2,1)} %q_ref.3, bf16[512,2688]{1,0:T(8,128)(2,1)} %rest_0_.5, bf16[4096,2688]{1,0:T(8,128)(2,1)} %rest_1_.5, bf16[512,1024]{1,0:T(8,128)(2,1)S(1)} %collective-permute-done.rest_2_, ...), custom_call_target="tpu_custom_call" | custom-call | flops 13555990528 | bytes 10747904 | tf_op jit(solution)/shard_map/pallas_call | solution.py:415
  110.5 1.2 collective-permute-done.8
  111.7 3.6 %collective-permute-start.11 = (bf16[8,2048]{1,0:T(8,128)(2,1)S(1)}, bf16[8,2048]{1,0:T(8,128)(2,1)S(1)}, u32[]{:S(2)}, u32[]{:S(2)}) collective-permute-start(bf16[8,2048]{1,0:T(8,128)(2,1)S(1)} %add_convert_fusion.1), channel_id=1, source_target_pairs={{0,12},{2,14},{4,8},{6,10},{8,4},{10,6},{12,0},{14,2},{16,28},{18,... | collective-permute-start | bytes 98312 | tf_op jit(solution)/shard_map/ppermute | solution.py:41
  115.7 1.0 collective-permute-start.9
  117.1 2.0 %collective-permute-done.10 = bf16[8,2048]{1,0:T(8,128)(2,1)S(1)} collective-permute-done((bf16[8,2048]{1,0:T(8,128)(2,1)S(1)}, bf16[8,2048]{1,0:T(8,128)(2,1)S(1)}, u32[]{:S(2)}, u32[]{:S(2)}) %collective-permute-start.10) | collective-permute-done | bytes 32800 | tf_op jit(solution)/shard_map/ppermute | solution.py:41
  119.6 3.6 %collective-permute-start.14 = (bf16[8,2048]{1,0:T(8,128)(2,1)S(1)}, bf16[8,2048]{1,0:T(8,128)(2,1)S(1)}, u32[]{:S(2)}, u32[]{:S(2)}) collective-permute-start(bf16[8,2048]{1,0:T(8,128)(2,1)S(1)} %add_convert_fusion.mine_ref), channel_id=1, source_target_pairs={{0,17},{1,16},{2,19},{3,18},{4,21},{5,20},{6,23},{7,22},{8,25},{9,... | collective-permute-start | bytes 98312 | tf_op jit(solution)/shard_map/ppermute | solution.py:635
  124.1 1.3 %collective-permute-done.14.beyond_ref = bf16[8,2048]{1,0:T(8,128)(2,1)S(1)} collective-permute-done((bf16[8,2048]{1,0:T(8,128)(2,1)S(1)}, bf16[8,2048]{1,0:T(8,128)(2,1)S(1)}, u32[]{:S(2)}, u32[]{:S(2)}) %collective-permute-start.14) | collective-permute-done | bytes 32800 | tf_op jit(solution)/shard_map/ppermute | solution.py:635
  125.4 1.7 %collective-permute-done.13.there_ref = bf16[8,2048]{1,0:T(8,128)(2,1)S(1)} collective-permute-done((bf16[8,2048]{1,0:T(8,128)(2,1)S(1)}, bf16[8,2048]{1,0:T(8,128)(2,1)S(1)}, u32[]{:S(2)}, u32[]{:S(2)}) %collective-permute-start.13) | collective-permute-done | bytes 32800 | tf_op jit(solution)/shard_map/ppermute | solution.py:41
  127.2 1.4 %collective-permute-done.12.other_ref = bf16[8,2048]{1,0:T(8,128)(2,1)S(1)} collective-permute-done((bf16[8,2048]{1,0:T(8,128)(2,1)S(1)}, bf16[8,2048]{1,0:T(8,128)(2,1)S(1)}, u32[]{:S(2)}, u32[]{:S(2)}) %collective-permute-start.12) | collective-permute-done | bytes 32800 | tf_op jit(solution)/shard_map/ppermute | solution.py:41
  128.7 1.2 collective-permute-done.15.other_ref
  (32 shorter events, 4.3 us)
Async XLA Ops:
  0.6 7.1 %copy-start.4 = (bf16[2688]{0:T(1024)(128)(2,1)S(1)}, bf16[2688]{0:T(1024)(128)(2,1)}, u32[]{:S(2)}) copy-start(bf16[2688]{0:T(1024)(128)(2,1)} %param.10) | copy-start | bytes 16132
  0.6 7.1 %copy-start.2 = (bf16[2688,24]{0,1:T(8,128)(2,1)S(1)}, bf16[2688,24]{0,1:T(8,128)(2,1)}, u32[]{:S(2)}) copy-start(bf16[2688,24]{0,1:T(8,128)(2,1)} %param.17) | copy-start | bytes 387076
  2.8 28.2 %collective-permute-start.5 = (bf16[512,1024]{1,0:T(8,128)(2,1)}, bf16[512,1024]{1,0:T(8,128)(2,1)S(1)}, u32[]{:S(2)}, u32[]{:S(2)}) collective-permute-start(bf16[512,1024]{1,0:T(8,128)(2,1)} %shard_map.115.own_ref.rest_5_.rest_8_), channel_id=1, source_target_pairs={{0,4},{2,6},{4,8},{6,10},{8,12},{10,14},{12,16},{14,18},{16,20},{1... | collective-permute-start | bytes 3145736 | tf_op jit(solution)/shard_map/ppermute | solution.py:37
  7.8 12.0 %copy-start.3 = (s32[512]{0:T(512)S(1)}, s32[512]{0:T(512)}, u32[]{:S(2)}) copy-start(s32[512]{0:T(512)} %param.11) | copy-start | bytes 6148
  15.4 4.3 %collective-permute-start.3 = (f32[32,512]{1,0:T(8,128)S(1)}, f32[32,512]{1,0:T(8,128)S(1)}, u32[]{:S(2)}, u32[]{:S(2)}) collective-permute-start(f32[32,512]{1,0:T(8,128)S(1)} %get-tuple-element.11.mine_ref), channel_id=1, source_target_pairs={{0,1},{1,0},{2,3},{3,2},{4,5},{5,4},{6,7},{7,6},{8,9},{9,8},{10,11... | collective-permute-start | bytes 196616 | tf_op jit(solution)/shard_map/ppermute | solution.py:41
  19.8 11.2 %collective-permute-start.4 = (bf16[32,512]{1,0:T(8,128)(2,1)S(1)}, bf16[32,512]{1,0:T(8,128)(2,1)S(1)}, u32[]{:S(2)}, u32[]{:S(2)}) collective-permute-start(bf16[32,512]{1,0:T(8,128)(2,1)S(1)} %shard_map.114.here_ref.t0_ref.rest_10_), channel_id=1, source_target_pairs={{0,4},{2,6},{4,8},{6,10},{8,12},{10,14},{12,16},{14,18},{16,20},{1... | collective-permute-start | bytes 98312 | tf_op jit(solution)/shard_map/ppermute | solution.py:37
  31.0 13.1 %copy-start.1 = (bf16[512,1024]{1,0:T(8,128)(2,1)}, bf16[512,1024]{1,0:T(8,128)(2,1)S(1)}, u32[]{:S(2)}) copy-start(bf16[512,1024]{1,0:T(8,128)(2,1)S(1)} %collective-permute-done.5.far_ref.rest_3_.rest_6_) | copy-start | bytes 3145732
  34.6 17.5 %collective-permute-start.6 = (bf16[544,1024]{1,0:T(8,128)(2,1)}, bf16[544,1024]{1,0:T(8,128)(2,1)S(1)}, u32[]{:S(2)}, u32[]{:S(2)}) collective-permute-start(bf16[544,1024]{1,0:T(8,128)(2,1)} %shard_map.116), channel_id=1, source_target_pairs={{0,2},{2,0},{4,6},{6,4},{8,10},{10,8},{12,14},{14,12},{16,18},{18,... | collective-permute-start | bytes 3342344 | tf_op jit(solution)/shard_map/ppermute | solution.py:41
  34.6 26.1 %collective-permute-start.7 = (bf16[512,1024]{1,0:T(8,128)(2,1)S(1)}, bf16[512,1024]{1,0:T(8,128)(2,1)}, u32[]{:S(2)}, u32[]{:S(2)}) collective-permute-start(bf16[512,1024]{1,0:T(8,128)(2,1)S(1)} %get-tuple-element.14), channel_id=1, source_target_pairs={{0,1},{1,0},{2,3},{3,2},{4,5},{5,4},{6,7},{7,6},{8,9},{9,8},{10,11... | collective-permute-start | bytes 3145736 | tf_op jit(solution)/shard_map/ppermute | solution.py:545
  44.0 41.7 %collective-permute-start.2 = (bf16[512,1024]{1,0:T(8,128)(2,1)}, bf16[512,1024]{1,0:T(8,128)(2,1)}, u32[]{:S(2)}, u32[]{:S(2)}) collective-permute-start(bf16[512,1024]{1,0:T(8,128)(2,1)} %get-tuple-element.10.rest_5_.rest_8_), channel_id=1, source_target_pairs={{0,2},{2,4},{4,6},{6,8},{8,10},{10,12},{12,14},{14,16},{16,18},{18... | collective-permute-start | bytes 3145736 | tf_op jit(solution)/shard_map/ppermute | solution.py:37
  47.1 38.6 %collective-permute-start.1 = (bf16[512,1024]{1,0:T(8,128)(2,1)}, bf16[512,1024]{1,0:T(8,128)(2,1)}, u32[]{:S(2)}, u32[]{:S(2)}) collective-permute-start(bf16[512,1024]{1,0:T(8,128)(2,1)} %get-tuple-element.10.rest_5_.rest_8_), channel_id=1, source_target_pairs={{0,4},{2,6},{4,8},{6,10},{8,12},{10,14},{12,16},{14,18},{16,20},{1... | collective-permute-start | bytes 3145736 | tf_op jit(solution)/shard_map/ppermute | solution.py:37
  51.6 34.1 %collective-permute-start = (bf16[512,1024]{1,0:T(8,128)(2,1)}, bf16[512,1024]{1,0:T(8,128)(2,1)S(1)}, u32[]{:S(2)}, u32[]{:S(2)}) collective-permute-start(bf16[512,1024]{1,0:T(8,128)(2,1)} %get-tuple-element.9), channel_id=1, source_target_pairs={{0,1},{1,0},{2,3},{3,2},{4,5},{5,4},{6,7},{7,6},{8,9},{9,8},{10,11... | collective-permute-start | bytes 3145736 | tf_op jit(solution)/shard_map/ppermute | solution.py:545
  52.1 8.7 %copy-start = (bf16[544,1024]{1,0:T(8,128)(2,1)}, bf16[544,1024]{1,0:T(8,128)(2,1)S(1)}, u32[]{:S(2)}) copy-start(bf16[544,1024]{1,0:T(8,128)(2,1)S(1)} %collective-permute-done.6.t1_ref.rest_4_.rest_7_) | copy-start | bytes 3342340
  110.4 1.3 collective-permute-start.8
  111.7 5.5 %collective-permute-start.11 = (bf16[8,2048]{1,0:T(8,128)(2,1)S(1)}, bf16[8,2048]{1,0:T(8,128)(2,1)S(1)}, u32[]{:S(2)}, u32[]{:S(2)}) collective-permute-start(bf16[8,2048]{1,0:T(8,128)(2,1)S(1)} %add_convert_fusion.1), channel_id=1, source_target_pairs={{0,12},{2,14},{4,8},{6,10},{8,4},{10,6},{12,0},{14,2},{16,28},{18,... | collective-permute-start | bytes 98312 | tf_op jit(solution)/shard_map/ppermute | solution.py:41
  115.2 3.9 %collective-permute-start.10 = (bf16[8,2048]{1,0:T(8,128)(2,1)S(1)}, bf16[8,2048]{1,0:T(8,128)(2,1)S(1)}, u32[]{:S(2)}, u32[]{:S(2)}) collective-permute-start(bf16[8,2048]{1,0:T(8,128)(2,1)S(1)} %add_convert_fusion.1), channel_id=1, source_target_pairs={{0,8},{2,10},{4,12},{6,14},{8,0},{10,2},{12,4},{14,6},{16,24},{18,... | collective-permute-start | bytes 98312 | tf_op jit(solution)/shard_map/ppermute | solution.py:41
  115.7 3.9 %collective-permute-start.9 = (bf16[8,2048]{1,0:T(8,128)(2,1)S(1)}, bf16[8,2048]{1,0:T(8,128)(2,1)S(1)}, u32[]{:S(2)}, u32[]{:S(2)}) collective-permute-start(bf16[8,2048]{1,0:T(8,128)(2,1)S(1)} %add_convert_fusion.1), channel_id=1, source_target_pairs={{0,4},{2,6},{4,0},{6,2},{8,12},{10,14},{12,8},{14,10},{16,20},{18,... | collective-permute-start | bytes 98312 | tf_op jit(solution)/shard_map/ppermute | solution.py:41
  119.6 5.8 %collective-permute-start.14 = (bf16[8,2048]{1,0:T(8,128)(2,1)S(1)}, bf16[8,2048]{1,0:T(8,128)(2,1)S(1)}, u32[]{:S(2)}, u32[]{:S(2)}) collective-permute-start(bf16[8,2048]{1,0:T(8,128)(2,1)S(1)} %add_convert_fusion.mine_ref), channel_id=1, source_target_pairs={{0,17},{1,16},{2,19},{3,18},{4,21},{5,20},{6,23},{7,22},{8,25},{9,... | collective-permute-start | bytes 98312 | tf_op jit(solution)/shard_map/ppermute | solution.py:635
  123.2 3.9 %collective-permute-start.13 = (bf16[8,2048]{1,0:T(8,128)(2,1)S(1)}, bf16[8,2048]{1,0:T(8,128)(2,1)S(1)}, u32[]{:S(2)}, u32[]{:S(2)}) collective-permute-start(bf16[8,2048]{1,0:T(8,128)(2,1)S(1)} %add_convert_fusion.mine_ref), channel_id=1, source_target_pairs={{0,1},{1,0},{2,3},{3,2},{4,5},{5,4},{6,7},{7,6},{8,9},{9,8},{10,11... | collective-permute-start | bytes 98312 | tf_op jit(solution)/shard_map/ppermute | solution.py:41
  123.8 4.8 %collective-permute-start.12 = (bf16[8,2048]{1,0:T(8,128)(2,1)S(1)}, bf16[8,2048]{1,0:T(8,128)(2,1)S(1)}, u32[]{:S(2)}, u32[]{:S(2)}) collective-permute-start(bf16[8,2048]{1,0:T(8,128)(2,1)S(1)} %add_convert_fusion.mine_ref), channel_id=1, source_target_pairs={{0,16},{2,18},{4,20},{6,22},{8,24},{10,26},{12,28},{14,30},{16,0},... | collective-permute-start | bytes 98312 | tf_op jit(solution)/shard_map/ppermute | solution.py:41
  128.6 1.3 %collective-permute-start.15 = (f32[8,2176]{1,0:T(8,128)S(1)}, f32[8,2176]{1,0:T(8,128)S(1)}, u32[]{:S(2)}, u32[]{:S(2)}) collective-permute-start(f32[8,2176]{1,0:T(8,128)S(1)} %shard_map.120.mine_ref), channel_id=1, source_target_pairs={{0,2},{2,0},{4,6},{6,4},{8,10},{10,8},{12,14},{14,12},{16,18},{18,... | collective-permute-start | bytes 208904 | tf_op jit(solution)/shard_map/ppermute | solution.py:41

commit v8 on v6

--- a/solution.py
+++ b/solution.py
@@ -99,14 +99,16 @@
     )(first_block, *operands)
 
 
-def open_body(offset_ref, gradient_ref, weight_ref, x_ref, norm_ref, down_ref, out_ref, low_ref):
+def open_body(offset_ref, gradient_ref, weight_ref, x_ref, norm_ref, down_ref, out_ref, low_ref, sent_ref):
     out_ref[...] = dotf(gradient_ref[...], weight_ref[...], NT).astype(out_ref.dtype)
     hidden = x_ref[...].astype(jnp.float32)
     weighted = (hidden * norm_ref[...].astype(jnp.float32)).astype(jnp.bfloat16)
     reduced = dotf(weighted, down_ref[...], NT)
     squares = jnp.sum(hidden * hidden, axis=1, keepdims=True)
     squares = jnp.broadcast_to(squares, (squares.shape[0], LANES - 3 * ADAPTER_RANK))
-    low_ref[...] = jnp.concatenate([reduced, squares], 1).T[:TABLE]
+    low = jnp.concatenate([reduced, squares], 1).T[:TABLE]
+    low_ref[...] = low
+    sent_ref[...] = low.astype(sent_ref.dtype)
 
 
 def open_call(gradient, weight, first_block, blocks, width, x, norm, down):
@@ -127,11 +129,13 @@
             out_specs=[
                 pl.BlockSpec((rows, width), lambda i, off: (0, i)),
                 pl.BlockSpec((TABLE, slab), lambda i, off: (0, i)),
+                pl.BlockSpec((TABLE, slab), lambda i, off: (0, i)),
             ],
         ),
         out_shape=[
             jax.ShapeDtypeStruct((rows, blocks * width), jnp.bfloat16),
             jax.ShapeDtypeStruct((TABLE, rows), jnp.float32),
+            jax.ShapeDtypeStruct((TABLE, rows), jnp.bfloat16),
         ],
         cost_estimate=pl.CostEstimate(
             flops=2 * rows * depth * width * blocks,
@@ -143,7 +147,7 @@
 
 
 def table_body(mine_ref, theirs_ref, doc_ref, out_ref):
-    joined = mine_ref[...] + theirs_ref[...]
+    joined = mine_ref[...] + theirs_ref[...].astype(jnp.float32)
     inverse = lax.rsqrt(joined[3 * ADAPTER_RANK : 3 * ADAPTER_RANK + 1] / float(MODEL_WIDTH) + 1e-06)
     low = joined * inverse
     rank = ADAPTER_RANK
@@ -493,7 +497,7 @@
         for d in range(1, tp):
             first = scalar(((tp_at + d) % tp) * half + c * per)
             if c == 0 and d == 1:
-                part, low = open_call(
+                part, low, sent = open_call(
                     projection_gradient,
                     output_weight,
                     first,
@@ -528,8 +532,9 @@
     move = 1
     while 2 * move < tp:
         low = low + xor_move(low, "tp", move)
+        sent = low.astype(jnp.bfloat16)
         move *= 2
-    other = xor_move(low, "tp", move)
+    other = xor_move(sent, "tp", move)
     table = pl.pallas_call(
         table_body, out_shape=jax.ShapeDtypeStruct((TABLE, rows), jnp.bfloat16), compiler_params=SMALL
     )(

time: 130 us -> 130 us (level)
  no operation moved by 1% of the time
where the time goes in v8:
time: 130 us
  Pallas kernels  72.4 us (56%)
  starting transfers between devices  28.9 us (22%)
  waiting for transfers between devices  27.9 us (21%)
    pallas_call x2, Pallas kernels, attend(): pl.pallas_call(functools.partial(attend_body, steps, units, base, alone),...  49.5 us
    ppermute x4, starting transfers between devices, shifted(): lax.ppermute(value, axis, [(source, source + steps) for source in range(f...  15.8 us
    ppermute x8, waiting for transfers between devices, xor_move(): lax.ppermute(value, axis, [(at, at ^ step) for at in range(lax.axis_size(...  11.7 us
    ppermute x8, starting transfers between devices, xor_move(): lax.ppermute(value, axis, [(at, at ^ step) for at in range(lax.axis_size(...  11 us
    ppermute x2, waiting for transfers between devices, local(): lax.ppermute(part, 'tp', [(at, (at + d) % tp) for at in range(tp)])  8.14 us
    ppermute x4, waiting for transfers between devices, shifted(): lax.ppermute(value, axis, [(source, source + steps) for source in range(f...  8.07 us
    pallas_call x1, Pallas kernels, project(): pl.pallas_call(project_body, grid_spec=pltpu.PrefetchScalarGridSpec(num_s...  7.91 us
    pallas_call x1, Pallas kernels, open_call(): pl.pallas_call(open_body, grid_spec=pltpu.PrefetchScalarGridSpec(num_scal...  7.71 us
  transfers between devices with their start and end apart: 14, of which 9 were waited for; matrix products, arithmetic and copies ran while one was open for 0% of the time, Pallas kernels for 32%

profile of v8, /device:TPU:0, one launch (start us, length us, event | category | flops | bytes accessed | tf_op | source)
XLA Modules:
  0.0 130.1 jit_solution(4110398443937437371)
XLA Ops:
  0.7 2.2 %shard_map.115.own_ref.rest_5_.rest_8_ = bf16[512,1024]{1,0:T(8,128)(2,1)} custom-call(bf16[512,1024]{1,0:T(8,128)(2,1)} %k_ref.1, bf16[512,1024]{1,0:T(8,128)(2,1)} %v_ref.1), custom_call_target="tpu_custom_call" | custom-call | tf_op jit(solution)/shard_map/pallas_call | solution.py:63
  2.8 4.9 %collective-permute-start.5 = (bf16[512,1024]{1,0:T(8,128)(2,1)}, bf16[512,1024]{1,0:T(8,128)(2,1)S(1)}, u32[]{:S(2)}, u32[]{:S(2)}) collective-permute-start(bf16[512,1024]{1,0:T(8,128)(2,1)} %shard_map.115.own_ref.rest_5_.rest_8_), channel_id=1, source_target_pairs={{0,4},{2,6},{4,8},{6,10},{8,12},{10,14},{12,16},{14,18},{16,20},{1... | collective-permute-start | bytes 3145736 | tf_op jit(solution)/shard_map/ppermute | solution.py:37
  7.8 7.7 %shard_map.113 = (bf16[512,1024]{1,0:T(8,128)(2,1)S(1)}, f32[32,512]{1,0:T(8,128)S(1)}, bf16[32,512]{1,0:T(8,128)(2,1)S(1)}) custom-call(s32[1]{0:T(128)} %bitcast.3.offset_ref, bf16[512,2688]{1,0:T(8,128)(2,1)} %rest_0_.5, bf16[4096,2688]{1,0:T(8,128)(2,1)} %rest_1_.5, bf16[512,2688]{1,0:T(8,128)(2,1)} %x_ref.1, ...), custom_call_target="tpu_custom_call" | custom-call | flops 2818572288 | bytes 12058624 | tf_op jit(solution)/shard_map/pallas_call | solution.py:117
  15.5 1.6 %collective-permute-start.3 = (bf16[32,512]{1,0:T(8,128)(2,1)S(1)}, bf16[32,512]{1,0:T(8,128)(2,1)S(1)}, u32[]{:S(2)}, u32[]{:S(2)}) collective-permute-start(bf16[32,512]{1,0:T(8,128)(2,1)S(1)} %get-tuple-element.13), channel_id=1, source_target_pairs={{0,1},{1,0},{2,3},{3,2},{4,5},{5,4},{6,7},{7,6},{8,9},{9,8},{10,11... | collective-permute-start | bytes 98312 | tf_op jit(solution)/shard_map/ppermute | solution.py:41
  17.1 2.4 %collective-permute-done.3.theirs_ref = bf16[32,512]{1,0:T(8,128)(2,1)S(1)} collective-permute-done((bf16[32,512]{1,0:T(8,128)(2,1)S(1)}, bf16[32,512]{1,0:T(8,128)(2,1)S(1)}, u32[]{:S(2)}, u32[]{:S(2)}) %collective-permute-start.3) | collective-permute-done | bytes 32800 | tf_op jit(solution)/shard_map/ppermute | solution.py:41
  19.5 3.4 %collective-permute-start.4 = (bf16[32,512]{1,0:T(8,128)(2,1)S(1)}, bf16[32,512]{1,0:T(8,128)(2,1)S(1)}, u32[]{:S(2)}, u32[]{:S(2)}) collective-permute-start(bf16[32,512]{1,0:T(8,128)(2,1)S(1)} %shard_map.114.here_ref.t0_ref.rest_10_), channel_id=1, source_target_pairs={{0,4},{2,6},{4,8},{6,10},{8,12},{10,14},{12,16},{14,18},{16,20},{1... | collective-permute-start | bytes 98312 | tf_op jit(solution)/shard_map/ppermute | solution.py:37
  22.9 8.1 %collective-permute-done.4.there_ref.t2_ref = bf16[32,512]{1,0:T(8,128)(2,1)S(1)} collective-permute-done((bf16[32,512]{1,0:T(8,128)(2,1)S(1)}, bf16[32,512]{1,0:T(8,128)(2,1)S(1)}, u32[]{:S(2)}, u32[]{:S(2)}) %collective-permute-start.4) | collective-permute-done | bytes 32800 | tf_op jit(solution)/shard_map/ppermute | solution.py:37
  31.0 3.6 %shard_map.116 = bf16[544,1024]{1,0:T(8,128)(2,1)} custom-call(s32[1]{0:T(128)} %bitcast.6.second_ref, bf16[512,1024]{1,0:T(8,128)(2,1)S(1)} %collective-permute-done.5.far_ref.rest_3_.rest_6_, bf16[512,1024]{1,0:T(8,128)(2,1)} %shard_map.115.own_ref.rest_5_.rest_8_, bf16[32,512]{1,0:T(8,128)(2,1)S(1)} %collective-permute-done.4.there_ref.t2_ref, ...), custom_call_target="tpu_custom_call" | custom-call | tf_op jit(solution)/shard_map/pallas_call | solution.py:178
  34.6 1.5 %collective-permute-start.7 = (bf16[512,1024]{1,0:T(8,128)(2,1)S(1)}, bf16[512,1024]{1,0:T(8,128)(2,1)}, u32[]{:S(2)}, u32[]{:S(2)}) collective-permute-start(bf16[512,1024]{1,0:T(8,128)(2,1)S(1)} %get-tuple-element.16), channel_id=1, source_target_pairs={{0,1},{1,0},{2,3},{3,2},{4,5},{5,4},{6,7},{7,6},{8,9},{9,8},{10,11... | collective-permute-start | bytes 3145736 | tf_op jit(solution)/shard_map/ppermute | solution.py:526
  36.2 7.9 %shard_map.112 = (bf16[512,1024]{1,0:T(8,128)(2,1)}, bf16[512,1024]{1,0:T(8,128)(2,1)}) custom-call(s32[1]{0:T(128)} %bitcast.1.offset_ref, bf16[512,2688]{1,0:T(8,128)(2,1)} %rest_0_.5, bf16[4096,2688]{1,0:T(8,128)(2,1)} %rest_1_.5, bf16[512,1024]{1,0:T(8,128)(2,1)} %k_ref.1, bf16[512,1024]{1,0:T(8,128)(2,1)} %v_ref.1), custom_call_target="tpu_custom_call" | custom-call | flops 2818572288 | bytes 9306112 | tf_op jit(solution)/shard_map/pallas_call | solution.py:87
  44.1 3.1 %collective-permute-start.2 = (bf16[512,1024]{1,0:T(8,128)(2,1)}, bf16[512,1024]{1,0:T(8,128)(2,1)}, u32[]{:S(2)}, u32[]{:S(2)}) collective-permute-start(bf16[512,1024]{1,0:T(8,128)(2,1)} %get-tuple-element.11.rest_5_.rest_8_), channel_id=1, source_target_pairs={{0,2},{2,4},{4,6},{6,8},{8,10},{10,12},{12,14},{14,16},{16,18},{18... | collective-permute-start | bytes 3145736 | tf_op jit(solution)/shard_map/ppermute | solution.py:37
  47.2 4.4 %collective-permute-start.1 = (bf16[512,1024]{1,0:T(8,128)(2,1)}, bf16[512,1024]{1,0:T(8,128)(2,1)}, u32[]{:S(2)}, u32[]{:S(2)}) collective-permute-start(bf16[512,1024]{1,0:T(8,128)(2,1)} %get-tuple-element.11.rest_5_.rest_8_), channel_id=1, source_target_pairs={{0,4},{2,6},{4,8},{6,10},{8,12},{10,14},{12,16},{14,18},{16,20},{1... | collective-permute-start | bytes 3145736 | tf_op jit(solution)/shard_map/ppermute | solution.py:37
  52.7 8.1 %collective-permute-done.7.rest_2_ = bf16[512,1024]{1,0:T(8,128)(2,1)} collective-permute-done((bf16[512,1024]{1,0:T(8,128)(2,1)S(1)}, bf16[512,1024]{1,0:T(8,128)(2,1)}, u32[]{:S(2)}, u32[]{:S(2)}) %collective-permute-start.7) | collective-permute-done | bytes 1048608 | tf_op jit(solution)/shard_map/ppermute | solution.py:526
  60.8 24.9 %shard_map.118.rest_12_ = bf16[8,2048]{1,0:T(8,128)(2,1)S(1)} custom-call(s32[1]{0:T(128)} %bitcast.7.offset_ref, bf16[512,2048]{1,0:T(8,128)(2,1)} %q_ref.3, bf16[512,2688]{1,0:T(8,128)(2,1)} %rest_0_.5, bf16[4096,2688]{1,0:T(8,128)(2,1)} %rest_1_.5, bf16[512,1024]{1,0:T(8,128)(2,1)} %collective-permute-done.7.rest_2_, bf16[512,1024]{1,0:T(8,128)(2,1)} %copy-done.1, ...), custom_call_target="tpu_custom_call" | custom-call | flops 13555990528 | bytes 10747904 | tf_op jit(solution)/shard_map/pallas_call | solution.py:419
  85.7 24.6 %shard_map.119 = bf16[8,4096]{1,0:T(8,128)(2,1)S(1)} custom-call(s32[1]{0:T(128)} %bitcast.offset_ref, bf16[512,2048]{1,0:T(8,128)(2,1)} %q_ref.3, bf16[512,2688]{1,0:T(8,128)(2,1)} %rest_0_.5, bf16[4096,2688]{1,0:T(8,128)(2,1)} %rest_1_.5, bf16[512,1024]{1,0:T(8,128)(2,1)S(1)} %collective-permute-done.rest_2_, ...), custom_call_target="tpu_custom_call" | custom-call | flops 13555990528 | bytes 10747904 | tf_op jit(solution)/shard_map/pallas_call | solution.py:419
  110.5 1.2 collective-permute-done.8
  111.7 3.6 %collective-permute-start.11 = (bf16[8,4096]{1,0:T(8,128)(2,1)S(1)}, bf16[8,4096]{1,0:T(8,128)(2,1)S(1)}, u32[]{:S(2)}, u32[]{:S(2)}) collective-permute-start(bf16[8,4096]{1,0:T(8,128)(2,1)S(1)} %add_convert_fusion.1), channel_id=1, source_target_pairs={{0,12},{2,14},{4,8},{6,10},{8,4},{10,6},{12,0},{14,2},{16,28},{18,... | collective-permute-start | bytes 196616 | tf_op jit(solution)/shard_map/ppermute | solution.py:41
  115.8 1.0 collective-permute-start.9
  116.7 1.0 collective-permute-done.11
  117.7 1.9 %collective-permute-done.10 = bf16[8,4096]{1,0:T(8,128)(2,1)S(1)} collective-permute-done((bf16[8,4096]{1,0:T(8,128)(2,1)S(1)}, bf16[8,4096]{1,0:T(8,128)(2,1)S(1)}, u32[]{:S(2)}, u32[]{:S(2)}) %collective-permute-start.10) | collective-permute-done | bytes 65568 | tf_op jit(solution)/shard_map/ppermute | solution.py:41
  120.1 2.8 %collective-permute-start.12 = (bf16[8,4096]{1,0:T(8,128)(2,1)S(1)}, bf16[8,4096]{1,0:T(8,128)(2,1)S(1)}, u32[]{:S(2)}, u32[]{:S(2)}) collective-permute-start(bf16[8,4096]{1,0:T(8,128)(2,1)S(1)} %add_convert_fusion.mine_ref.refs_0_), channel_id=1, source_target_pairs={{0,16},{2,18},{4,20},{6,22},{8,24},{10,26},{12,28},{14,30},{16,0},... | collective-permute-start | bytes 196616 | tf_op jit(solution)/shard_map/ppermute | solution.py:41
  122.8 2.7 %collective-permute-done.12.theirs_ref.refs_1_ = bf16[8,4096]{1,0:T(8,128)(2,1)S(1)} collective-permute-done((bf16[8,4096]{1,0:T(8,128)(2,1)S(1)}, bf16[8,4096]{1,0:T(8,128)(2,1)S(1)}, u32[]{:S(2)}, u32[]{:S(2)}) %collective-permute-start.12) | collective-permute-done | bytes 65568 | tf_op jit(solution)/shard_map/ppermute | solution.py:41
  125.6 1.6 %collective-permute-start.13 = (f32[8,128]{1,0:T(8,128)S(1)}, f32[8,128]{1,0:T(8,128)S(1)}, u32[]{:S(2)}, u32[]{:S(2)}) collective-permute-start(f32[8,128]{1,0:T(8,128)S(1)} %shard_map.120.refs_2_), channel_id=1, source_target_pairs={{0,1},{1,0},{2,3},{3,2},{4,5},{5,4},{6,7},{7,6},{8,9},{9,8},{10,11... | collective-permute-start | bytes 12296 | tf_op jit(solution)/shard_map/ppermute | solution.py:41
  127.2 2.1 %collective-permute-done.13.refs_3_ = f32[8,128]{1,0:T(8,128)S(1)} collective-permute-done((f32[8,128]{1,0:T(8,128)S(1)}, f32[8,128]{1,0:T(8,128)S(1)}, u32[]{:S(2)}, u32[]{:S(2)}) %collective-permute-start.13) | collective-permute-done | bytes 4128 | tf_op jit(solution)/shard_map/ppermute | solution.py:41
  (27 shorter events, 3.0 us)
Async XLA Ops:
  0.6 7.1 %copy-start.4 = (bf16[2688]{0:T(1024)(128)(2,1)S(1)}, bf16[2688]{0:T(1024)(128)(2,1)}, u32[]{:S(2)}) copy-start(bf16[2688]{0:T(1024)(128)(2,1)} %param.10) | copy-start | bytes 16132
  0.6 7.2 %copy-start.2 = (bf16[2688,24]{0,1:T(8,128)(2,1)S(1)}, bf16[2688,24]{0,1:T(8,128)(2,1)}, u32[]{:S(2)}) copy-start(bf16[2688,24]{0,1:T(8,128)(2,1)} %param.17) | copy-start | bytes 387076
  2.8 28.2 %collective-permute-start.5 = (bf16[512,1024]{1,0:T(8,128)(2,1)}, bf16[512,1024]{1,0:T(8,128)(2,1)S(1)}, u32[]{:S(2)}, u32[]{:S(2)}) collective-permute-start(bf16[512,1024]{1,0:T(8,128)(2,1)} %shard_map.115.own_ref.rest_5_.rest_8_), channel_id=1, source_target_pairs={{0,4},{2,6},{4,8},{6,10},{8,12},{10,14},{12,16},{14,18},{16,20},{1... | collective-permute-start | bytes 3145736 | tf_op jit(solution)/shard_map/ppermute | solution.py:37
  7.8 11.7 %copy-start.3 = (s32[512]{0:T(512)S(1)}, s32[512]{0:T(512)}, u32[]{:S(2)}) copy-start(s32[512]{0:T(512)} %param.11) | copy-start | bytes 6148
  15.5 4.0 %collective-permute-start.3 = (bf16[32,512]{1,0:T(8,128)(2,1)S(1)}, bf16[32,512]{1,0:T(8,128)(2,1)S(1)}, u32[]{:S(2)}, u32[]{:S(2)}) collective-permute-start(bf16[32,512]{1,0:T(8,128)(2,1)S(1)} %get-tuple-element.13), channel_id=1, source_target_pairs={{0,1},{1,0},{2,3},{3,2},{4,5},{5,4},{6,7},{7,6},{8,9},{9,8},{10,11... | collective-permute-start | bytes 98312 | tf_op jit(solution)/shard_map/ppermute | solution.py:41
  19.5 11.5 %collective-permute-start.4 = (bf16[32,512]{1,0:T(8,128)(2,1)S(1)}, bf16[32,512]{1,0:T(8,128)(2,1)S(1)}, u32[]{:S(2)}, u32[]{:S(2)}) collective-permute-start(bf16[32,512]{1,0:T(8,128)(2,1)S(1)} %shard_map.114.here_ref.t0_ref.rest_10_), channel_id=1, source_target_pairs={{0,4},{2,6},{4,8},{6,10},{8,12},{10,14},{12,16},{14,18},{16,20},{1... | collective-permute-start | bytes 98312 | tf_op jit(solution)/shard_map/ppermute | solution.py:37
  31.0 13.1 %copy-start.1 = (bf16[512,1024]{1,0:T(8,128)(2,1)}, bf16[512,1024]{1,0:T(8,128)(2,1)S(1)}, u32[]{:S(2)}) copy-start(bf16[512,1024]{1,0:T(8,128)(2,1)S(1)} %collective-permute-done.5.far_ref.rest_3_.rest_6_) | copy-start | bytes 3145732
  34.6 17.5 %collective-permute-start.6 = (bf16[544,1024]{1,0:T(8,128)(2,1)}, bf16[544,1024]{1,0:T(8,128)(2,1)S(1)}, u32[]{:S(2)}, u32[]{:S(2)}) collective-permute-start(bf16[544,1024]{1,0:T(8,128)(2,1)} %shard_map.116), channel_id=1, source_target_pairs={{0,2},{2,0},{4,6},{6,4},{8,10},{10,8},{12,14},{14,12},{16,18},{18,... | collective-permute-start | bytes 3342344 | tf_op jit(solution)/shard_map/ppermute | solution.py:41
  34.6 26.1 %collective-permute-start.7 = (bf16[512,1024]{1,0:T(8,128)(2,1)S(1)}, bf16[512,1024]{1,0:T(8,128)(2,1)}, u32[]{:S(2)}, u32[]{:S(2)}) collective-permute-start(bf16[512,1024]{1,0:T(8,128)(2,1)S(1)} %get-tuple-element.16), channel_id=1, source_target_pairs={{0,1},{1,0},{2,3},{3,2},{4,5},{5,4},{6,7},{7,6},{8,9},{9,8},{10,11... | collective-permute-start | bytes 3145736 | tf_op jit(solution)/shard_map/ppermute | solution.py:526
  44.1 41.6 %collective-permute-start.2 = (bf16[512,1024]{1,0:T(8,128)(2,1)}, bf16[512,1024]{1,0:T(8,128)(2,1)}, u32[]{:S(2)}, u32[]{:S(2)}) collective-permute-start(bf16[512,1024]{1,0:T(8,128)(2,1)} %get-tuple-element.11.rest_5_.rest_8_), channel_id=1, source_target_pairs={{0,2},{2,4},{4,6},{6,8},{8,10},{10,12},{12,14},{14,16},{16,18},{18... | collective-permute-start | bytes 3145736 | tf_op jit(solution)/shard_map/ppermute | solution.py:37
  47.2 38.5 %collective-permute-start.1 = (bf16[512,1024]{1,0:T(8,128)(2,1)}, bf16[512,1024]{1,0:T(8,128)(2,1)}, u32[]{:S(2)}, u32[]{:S(2)}) collective-permute-start(bf16[512,1024]{1,0:T(8,128)(2,1)} %get-tuple-element.11.rest_5_.rest_8_), channel_id=1, source_target_pairs={{0,4},{2,6},{4,8},{6,10},{8,12},{10,14},{12,16},{14,18},{16,20},{1... | collective-permute-start | bytes 3145736 | tf_op jit(solution)/shard_map/ppermute | solution.py:37
  51.6 34.1 %collective-permute-start = (bf16[512,1024]{1,0:T(8,128)(2,1)}, bf16[512,1024]{1,0:T(8,128)(2,1)S(1)}, u32[]{:S(2)}, u32[]{:S(2)}) collective-permute-start(bf16[512,1024]{1,0:T(8,128)(2,1)} %get-tuple-element.10), channel_id=1, source_target_pairs={{0,1},{1,0},{2,3},{3,2},{4,5},{5,4},{6,7},{7,6},{8,9},{9,8},{10,11... | collective-permute-start | bytes 3145736 | tf_op jit(solution)/shard_map/ppermute | solution.py:526
  52.1 8.7 %copy-start = (bf16[544,1024]{1,0:T(8,128)(2,1)}, bf16[544,1024]{1,0:T(8,128)(2,1)S(1)}, u32[]{:S(2)}) copy-start(bf16[544,1024]{1,0:T(8,128)(2,1)S(1)} %collective-permute-done.6.t1_ref.rest_4_.rest_7_) | copy-start | bytes 3342340
  110.4 1.3 %collective-permute-start.8 = (bf16[8,4096]{1,0:T(8,128)(2,1)S(1)}, bf16[8,4096]{1,0:T(8,128)(2,1)S(1)}, u32[]{:S(2)}, u32[]{:S(2)}) collective-permute-start(bf16[8,4096]{1,0:T(8,128)(2,1)S(1)} %shard_map.119), channel_id=1, source_target_pairs={{0,2},{2,0},{4,6},{6,4},{8,10},{10,8},{12,14},{14,12},{16,18},{18,... | collective-permute-start | bytes 196616 | tf_op jit(solution)/shard_map/ppermute | solution.py:41
  111.7 6.0 %collective-permute-start.11 = (bf16[8,4096]{1,0:T(8,128)(2,1)S(1)}, bf16[8,4096]{1,0:T(8,128)(2,1)S(1)}, u32[]{:S(2)}, u32[]{:S(2)}) collective-permute-start(bf16[8,4096]{1,0:T(8,128)(2,1)S(1)} %add_convert_fusion.1), channel_id=1, source_target_pairs={{0,12},{2,14},{4,8},{6,10},{8,4},{10,6},{12,0},{14,2},{16,28},{18,... | collective-permute-start | bytes 196616 | tf_op jit(solution)/shard_map/ppermute | solution.py:41
  115.3 4.3 %collective-permute-start.10 = (bf16[8,4096]{1,0:T(8,128)(2,1)S(1)}, bf16[8,4096]{1,0:T(8,128)(2,1)S(1)}, u32[]{:S(2)}, u32[]{:S(2)}) collective-permute-start(bf16[8,4096]{1,0:T(8,128)(2,1)S(1)} %add_convert_fusion.1), channel_id=1, source_target_pairs={{0,8},{2,10},{4,12},{6,14},{8,0},{10,2},{12,4},{14,6},{16,24},{18,... | collective-permute-start | bytes 196616 | tf_op jit(solution)/shard_map/ppermute | solution.py:41
  115.8 4.3 %collective-permute-start.9 = (bf16[8,4096]{1,0:T(8,128)(2,1)S(1)}, bf16[8,4096]{1,0:T(8,128)(2,1)S(1)}, u32[]{:S(2)}, u32[]{:S(2)}) collective-permute-start(bf16[8,4096]{1,0:T(8,128)(2,1)S(1)} %add_convert_fusion.1), channel_id=1, source_target_pairs={{0,4},{2,6},{4,0},{6,2},{8,12},{10,14},{12,8},{14,10},{16,20},{18,... | collective-permute-start | bytes 196616 | tf_op jit(solution)/shard_map/ppermute | solution.py:41
  120.1 5.5 %collective-permute-start.12 = (bf16[8,4096]{1,0:T(8,128)(2,1)S(1)}, bf16[8,4096]{1,0:T(8,128)(2,1)S(1)}, u32[]{:S(2)}, u32[]{:S(2)}) collective-permute-start(bf16[8,4096]{1,0:T(8,128)(2,1)S(1)} %add_convert_fusion.mine_ref.refs_0_), channel_id=1, source_target_pairs={{0,16},{2,18},{4,20},{6,22},{8,24},{10,26},{12,28},{14,30},{16,0},... | collective-permute-start | bytes 196616 | tf_op jit(solution)/shard_map/ppermute | solution.py:41
  125.6 3.7 %collective-permute-start.13 = (f32[8,128]{1,0:T(8,128)S(1)}, f32[8,128]{1,0:T(8,128)S(1)}, u32[]{:S(2)}, u32[]{:S(2)}) collective-permute-start(f32[8,128]{1,0:T(8,128)S(1)} %shard_map.120.refs_2_), channel_id=1, source_target_pairs={{0,1},{1,0},{2,3},{3,2},{4,5},{5,4},{6,7},{7,6},{8,9},{9,8},{10,11... | collective-permute-start | bytes 12296 | tf_op jit(solution)/shard_map/ppermute | solution.py:41
